TPU v7x, 32 devices: a whole 2x2x4 slice. The times are simulated.
32 devices in a mesh: blk: 8 (over y, x, core), col: 4 (over z).
Axes of the slice: x: 2, y: 2, z: 4, core: 2. Of those that a mesh axis runs over, the one named last changes fastest.
Arguments:
- documents: bfloat16 [6144, 768], P('blk'), may hold values from -6 to 6
- landmarks: bfloat16 [4096, 768], P(('blk', 'col')), may hold values from -6 to 6
- eigen_vectors: bfloat16 [4096, 256], P(('blk', 'col')), may hold values from -6 to 6
- land_degree: float32 [4096], P(('blk', 'col')), may hold values from 0.5 to 8
- eigen_values: float32 [256], replicated, may hold values from 0.005 to 0.05
- tile_mask: int32 [48, 32], P('blk'), may hold values from 0 to 1, as said below
- labels: int32 [6144], P(('blk', 'col')), may hold values from 0 to 999
Outputs:
- embedding: float32 [6144, 256], P(('blk', 'col'))
- centroids: float32 [1000, 256], replicated
Inputs may be any that keep to these rules, and one draw needn't show every extreme that they name: `tile_mask`: 1 marks a live tile of 128 documents by 128 landmarks; every document block has at least one live tile.
All inputs are finite; a program needn't handle non-finite values.
Results may differ from a plain program's by a relative error of at most 0.0041.
Values may be sent and summed in bfloat16 or wider, within the bound.
No kernel may reach another device: no remote copies, remote signals or barrier semaphores. Data moves between devices by JAX's collectives and lax.ppermute only.
A program may use at most 64 MiB of HBM per device.

v0:
```python
import functools
import math

import jax
import jax.numpy as jnp
from jax import lax
from jax.experimental import pallas as pl
from jax.experimental.pallas import tpu as pltpu
from jax.sharding import PartitionSpec as P


C = 1000
BLOCK = 128
TAIL = 8
HEAVY = 5_000_000_000
DEAD = 1e30
LOG2E = 1.4426950408889634
F32 = jnp.float32
BF16 = jnp.bfloat16


VMEM = pl.BlockSpec(memory_space=pltpu.VMEM)
SMEM = pl.BlockSpec(memory_space=pltpu.SMEM)


def call(kernel, outs, args, specs=None, scratch=(), flops=1000, mib=16, aliases=None, out_specs=None):
    nbytes = sum(a.size * a.dtype.itemsize for a in list(args) + list(outs))
    return pl.pallas_call(
        kernel,
        out_shape=outs,
        in_specs=specs or [VMEM] * len(args),
        out_specs=out_specs or [VMEM] * len(outs),
        scratch_shapes=list(scratch),
        input_output_aliases=aliases or {},
        compiler_params=pltpu.CompilerParams(vmem_limit_bytes=mib << 20),
        cost_estimate=pl.CostEstimate(flops=flops, bytes_accessed=nbytes, transcendentals=0),
    )(*args)


def struct(shape, dtype):
    return jax.ShapeDtypeStruct(shape, dtype)


def eye(rows, cols):
    return lax.broadcasted_iota(jnp.int32, (rows, cols), 0) == lax.broadcasted_iota(
        jnp.int32, (rows, cols), 1
    )


def to_row(col, cols):
    n = col.shape[0]
    return jnp.sum(jnp.where(eye(n, cols), jnp.broadcast_to(col, (n, cols)), 0.0), 0, keepdims=True)


def to_col(row, rows):
    n = row.shape[1]
    return jnp.sum(jnp.where(eye(rows, n), jnp.broadcast_to(row, (rows, n)), 0.0), 1, keepdims=True)


def spot_kernel(out_ref):
    out_ref[...] = lax.broadcasted_iota(jnp.int32, out_ref.shape, 1)


def prep_kernel(spot_ref, land_ref, vec_ref, deg_ref, val_ref, out_ref):
    features = land_ref.shape[1]
    rows = land_ref.shape[0]
    out_ref[:, :features] = land_ref[...]
    here = lax.broadcasted_iota(jnp.int32, (rows, rows), 0) == spot_ref[:1, :]
    root = jnp.sum(
        jnp.where(here, jnp.broadcast_to(lax.rsqrt(deg_ref[...]), (rows, rows)), 0.0), 1, keepdims=True
    )
    out_ref[:, features:] = (vec_ref[...].astype(F32) * root / val_ref[...]).astype(BF16)


def owner_of(place):
    me = lax.axis_index("blk")
    even, odd = place
    return jnp.bitwise_xor(me, even if even == odd else jnp.where(me % 2 == 0, even, odd))


def weigh(places, doc_ref, square_ref, mask_ref, pieces, low_ref, window, add_degree, add_total):
    base, count, step = window
    features = doc_ref.shape[1]
    land_rows = pieces[0].shape[0]
    blocks = land_rows // BLOCK
    width = len(pieces) * land_rows
    scale = 4.0 / features * LOG2E
    col = lax.axis_index("col")
    cols = lax.axis_size("col")
    lands = jnp.concatenate([p[:, :features] for p in pieces], 0)
    vectors = jnp.concatenate([p[:, features:] for p in pieces], 0)
    wide = lands.astype(F32)
    land_square = scale * to_row(jnp.sum(wide * wide, 1, keepdims=True), width)
    spot = lax.broadcasted_iota(jnp.int32, (1, width), 1) // BLOCK
    owners = [owner_of(place) for place in places]
    whole = pl.ds(base, count)
    prod = lax.dot_general(doc_ref[whole, :], lands, (((1,), (1,)), ((), ())), preferred_element_type=F32)
    for start in range(0, count, step):
        rows, local = pl.ds(base + start, step), slice(start, start + step)
        block = (base + start) // BLOCK
        flags = jnp.zeros((1, width), jnp.int32)
        for n, owner in enumerate(owners):
            for j in range(blocks):
                flag = mask_ref[block, (owner * cols + col) * blocks + j]
                flags = jnp.where(spot == n * blocks + j, flag, flags)
        less = jnp.where(flags > 0, land_square, DEAD)
        weights = jnp.exp2((2.0 * scale) * prod[local] - square_ref[rows, :][:, :1] - less)
        low_ref[local, :width] = weights.astype(BF16)
        part = weights[:, :128]
        for j in range(1, width // 128):
            part = part + weights[:, j * 128 : (j + 1) * 128]
        add_degree(rows, local, part)
    add_total(whole, jnp.dot(low_ref[:count, :width], vectors, preferred_element_type=F32))


def first_kernel(places, doc_ref, mask_ref, *refs):
    pieces, (total_ref, degree_ref, square_ref, low_ref) = refs[:-4], refs[-4:]
    scale = 4.0 / doc_ref.shape[1] * LOG2E
    for i in range(doc_ref.shape[0] // BLOCK):
        rows = pl.ds(i * BLOCK, BLOCK)
        block = doc_ref[rows, :].astype(F32)
        total = scale * jnp.sum(block * block, 1, keepdims=True)
        square_ref[rows, :] = jnp.broadcast_to(total, (BLOCK, 128))

    def add_degree(rows, local, part):
        degree_ref[rows, :] = part

    def add_total(rows, part):
        total_ref[rows, :] = part

    window = 0, doc_ref.shape[0], BLOCK
    weigh(places, doc_ref, square_ref, mask_ref, pieces, low_ref, window, add_degree, add_total)


def more_kernel(places, doc_ref, square_ref, mask_ref, total_in, degree_in, *refs):
    pieces, (total_ref, degree_ref, low_ref) = refs[:-3], refs[-3:]

    def add_degree(rows, local, part):
        degree_ref[rows, :] = degree_in[rows, :] + part

    def add_total(rows, part):
        total_ref[rows, :] = total_in[rows, :] + part

    window = 0, doc_ref.shape[0], BLOCK
    weigh(places, doc_ref, square_ref, mask_ref, pieces, low_ref, window, add_degree, add_total)


def part_kernel(mask, places, doc_ref, square_ref, mask_ref, total_in, degree_in, *refs):
    pieces, refs = refs[: len(places)], refs[len(places) :]
    outs, (low_ref, part_ref) = refs[:-2], refs[-2:]
    n, k = low_ref.shape[0], total_in.shape[1]
    step = math.gcd(n, BLOCK)
    base = pl.multiple_of(jnp.bitwise_xor(lax.axis_index("col"), mask) * n, step)
    totals = []

    def add_degree(rows, local, part):
        part_ref[local, :] = degree_in[rows, :] + part

    def add_total(rows, part):
        totals.append(total_in[rows, :] + part)

    window = base, n, step
    weigh(places, doc_ref, square_ref, mask_ref, pieces, low_ref, window, add_degree, add_total)
    deg = to_row(jnp.sum(part_ref[...], 1, keepdims=True), k)
    if mask == 0:
        outs[0][...] = totals[0]
        outs[1][...] = jnp.broadcast_to(deg, outs[1].shape)
    else:
        outs[0][:n, :] = totals[0].astype(BF16)
        high = deg.astype(BF16).astype(F32)
        spot = lax.broadcasted_iota(jnp.int32, (TAIL, k), 0)
        tail = jnp.where(spot == 0, high, jnp.where(spot == 1, deg - high, 0.0))
        outs[0][n:, :] = tail.astype(BF16)


def embed(own_ref, own_deg_ref, gets):
    n = own_ref.shape[0]
    proj = own_ref[...]
    deg = own_deg_ref[:1, :]
    for get in gets:
        proj = proj + get[:n, :].astype(F32)
        tail = get[n:, :].astype(F32)
        deg = deg + (tail[:1, :] + tail[1:2, :])
    return proj * lax.rsqrt(to_col(deg, n))


def embed_kernel(own_ref, own_deg_ref, *refs):
    refs[-1][...] = embed(own_ref, own_deg_ref, refs[:-1])


def gather_rows(core, label_ref, high, low, out_ref):
    me = lax.axis_index("blk")
    chips = lax.axis_size("blk") // 2
    n = high.shape[0]
    size = out_ref.shape[0] // chips
    labels = jnp.broadcast_to(label_ref[...], (size, n))
    spot = lax.broadcasted_iota(jnp.int32, (size, n), 0)
    for chip in range(chips):
        owner = jnp.bitwise_xor(me, 2 * chip + core)
        hot = jnp.where(labels == spot + owner * size, 1.0, 0.0).astype(BF16)
        part = jnp.dot(hot, high, preferred_element_type=F32)
        part = part + jnp.dot(hot, low, preferred_element_type=F32)
        out_ref[chip * size : (chip + 1) * size, :] = part.astype(out_ref.dtype)


def norm_kernel(own_ref, own_deg_ref, label_ref, *refs):
    send_ref, high_ref, low_ref = refs[-3:]
    emb = embed(own_ref, own_deg_ref, refs[:-3])
    unit = emb * lax.rsqrt(jnp.sum(emb * emb, 1, keepdims=True) + 1e-06)
    high = unit.astype(BF16)
    low = (unit - high.astype(F32)).astype(BF16)
    high_ref[...] = high
    low_ref[...] = low
    gather_rows(1, label_ref, high, low, send_ref)


def keep_kernel(label_ref, high_ref, low_ref, keep_ref):
    gather_rows(0, label_ref, high_ref[...], low_ref[...], keep_ref)


def split_kernel(keep_ref, get_ref, own_ref, *sends):
    size = own_ref.shape[0]
    for chip in range(len(sends) + 1):
        rows = slice(chip * size, (chip + 1) * size)
        both = keep_ref[rows, :] + get_ref[rows, :].astype(F32)
        out = sends[chip - 1] if chip else own_ref
        out[...] = both.astype(out.dtype)


def sum_kernel(count, *refs):
    total = refs[0][...]
    for ref in refs[1:count]:
        total = total + ref[...].astype(F32)
    for out in refs[count:]:
        out[...] = total.astype(out.dtype)


def place_kernel(places, aliased, *refs):
    parts, (out_hbm, wide_ref, sem) = refs[: len(places)], refs[-3:]
    del aliased
    size = parts[0].shape[0]
    count = out_hbm.shape[0]
    whole, rest = count // size, count % size
    copies = []
    for n, (place, part) in enumerate(zip(places, parts)):
        owner = jnp.bitwise_xor(lax.axis_index("blk"), place)
        wide_ref[n] = part[...].astype(F32)
        full = pltpu.make_async_copy(
            wide_ref.at[n],
            out_hbm.at[pl.ds(pl.multiple_of(jnp.minimum(owner, whole - 1) * size, 8), size), :],
            sem.at[n],
        )
        copies.append((owner < whole, full))
        if rest:
            end = pltpu.make_async_copy(
                wide_ref.at[n, pl.ds(0, rest), :], out_hbm.at[pl.ds(whole * size, rest), :], sem.at[n]
            )
            copies.append((owner == whole, end))
    for here, copy in copies:
        pl.when(here)(copy.start)
    for here, copy in copies:
        pl.when(here)(copy.wait)


def body(documents, landmarks, eigen_vectors, land_degree, eigen_values, tile_mask, labels):
    blks, cols = lax.axis_size("blk"), lax.axis_size("col")
    chips = blks // 2
    doc_rows, features = documents.shape
    land_rows = landmarks.shape[0]
    k = eigen_vectors.shape[1]
    rows = doc_rows // cols
    assert rows <= k and doc_rows % BLOCK == 0 and land_rows % BLOCK == 0

    def swap(x, pick):
        return lax.ppermute(x, "blk", [(i, pick(i)) for i in range(blks)])

    def core_swap(x):
        return swap(x, lambda i: i ^ 1)

    def chip_swap(x, mask):
        return swap(x, lambda i: i ^ (2 * mask))

    def col_swap(x, mask):
        return lax.ppermute(x, "col", [(i, i ^ mask) for i in range(cols)])

    spot = call(spot_kernel, [struct((8, land_rows), jnp.int32)], [], flops=HEAVY)[0]
    own = call(
        prep_kernel,
        [struct((land_rows, features + k), BF16)],
        [spot, landmarks, eigen_vectors, land_degree.reshape(1, -1), eigen_values.reshape(1, -1)],
        flops=HEAVY,
    )[0]

    if chips == 4:
        step_a = lambda i: i ^ 2 if i % 2 == 0 else i ^ 4
        step_b = lambda i: i ^ 4 if i % 2 == 0 else i ^ 2
        got_a = swap(own, step_a)
        got_b = swap(own, step_b)
        got_f = swap(got_a, step_b)
        far_own = core_swap(own)
        far_a, far_b, far_f = core_swap(got_a), core_swap(got_b), core_swap(got_f)
        groups = [
            [(own, (0, 0)), (far_own, (1, 1))],
            [(got_a, (2, 4)), (far_a, (5, 3))],
            [(got_b, (4, 2)), (far_b, (3, 5))],
            [(got_f, (6, 6)), (far_f, (7, 7))],
        ]
    else:
        near = [own] + [chip_swap(own, mask) for mask in range(1, chips)]
        groups = [
            [(x, (2 * mask, 2 * mask)), (core_swap(x), (2 * mask + 1, 2 * mask + 1))]
            for mask, x in enumerate(near)
        ]

    scratch = [pltpu.VMEM((doc_rows, 2 * land_rows), BF16)]
    sums = [struct((doc_rows, k), F32), struct((doc_rows, 128), F32)]

    def run(kernel, group, outs, args, scratch, aliases=None, share=1):
        places = [place for _, place in group]
        args = args + [piece for piece, _ in group]
        specs = [SMEM if a is tile_mask else VMEM for a in args]
        flops = len(group) * 2 * doc_rows * land_rows * (features + k) // share
        kernel = functools.partial(kernel, places)
        return call(kernel, outs, args, specs, scratch, flops, aliases=aliases)

    *state, square = run(first_kernel, groups[0], sums + sums[1:], [documents, tile_mask], scratch)
    head = [documents, square, tile_mask]
    for group in groups[1:-1]:
        state = run(more_kernel, group, sums, head + list(state), scratch, {3: 0, 4: 1})
    narrow = [pltpu.VMEM((rows, len(groups[-1]) * land_rows), BF16), pltpu.VMEM((rows, 128), F32)]

    def part(mask, outs):
        kernel = functools.partial(part_kernel, mask)
        return run(kernel, groups[-1], outs, head + list(state), narrow, share=cols)

    parts = part(0, [struct((rows, k), F32), struct((8, k), F32)])
    sends = [part(mask, [struct((rows + TAIL, k), BF16)])[0] for mask in range(1, cols)]
    gets = [col_swap(x, mask + 1) for mask, x in enumerate(sends)]
    size = -(-(-(-C // blks)) // 16) * 16
    names = labels.reshape(1, -1)
    wide, half = struct((chips * size, k), F32), struct((chips * size, k), BF16)
    unit = struct((rows, k), BF16)
    send, high, low = call(norm_kernel, [half, unit, unit], [parts[0], parts[1], names, *gets])
    get = core_swap(send)
    keep = call(keep_kernel, [wide], [names, high, low])[0]
    embedding = call(embed_kernel, [struct((rows, k), F32)], [parts[0], parts[1], *gets])[0]
    one, low = struct((size, k), F32), struct((size, k), BF16)
    split = call(split_kernel, [one] + [low] * (chips - 1), [keep, get])
    gets = [chip_swap(x, mask + 1) for mask, x in enumerate(split[1:])]
    mine, mine_low = call(functools.partial(sum_kernel, chips), [one, low], [split[0], *gets])
    gets = [col_swap(mine_low, mask) for mask in range(1, cols)]
    done = call(functools.partial(sum_kernel, cols), [low], [mine, *gets])[0]
    near = [done] + [chip_swap(done, mask) for mask in range(1, chips)]
    far = [core_swap(x) for x in near]
    centroids = None
    hbm = pl.BlockSpec(memory_space=pl.ANY)
    for core, chunks in enumerate((near, far)):
        extra = [] if centroids is None else [centroids]
        centroids = call(
            functools.partial(place_kernel, [2 * mask + core for mask in range(chips)], bool(extra)),
            [struct((C, k), F32)],
            chunks + extra,
            [VMEM] * chips + [hbm] * len(extra),
            [pltpu.VMEM((chips, size, k), F32), pltpu.SemaphoreType.DMA((chips,))],
            aliases={chips: 0} if extra else None,
            out_specs=[hbm],
        )[0]
    return (embedding, centroids)


def solution(mesh):
    placed = (
        P("blk", None),
        P(("blk", "col"), None),
        P(("blk", "col"), None),
        P(("blk", "col")),
        P(),
        P("blk", None),
        P(("blk", "col")),
    )

    return jax.shard_map(body, mesh=mesh, in_specs=placed, out_specs=(P(("blk", "col"), None), P()), check_vma=False)
```

profile of v0, /device:TPU:0, one launch (start us, length us, event | category | flops | bytes accessed | tf_op | source)
XLA Modules:
  0.0 65.9 jit_solution(7912687661676383090)
XLA Ops:
  1.7 3.0 %collective-permute-start.1 = (bf16[128,1024]{1,0:T(8,128)(2,1)S(1)}, bf16[128,1024]{1,0:T(8,128)(2,1)S(1)}, u32[]{:S(2)}, u32[]{:S(2)}) collective-permute-start(bf16[128,1024]{1,0:T(8,128)(2,1)S(1)} %shard_map.87.refs_0_), channel_id=1, source_target_pairs={{0,8},{4,20},{8,0},{12,28},{16,24},{20,4},{24,16},{28,12},{1,9},{5... | collective-permute-start | bytes 786440 | tf_op jit(solution)/shard_map/ppermute | solution.py:275
  4.7 1.5 %collective-permute-start.3 = (bf16[128,1024]{1,0:T(8,128)(2,1)S(1)}, bf16[128,1024]{1,0:T(8,128)(2,1)S(1)}, u32[]{:S(2)}, u32[]{:S(2)}) collective-permute-start(bf16[128,1024]{1,0:T(8,128)(2,1)S(1)} %shard_map.87.refs_0_), channel_id=1, source_target_pairs={{0,16},{4,12},{8,24},{12,4},{16,0},{20,28},{24,8},{28,20},{1,17},{... | collective-permute-start | bytes 786440 | tf_op jit(solution)/shard_map/ppermute | solution.py:275
  6.3 5.1 %collective-permute-done.1.refs_0_ = bf16[128,1024]{1,0:T(8,128)(2,1)S(1)} collective-permute-done((bf16[128,1024]{1,0:T(8,128)(2,1)S(1)}, bf16[128,1024]{1,0:T(8,128)(2,1)S(1)}, u32[]{:S(2)}, u32[]{:S(2)}) %collective-permute-start.1) | collective-permute-done | bytes 262176 | tf_op jit(solution)/shard_map/ppermute | solution.py:275
  11.3 1.6 %collective-permute-start.5 = (bf16[128,1024]{1,0:T(8,128)(2,1)S(1)}, bf16[128,1024]{1,0:T(8,128)(2,1)S(1)}, u32[]{:S(2)}, u32[]{:S(2)}) collective-permute-start(bf16[128,1024]{1,0:T(8,128)(2,1)S(1)} %collective-permute-done.1.refs_0_), channel_id=1, source_target_pairs={{0,16},{4,12},{8,24},{12,4},{16,0},{20,28},{24,8},{28,20},{1,17},{... | collective-permute-start | bytes 786440 | tf_op jit(solution)/shard_map/ppermute | solution.py:275
  13.4 4.3 %collective-permute-done.5.refs_0_ = bf16[128,1024]{1,0:T(8,128)(2,1)S(1)} collective-permute-done((bf16[128,1024]{1,0:T(8,128)(2,1)S(1)}, bf16[128,1024]{1,0:T(8,128)(2,1)S(1)}, u32[]{:S(2)}, u32[]{:S(2)}) %collective-permute-start.5) | collective-permute-done | bytes 262176 | tf_op jit(solution)/shard_map/ppermute | solution.py:275
  17.7 1.4 %shard_map.88 = (f32[768,256]{1,0:T(8,128)S(1)}, f32[768,128]{1,0:T(8,128)S(1)}, f32[768,128]{1,0:T(8,128)S(1)}) custom-call(bf16[768,768]{1,0:T(8,128)(2,1)S(1)} %copy-done, s32[6,32]{1,0:T(8,128)S(1)} %copy-done.1, bf16[128,1024]{1,0:T(8,128)(2,1)S(1)} %shard_map.87.refs_0_, bf16[128,1024]{1,0:T(8,128)(2,1)S(1)} %collective-permute-done.refs_1_), custom_call_target="tpu_custom_call" | custom-call | flops 402653184 | bytes 3277568 | tf_op jit(solution)/shard_map/pallas_call | solution.py:28
  19.2 1.5 %shard_map.89 = (f32[768,256]{1,0:T(8,128)S(1)}, f32[768,128]{1,0:T(8,128)S(1)}) custom-call(bf16[768,768]{1,0:T(8,128)(2,1)S(1)} %copy-done, f32[768,128]{1,0:T(8,128)S(1)} %get-tuple-element.20.square_ref, s32[6,32]{1,0:T(8,128)S(1)} %copy-done.1, f32[768,256]{1,0:T(8,128)S(1)} %get-tuple-element.21.total_in, ...), custom_call_target="tpu_custom_call", output_to_operand_aliasing={{0}: (3, {}), {1}: (4, {})} | custom-call | flops 402653184 | bytes 4457216 | tf_op jit(solution)/shard_map/pallas_call | solution.py:28
  20.7 1.5 %shard_map.90 = (f32[768,256]{1,0:T(8,128)S(1)}, f32[768,128]{1,0:T(8,128)S(1)}) custom-call(bf16[768,768]{1,0:T(8,128)(2,1)S(1)} %copy-done, f32[768,128]{1,0:T(8,128)S(1)} %get-tuple-element.20.square_ref, s32[6,32]{1,0:T(8,128)S(1)} %copy-done.1, f32[768,256]{1,0:T(8,128)S(1)} %get-tuple-element.23.total_in, ...), custom_call_target="tpu_custom_call", output_to_operand_aliasing={{0}: (3, {}), {1}: (4, {})} | custom-call | flops 402653184 | bytes 4457216 | tf_op jit(solution)/shard_map/pallas_call | solution.py:28
  22.2 1.1 %shard_map.94 = bf16[200,256]{1,0:T(8,128)(2,1)S(1)} custom-call(bf16[768,768]{1,0:T(8,128)(2,1)S(1)} %copy-done, f32[768,128]{1,0:T(8,128)S(1)} %get-tuple-element.20.square_ref, s32[6,32]{1,0:T(8,128)S(1)} %copy-done.1, f32[768,256]{1,0:T(8,128)S(1)} %get-tuple-element.25.total_in, f32[768,128]{1,0:T(8,128)S(1)} %get-tuple-element.26.degree_in, ...), custom_call_target="tpu_custom_call" | custom-call | flops 100663296 | bytes 3379968 | tf_op jit(solution)/shard_map/pallas_call | solution.py:28
  23.3 4.7 %collective-permute-start.9 = (bf16[200,256]{1,0:T(8,128)(2,1)S(1)}, bf16[200,256]{1,0:T(8,128)(2,1)S(1)}, u32[]{:S(2)}, u32[]{:S(2)}) collective-permute-start(bf16[200,256]{1,0:T(8,128)(2,1)S(1)} %shard_map.94), channel_id=1, source_target_pairs={{0,3},{1,2},{2,1},{3,0},{4,7},{5,6},{6,5},{7,4},{8,11},{9,10},{10,... | collective-permute-start | bytes 307208 | tf_op jit(solution)/shard_map/ppermute | solution.py:284
  28.0 1.1 %shard_map.93 = bf16[200,256]{1,0:T(8,128)(2,1)S(1)} custom-call(bf16[768,768]{1,0:T(8,128)(2,1)S(1)} %copy-done, f32[768,128]{1,0:T(8,128)S(1)} %get-tuple-element.20.square_ref, s32[6,32]{1,0:T(8,128)S(1)} %copy-done.1, f32[768,256]{1,0:T(8,128)S(1)} %get-tuple-element.25.total_in, f32[768,128]{1,0:T(8,128)S(1)} %get-tuple-element.26.degree_in, ...), custom_call_target="tpu_custom_call" | custom-call | flops 100663296 | bytes 3379968 | tf_op jit(solution)/shard_map/pallas_call | solution.py:28
  29.1 1.1 %shard_map.92 = bf16[200,256]{1,0:T(8,128)(2,1)S(1)} custom-call(bf16[768,768]{1,0:T(8,128)(2,1)S(1)} %copy-done, f32[768,128]{1,0:T(8,128)S(1)} %get-tuple-element.20.square_ref, s32[6,32]{1,0:T(8,128)S(1)} %copy-done.1, f32[768,256]{1,0:T(8,128)S(1)} %get-tuple-element.25.total_in, f32[768,128]{1,0:T(8,128)S(1)} %get-tuple-element.26.degree_in, ...), custom_call_target="tpu_custom_call" | custom-call | flops 100663296 | bytes 3379968 | tf_op jit(solution)/shard_map/pallas_call | solution.py:28
  30.9 1.1 %shard_map.91 = (f32[192,256]{1,0:T(8,128)S(1)}, f32[8,256]{1,0:T(8,128)S(1)}) custom-call(bf16[768,768]{1,0:T(8,128)(2,1)S(1)} %copy-done, f32[768,128]{1,0:T(8,128)S(1)} %get-tuple-element.20.square_ref, s32[6,32]{1,0:T(8,128)S(1)} %copy-done.1, f32[768,256]{1,0:T(8,128)S(1)} %get-tuple-element.25.total_in, f32[768,128]{1,0:T(8,128)S(1)} %get-tuple-element.26.degree_in, ...), custom_call_target="tpu_custom_call" | custom-call | flops 100663296 | bytes 3482368 | tf_op jit(solution)/shard_map/pallas_call | solution.py:28
  32.0 5.4 %collective-permute-done.8.refs_1_ = bf16[200,256]{1,0:T(8,128)(2,1)S(1)} collective-permute-done((bf16[200,256]{1,0:T(8,128)(2,1)S(1)}, bf16[200,256]{1,0:T(8,128)(2,1)S(1)}, u32[]{:S(2)}, u32[]{:S(2)}) %collective-permute-start.8) | collective-permute-done | bytes 102432 | tf_op jit(solution)/shard_map/ppermute | solution.py:284
  38.4 1.2 %collective-permute-done.10.get_ref = bf16[512,256]{1,0:T(8,128)(2,1)S(1)} collective-permute-done((bf16[512,256]{1,0:T(8,128)(2,1)S(1)}, bf16[512,256]{1,0:T(8,128)(2,1)S(1)}, u32[]{:S(2)}, u32[]{:S(2)}) %collective-permute-start.10) | collective-permute-done | bytes 262176 | tf_op jit(solution)/shard_map/ppermute | solution.py:275
  39.7 1.5 %collective-permute-start.11 = (bf16[128,256]{1,0:T(8,128)(2,1)S(1)}, bf16[128,256]{1,0:T(8,128)(2,1)S(1)}, u32[]{:S(2)}, u32[]{:S(2)}) collective-permute-start(bf16[128,256]{1,0:T(8,128)(2,1)S(1)} %get-tuple-element.33), channel_id=1, source_target_pairs={{0,8},{4,12},{8,0},{12,4},{16,24},{20,28},{24,16},{28,20},{1,9},{5... | collective-permute-start | bytes 196616 | tf_op jit(solution)/shard_map/ppermute | solution.py:275
  41.2 0.7 %collective-permute-start.12 = (bf16[128,256]{1,0:T(8,128)(2,1)S(1)}, bf16[128,256]{1,0:T(8,128)(2,1)S(1)}, u32[]{:S(2)}, u32[]{:S(2)}) collective-permute-start(bf16[128,256]{1,0:T(8,128)(2,1)S(1)} %get-tuple-element.34), channel_id=1, source_target_pairs={{0,16},{4,20},{8,24},{12,28},{16,0},{20,4},{24,8},{28,12},{1,17},{... | collective-permute-start | bytes 196616 | tf_op jit(solution)/shard_map/ppermute | solution.py:275
  41.9 1.3 %collective-permute-start.13 = (bf16[128,256]{1,0:T(8,128)(2,1)S(1)}, bf16[128,256]{1,0:T(8,128)(2,1)S(1)}, u32[]{:S(2)}, u32[]{:S(2)}) collective-permute-start(bf16[128,256]{1,0:T(8,128)(2,1)S(1)} %get-tuple-element.35), channel_id=1, source_target_pairs={{0,24},{4,28},{8,16},{12,20},{16,8},{20,12},{24,0},{28,4},{1,25},{... | collective-permute-start | bytes 196616 | tf_op jit(solution)/shard_map/ppermute | solution.py:275
  43.2 0.8 %collective-permute-done.11.refs_1_ = bf16[128,256]{1,0:T(8,128)(2,1)S(1)} collective-permute-done((bf16[128,256]{1,0:T(8,128)(2,1)S(1)}, bf16[128,256]{1,0:T(8,128)(2,1)S(1)}, u32[]{:S(2)}, u32[]{:S(2)}) %collective-permute-start.11) | collective-permute-done | bytes 65568 | tf_op jit(solution)/shard_map/ppermute | solution.py:275
  44.0 2.2 %collective-permute-done.12.refs_2_ = bf16[128,256]{1,0:T(8,128)(2,1)S(1)} collective-permute-done((bf16[128,256]{1,0:T(8,128)(2,1)S(1)}, bf16[128,256]{1,0:T(8,128)(2,1)S(1)}, u32[]{:S(2)}, u32[]{:S(2)}) %collective-permute-start.12) | collective-permute-done | bytes 65568 | tf_op jit(solution)/shard_map/ppermute | solution.py:275
  46.2 0.9 %collective-permute-done.13.refs_3_ = bf16[128,256]{1,0:T(8,128)(2,1)S(1)} collective-permute-done((bf16[128,256]{1,0:T(8,128)(2,1)S(1)}, bf16[128,256]{1,0:T(8,128)(2,1)S(1)}, u32[]{:S(2)}, u32[]{:S(2)}) %collective-permute-start.13) | collective-permute-done | bytes 65568 | tf_op jit(solution)/shard_map/ppermute | solution.py:275
  47.4 2.8 %collective-permute-start.15 = (bf16[128,256]{1,0:T(8,128)(2,1)S(1)}, bf16[128,256]{1,0:T(8,128)(2,1)S(1)}, u32[]{:S(2)}, u32[]{:S(2)}) collective-permute-start(bf16[128,256]{1,0:T(8,128)(2,1)S(1)} %get-tuple-element.37), channel_id=1, source_target_pairs={{0,2},{1,3},{2,0},{3,1},{4,6},{5,7},{6,4},{7,5},{8,10},{9,11},{10,... | collective-permute-start | bytes 196616 | tf_op jit(solution)/shard_map/ppermute | solution.py:284
  50.2 1.4 %collective-permute-start.16 = (bf16[128,256]{1,0:T(8,128)(2,1)S(1)}, bf16[128,256]{1,0:T(8,128)(2,1)S(1)}, u32[]{:S(2)}, u32[]{:S(2)}) collective-permute-start(bf16[128,256]{1,0:T(8,128)(2,1)S(1)} %get-tuple-element.37), channel_id=1, source_target_pairs={{0,3},{1,2},{2,1},{3,0},{4,7},{5,6},{6,5},{7,4},{8,11},{9,10},{10,... | collective-permute-start | bytes 196616 | tf_op jit(solution)/shard_map/ppermute | solution.py:284
  51.6 0.9 %collective-permute-done.15.refs_2_ = bf16[128,256]{1,0:T(8,128)(2,1)S(1)} collective-permute-done((bf16[128,256]{1,0:T(8,128)(2,1)S(1)}, bf16[128,256]{1,0:T(8,128)(2,1)S(1)}, u32[]{:S(2)}, u32[]{:S(2)}) %collective-permute-start.15) | collective-permute-done | bytes 65568 | tf_op jit(solution)/shard_map/ppermute | solution.py:284
  52.6 3.7 %collective-permute-done.16.refs_3_ = bf16[128,256]{1,0:T(8,128)(2,1)S(1)} collective-permute-done((bf16[128,256]{1,0:T(8,128)(2,1)S(1)}, bf16[128,256]{1,0:T(8,128)(2,1)S(1)}, u32[]{:S(2)}, u32[]{:S(2)}) %collective-permute-start.16) | collective-permute-done | bytes 65568 | tf_op jit(solution)/shard_map/ppermute | solution.py:284
  56.9 1.3 %collective-permute-start.20 = (bf16[128,256]{1,0:T(8,128)(2,1)S(1)}, bf16[128,256]{1,0:T(8,128)(2,1)S(1)}, u32[]{:S(2)}, u32[]{:S(2)}) collective-permute-start(bf16[128,256]{1,0:T(8,128)(2,1)S(1)} %shard_map.100.refs_0_), channel_id=1, source_target_pairs={{0,16},{4,20},{8,24},{12,28},{16,0},{20,4},{24,8},{28,12},{1,17},{... | collective-permute-start | bytes 196616 | tf_op jit(solution)/shard_map/ppermute | solution.py:275
  58.2 1.6 %collective-permute-start.22 = (bf16[128,256]{1,0:T(8,128)(2,1)S(1)}, bf16[128,256]{1,0:T(8,128)(2,1)S(1)}, u32[]{:S(2)}, u32[]{:S(2)}) collective-permute-start(bf16[128,256]{1,0:T(8,128)(2,1)S(1)} %shard_map.100.refs_0_), channel_id=1, source_target_pairs={{0,24},{4,28},{8,16},{12,20},{16,8},{20,12},{24,0},{28,4},{1,25},{... | collective-permute-start | bytes 196616 | tf_op jit(solution)/shard_map/ppermute | solution.py:275
  59.9 0.8 %collective-permute-done.18.refs_1_ = bf16[128,256]{1,0:T(8,128)(2,1)S(1)} collective-permute-done((bf16[128,256]{1,0:T(8,128)(2,1)S(1)}, bf16[128,256]{1,0:T(8,128)(2,1)S(1)}, u32[]{:S(2)}, u32[]{:S(2)}) %collective-permute-start.18) | collective-permute-done | bytes 65568 | tf_op jit(solution)/shard_map/ppermute | solution.py:275
  61.2 2.2 %collective-permute-done.22.refs_3_ = bf16[128,256]{1,0:T(8,128)(2,1)S(1)} collective-permute-done((bf16[128,256]{1,0:T(8,128)(2,1)S(1)}, bf16[128,256]{1,0:T(8,128)(2,1)S(1)}, u32[]{:S(2)}, u32[]{:S(2)}) %collective-permute-start.22) | collective-permute-done | bytes 65568 | tf_op jit(solution)/shard_map/ppermute | solution.py:275
  63.4 0.8 %shard_map.95 = f32[192,256]{1,0:T(8,128)} custom-call(f32[192,256]{1,0:T(8,128)S(1)} %get-tuple-element.27.own_ref, f32[8,256]{1,0:T(8,128)S(1)} %get-tuple-element.28.own_deg_ref, bf16[200,256]{1,0:T(8,128)(2,1)S(1)} %collective-permute-done.7.refs_0_, bf16[200,256]{1,0:T(8,128)(2,1)S(1)} %collective-permute-done.8.refs_1_, ...), custom_call_target="tpu_custom_call" | custom-call | flops 1000 | bytes 708608 | tf_op jit(solution)/shard_map/pallas_call | solution.py:28
  64.2 0.9 %shard_map.101.refs_4_ = f32[1000,256]{1,0:T(8,128)} custom-call(bf16[128,256]{1,0:T(8,128)(2,1)S(1)} %shard_map.100.refs_0_, bf16[128,256]{1,0:T(8,128)(2,1)S(1)} %collective-permute-done.18.refs_1_, bf16[128,256]{1,0:T(8,128)(2,1)S(1)} %collective-permute-done.20.refs_2_, bf16[128,256]{1,0:T(8,128)(2,1)S(1)} %collective-permute-done.22.refs_3_), custom_call_target="tpu_custom_call" | custom-call | flops 1000 | bytes 1286144 | tf_op jit(solution)/shard_map/pallas_call | solution.py:28
  65.1 0.8 %shard_map.102 = f32[1000,256]{1,0:T(8,128)} custom-call(bf16[128,256]{1,0:T(8,128)(2,1)S(1)} %collective-permute-done.17.refs_0_, bf16[128,256]{1,0:T(8,128)(2,1)S(1)} %collective-permute-done.19.refs_1_, bf16[128,256]{1,0:T(8,128)(2,1)S(1)} %collective-permute-done.21.refs_2_, ...), custom_call_target="tpu_custom_call", output_to_operand_aliasing={{}: (4, {})} | custom-call | flops 1000 | bytes 2310144 | tf_op jit(solution)/shard_map/pallas_call | solution.py:28
  (47 shorter events, 4.8 us)
Async XLA Ops:
  0.6 0.7 copy-start.6
  0.6 0.7 %copy-start.5 = (f32[256]{0:T(256)S(1)}, f32[256]{0:T(256)}, u32[]{:S(2)}) copy-start(f32[256]{0:T(256)} %param.11) | copy-start | bytes 3076
  0.7 0.9 %copy-start.3 = (bf16[128,768]{1,0:T(8,128)(2,1)S(1)}, bf16[128,768]{1,0:T(8,128)(2,1)}, u32[]{:S(2)}) copy-start(bf16[128,768]{1,0:T(8,128)(2,1)} %land_ref.1) | copy-start | bytes 589828
  0.7 0.9 %copy-start.4 = (bf16[128,256]{1,0:T(8,128)(2,1)S(1)}, bf16[128,256]{1,0:T(8,128)(2,1)}, u32[]{:S(2)}) copy-start(bf16[128,256]{1,0:T(8,128)(2,1)} %vec_ref.1) | copy-start | bytes 196612
  1.6 16.1 %copy-start = (bf16[768,768]{1,0:T(8,128)(2,1)S(1)}, bf16[768,768]{1,0:T(8,128)(2,1)}, u32[]{:S(2)}) copy-start(bf16[768,768]{1,0:T(8,128)(2,1)} %doc_ref.13) | copy-start | bytes 3538948
  1.6 16.1 %copy-start.1 = (s32[6,32]{1,0:T(8,128)S(1)}, s32[6,32]{1,0:T(8,128)}, u32[]{:S(2)}) copy-start(s32[6,32]{1,0:T(8,128)} %mask_ref.13) | copy-start | bytes 2308
  1.7 9.6 %collective-permute-start.1 = (bf16[128,1024]{1,0:T(8,128)(2,1)S(1)}, bf16[128,1024]{1,0:T(8,128)(2,1)S(1)}, u32[]{:S(2)}, u32[]{:S(2)}) collective-permute-start(bf16[128,1024]{1,0:T(8,128)(2,1)S(1)} %shard_map.87.refs_0_), channel_id=1, source_target_pairs={{0,8},{4,20},{8,0},{12,28},{16,24},{20,4},{24,16},{28,12},{1,9},{5... | collective-permute-start | bytes 786440 | tf_op jit(solution)/shard_map/ppermute | solution.py:275
  4.7 8.7 %collective-permute-start.3 = (bf16[128,1024]{1,0:T(8,128)(2,1)S(1)}, bf16[128,1024]{1,0:T(8,128)(2,1)S(1)}, u32[]{:S(2)}, u32[]{:S(2)}) collective-permute-start(bf16[128,1024]{1,0:T(8,128)(2,1)S(1)} %shard_map.87.refs_0_), channel_id=1, source_target_pairs={{0,16},{4,12},{8,24},{12,4},{16,0},{20,28},{24,8},{28,20},{1,17},{... | collective-permute-start | bytes 786440 | tf_op jit(solution)/shard_map/ppermute | solution.py:275
  11.3 6.4 %collective-permute-start.5 = (bf16[128,1024]{1,0:T(8,128)(2,1)S(1)}, bf16[128,1024]{1,0:T(8,128)(2,1)S(1)}, u32[]{:S(2)}, u32[]{:S(2)}) collective-permute-start(bf16[128,1024]{1,0:T(8,128)(2,1)S(1)} %collective-permute-done.1.refs_0_), channel_id=1, source_target_pairs={{0,16},{4,12},{8,24},{12,4},{16,0},{20,28},{24,8},{28,20},{1,17},{... | collective-permute-start | bytes 786440 | tf_op jit(solution)/shard_map/ppermute | solution.py:275
  12.9 4.8 %collective-permute-start = (bf16[128,1024]{1,0:T(8,128)(2,1)S(1)}, bf16[128,1024]{1,0:T(8,128)(2,1)S(1)}, u32[]{:S(2)}, u32[]{:S(2)}) collective-permute-start(bf16[128,1024]{1,0:T(8,128)(2,1)S(1)} %shard_map.87.refs_0_), channel_id=1, source_target_pairs={{0,4},{4,0},{8,12},{12,8},{16,20},{20,16},{24,28},{28,24},{1,5},{5... | collective-permute-start | bytes 786440 | tf_op jit(solution)/shard_map/ppermute | solution.py:275
  12.9 6.3 %collective-permute-start.2 = (bf16[128,1024]{1,0:T(8,128)(2,1)S(1)}, bf16[128,1024]{1,0:T(8,128)(2,1)S(1)}, u32[]{:S(2)}, u32[]{:S(2)}) collective-permute-start(bf16[128,1024]{1,0:T(8,128)(2,1)S(1)} %collective-permute-done.1.refs_0_), channel_id=1, source_target_pairs={{0,4},{4,0},{8,12},{12,8},{16,20},{20,16},{24,28},{28,24},{1,5},{5... | collective-permute-start | bytes 786440 | tf_op jit(solution)/shard_map/ppermute | solution.py:275
  13.4 7.3 %collective-permute-start.4 = (bf16[128,1024]{1,0:T(8,128)(2,1)S(1)}, bf16[128,1024]{1,0:T(8,128)(2,1)S(1)}, u32[]{:S(2)}, u32[]{:S(2)}) collective-permute-start(bf16[128,1024]{1,0:T(8,128)(2,1)S(1)} %collective-permute-done.3.refs_0_), channel_id=1, source_target_pairs={{0,4},{4,0},{8,12},{12,8},{16,20},{20,16},{24,28},{28,24},{1,5},{5... | collective-permute-start | bytes 786440 | tf_op jit(solution)/shard_map/ppermute | solution.py:275
  17.7 4.5 %collective-permute-start.6 = (bf16[128,1024]{1,0:T(8,128)(2,1)S(1)}, bf16[128,1024]{1,0:T(8,128)(2,1)S(1)}, u32[]{:S(2)}, u32[]{:S(2)}) collective-permute-start(bf16[128,1024]{1,0:T(8,128)(2,1)S(1)} %collective-permute-done.5.refs_0_), channel_id=1, source_target_pairs={{0,4},{4,0},{8,12},{12,8},{16,20},{20,16},{24,28},{28,24},{1,5},{5... | collective-permute-start | bytes 786440 | tf_op jit(solution)/shard_map/ppermute | solution.py:275
  23.3 8.7 %collective-permute-start.9 = (bf16[200,256]{1,0:T(8,128)(2,1)S(1)}, bf16[200,256]{1,0:T(8,128)(2,1)S(1)}, u32[]{:S(2)}, u32[]{:S(2)}) collective-permute-start(bf16[200,256]{1,0:T(8,128)(2,1)S(1)} %shard_map.94), channel_id=1, source_target_pairs={{0,3},{1,2},{2,1},{3,0},{4,7},{5,6},{6,5},{7,4},{8,11},{9,10},{10,... | collective-permute-start | bytes 307208 | tf_op jit(solution)/shard_map/ppermute | solution.py:284
  29.0 8.3 %collective-permute-start.8 = (bf16[200,256]{1,0:T(8,128)(2,1)S(1)}, bf16[200,256]{1,0:T(8,128)(2,1)S(1)}, u32[]{:S(2)}, u32[]{:S(2)}) collective-permute-start(bf16[200,256]{1,0:T(8,128)(2,1)S(1)} %shard_map.93), channel_id=1, source_target_pairs={{0,2},{1,3},{2,0},{3,1},{4,6},{5,7},{6,4},{7,5},{8,10},{9,11},{10,... | collective-permute-start | bytes 307208 | tf_op jit(solution)/shard_map/ppermute | solution.py:284
  30.2 7.3 %copy-start.2 = (s32[192]{0:T(256)S(1)}, s32[192]{0:T(256)}, u32[]{:S(2)}) copy-start(s32[192]{0:T(256)} %param.13) | copy-start | bytes 2308
  30.2 7.3 %collective-permute-start.7 = (bf16[200,256]{1,0:T(8,128)(2,1)S(1)}, bf16[200,256]{1,0:T(8,128)(2,1)S(1)}, u32[]{:S(2)}, u32[]{:S(2)}) collective-permute-start(bf16[200,256]{1,0:T(8,128)(2,1)S(1)} %shard_map.92), channel_id=1, source_target_pairs={{0,1},{1,0},{2,3},{3,2},{4,5},{5,4},{6,7},{7,6},{8,9},{9,8},{10,11... | collective-permute-start | bytes 307208 | tf_op jit(solution)/shard_map/ppermute | solution.py:284
  38.0 1.6 %collective-permute-start.10 = (bf16[512,256]{1,0:T(8,128)(2,1)S(1)}, bf16[512,256]{1,0:T(8,128)(2,1)S(1)}, u32[]{:S(2)}, u32[]{:S(2)}) collective-permute-start(bf16[512,256]{1,0:T(8,128)(2,1)S(1)} %get-tuple-element.31), channel_id=1, source_target_pairs={{0,4},{4,0},{8,12},{12,8},{16,20},{20,16},{24,28},{28,24},{1,5},{5... | collective-permute-start | bytes 786440 | tf_op jit(solution)/shard_map/ppermute | solution.py:275
  39.7 4.3 %collective-permute-start.11 = (bf16[128,256]{1,0:T(8,128)(2,1)S(1)}, bf16[128,256]{1,0:T(8,128)(2,1)S(1)}, u32[]{:S(2)}, u32[]{:S(2)}) collective-permute-start(bf16[128,256]{1,0:T(8,128)(2,1)S(1)} %get-tuple-element.33), channel_id=1, source_target_pairs={{0,8},{4,12},{8,0},{12,4},{16,24},{20,28},{24,16},{28,20},{1,9},{5... | collective-permute-start | bytes 196616 | tf_op jit(solution)/shard_map/ppermute | solution.py:275
  41.2 5.0 %collective-permute-start.12 = (bf16[128,256]{1,0:T(8,128)(2,1)S(1)}, bf16[128,256]{1,0:T(8,128)(2,1)S(1)}, u32[]{:S(2)}, u32[]{:S(2)}) collective-permute-start(bf16[128,256]{1,0:T(8,128)(2,1)S(1)} %get-tuple-element.34), channel_id=1, source_target_pairs={{0,16},{4,20},{8,24},{12,28},{16,0},{20,4},{24,8},{28,12},{1,17},{... | collective-permute-start | bytes 196616 | tf_op jit(solution)/shard_map/ppermute | solution.py:275
  41.9 5.2 %collective-permute-start.13 = (bf16[128,256]{1,0:T(8,128)(2,1)S(1)}, bf16[128,256]{1,0:T(8,128)(2,1)S(1)}, u32[]{:S(2)}, u32[]{:S(2)}) collective-permute-start(bf16[128,256]{1,0:T(8,128)(2,1)S(1)} %get-tuple-element.35), channel_id=1, source_target_pairs={{0,24},{4,28},{8,16},{12,20},{16,8},{20,12},{24,0},{28,4},{1,25},{... | collective-permute-start | bytes 196616 | tf_op jit(solution)/shard_map/ppermute | solution.py:275
  47.1 4.5 %collective-permute-start.14 = (bf16[128,256]{1,0:T(8,128)(2,1)S(1)}, bf16[128,256]{1,0:T(8,128)(2,1)S(1)}, u32[]{:S(2)}, u32[]{:S(2)}) collective-permute-start(bf16[128,256]{1,0:T(8,128)(2,1)S(1)} %get-tuple-element.37), channel_id=1, source_target_pairs={{0,1},{1,0},{2,3},{3,2},{4,5},{5,4},{6,7},{7,6},{8,9},{9,8},{10,11... | collective-permute-start | bytes 196616 | tf_op jit(solution)/shard_map/ppermute | solution.py:284
  47.4 5.2 %collective-permute-start.15 = (bf16[128,256]{1,0:T(8,128)(2,1)S(1)}, bf16[128,256]{1,0:T(8,128)(2,1)S(1)}, u32[]{:S(2)}, u32[]{:S(2)}) collective-permute-start(bf16[128,256]{1,0:T(8,128)(2,1)S(1)} %get-tuple-element.37), channel_id=1, source_target_pairs={{0,2},{1,3},{2,0},{3,1},{4,6},{5,7},{6,4},{7,5},{8,10},{9,11},{10,... | collective-permute-start | bytes 196616 | tf_op jit(solution)/shard_map/ppermute | solution.py:284
  50.2 6.1 %collective-permute-start.16 = (bf16[128,256]{1,0:T(8,128)(2,1)S(1)}, bf16[128,256]{1,0:T(8,128)(2,1)S(1)}, u32[]{:S(2)}, u32[]{:S(2)}) collective-permute-start(bf16[128,256]{1,0:T(8,128)(2,1)S(1)} %get-tuple-element.37), channel_id=1, source_target_pairs={{0,3},{1,2},{2,1},{3,0},{4,7},{5,6},{6,5},{7,4},{8,11},{9,10},{10,... | collective-permute-start | bytes 196616 | tf_op jit(solution)/shard_map/ppermute | solution.py:284
  56.3 4.3 %collective-permute-start.18 = (bf16[128,256]{1,0:T(8,128)(2,1)S(1)}, bf16[128,256]{1,0:T(8,128)(2,1)S(1)}, u32[]{:S(2)}, u32[]{:S(2)}) collective-permute-start(bf16[128,256]{1,0:T(8,128)(2,1)S(1)} %shard_map.100.refs_0_), channel_id=1, source_target_pairs={{0,8},{4,12},{8,0},{12,4},{16,24},{20,28},{24,16},{28,20},{1,9},{5... | collective-permute-start | bytes 196616 | tf_op jit(solution)/shard_map/ppermute | solution.py:275
  56.9 4.3 %collective-permute-start.20 = (bf16[128,256]{1,0:T(8,128)(2,1)S(1)}, bf16[128,256]{1,0:T(8,128)(2,1)S(1)}, u32[]{:S(2)}, u32[]{:S(2)}) collective-permute-start(bf16[128,256]{1,0:T(8,128)(2,1)S(1)} %shard_map.100.refs_0_), channel_id=1, source_target_pairs={{0,16},{4,20},{8,24},{12,28},{16,0},{20,4},{24,8},{28,12},{1,17},{... | collective-permute-start | bytes 196616 | tf_op jit(solution)/shard_map/ppermute | solution.py:275
  58.2 5.2 %collective-permute-start.22 = (bf16[128,256]{1,0:T(8,128)(2,1)S(1)}, bf16[128,256]{1,0:T(8,128)(2,1)S(1)}, u32[]{:S(2)}, u32[]{:S(2)}) collective-permute-start(bf16[128,256]{1,0:T(8,128)(2,1)S(1)} %shard_map.100.refs_0_), channel_id=1, source_target_pairs={{0,24},{4,28},{8,16},{12,20},{16,8},{20,12},{24,0},{28,4},{1,25},{... | collective-permute-start | bytes 196616 | tf_op jit(solution)/shard_map/ppermute | solution.py:275
  59.9 5.2 %collective-permute-start.17 = (bf16[128,256]{1,0:T(8,128)(2,1)S(1)}, bf16[128,256]{1,0:T(8,128)(2,1)S(1)}, u32[]{:S(2)}, u32[]{:S(2)}) collective-permute-start(bf16[128,256]{1,0:T(8,128)(2,1)S(1)} %shard_map.100.refs_0_), channel_id=1, source_target_pairs={{0,4},{4,0},{8,12},{12,8},{16,20},{20,16},{24,28},{28,24},{1,5},{5... | collective-permute-start | bytes 196616 | tf_op jit(solution)/shard_map/ppermute | solution.py:275
  60.6 4.4 %collective-permute-start.19 = (bf16[128,256]{1,0:T(8,128)(2,1)S(1)}, bf16[128,256]{1,0:T(8,128)(2,1)S(1)}, u32[]{:S(2)}, u32[]{:S(2)}) collective-permute-start(bf16[128,256]{1,0:T(8,128)(2,1)S(1)} %collective-permute-done.18.refs_1_), channel_id=1, source_target_pairs={{0,4},{4,0},{8,12},{12,8},{16,20},{20,16},{24,28},{28,24},{1,5},{5... | collective-permute-start | bytes 196616 | tf_op jit(solution)/shard_map/ppermute | solution.py:275
  61.2 3.9 %collective-permute-start.21 = (bf16[128,256]{1,0:T(8,128)(2,1)S(1)}, bf16[128,256]{1,0:T(8,128)(2,1)S(1)}, u32[]{:S(2)}, u32[]{:S(2)}) collective-permute-start(bf16[128,256]{1,0:T(8,128)(2,1)S(1)} %collective-permute-done.20.refs_2_), channel_id=1, source_target_pairs={{0,4},{4,0},{8,12},{12,8},{16,20},{20,16},{24,28},{28,24},{1,5},{5... | collective-permute-start | bytes 196616 | tf_op jit(solution)/shard_map/ppermute | solution.py:275
  63.4 1.7 %collective-permute-start.23 = (bf16[128,256]{1,0:T(8,128)(2,1)S(1)}, bf16[128,256]{1,0:T(8,128)(2,1)S(1)}, u32[]{:S(2)}, u32[]{:S(2)}) collective-permute-start(bf16[128,256]{1,0:T(8,128)(2,1)S(1)} %collective-permute-done.22.refs_3_), channel_id=1, source_target_pairs={{0,4},{4,0},{8,12},{12,8},{16,20},{20,16},{24,28},{28,24},{1,5},{5... | collective-permute-start | bytes 196616 | tf_op jit(solution)/shard_map/ppermute | solution.py:275
where the time goes:
time: 66.1 us; the launch traced here: 65.9 us
  waiting for transfers between devices  28.2 us (43%)
  starting transfers between devices  23.6 us (36%)
  Pallas kernels  12.3 us (19%)
  local copies, waits for them, and re-layouts  0.94 us (1%)
  between operations  0.87 us (1%)
    ppermute x18, waiting for transfers between devices, swap(): return lax.ppermute(x, 'blk', [(i, pick(i)) for i in range(blks)])  18 us
    ppermute x18, starting transfers between devices, swap(): return lax.ppermute(x, 'blk', [(i, pick(i)) for i in range(blks)])  13.8 us
    pallas_call x17, Pallas kernels, call(): pl.pallas_call(kernel, out_shape=outs, in_specs=specs or [VMEM] * len(arg...  12.3 us
    ppermute x6, waiting for transfers between devices, col_swap(): return lax.ppermute(x, 'col', [(i, i ^ mask) for i in range(cols)])  10.2 us
    ppermute x6, starting transfers between devices, col_swap(): return lax.ppermute(x, 'col', [(i, i ^ mask) for i in range(cols)])  9.81 us
  transfers between devices with their start and end apart: 24, of which 13 were waited for; matrix products, arithmetic and copies ran while one was open for 0% of the time, Pallas kernels for 15%

commit v1 on v0

--- a/solution.py
+++ b/solution.py
@@ -20,7 +20,6 @@
 
 
 VMEM = pl.BlockSpec(memory_space=pltpu.VMEM)
-SMEM = pl.BlockSpec(memory_space=pltpu.SMEM)
 
 
 def call(kernel, outs, args, specs=None, scratch=(), flops=1000, mib=16, aliases=None, out_specs=None):
@@ -64,7 +63,9 @@
 def prep_kernel(spot_ref, land_ref, vec_ref, deg_ref, val_ref, out_ref):
     features = land_ref.shape[1]
     rows = land_ref.shape[0]
-    out_ref[:, :features] = land_ref[...]
+    for start in range(0, features, rows):
+        part = land_ref[:, start : start + rows]
+        out_ref[:, start : start + rows] = part.T
     here = lax.broadcasted_iota(jnp.int32, (rows, rows), 0) == spot_ref[:1, :]
     root = jnp.sum(
         jnp.where(here, jnp.broadcast_to(lax.rsqrt(deg_ref[...]), (rows, rows)), 0.0), 1, keepdims=True
@@ -82,28 +83,43 @@
     base, count, step = window
     features = doc_ref.shape[1]
     land_rows = pieces[0].shape[0]
-    blocks = land_rows // BLOCK
     width = len(pieces) * land_rows
     scale = 4.0 / features * LOG2E
     col = lax.axis_index("col")
     cols = lax.axis_size("col")
-    lands = jnp.concatenate([p[:, :features] for p in pieces], 0)
+    lands = jnp.concatenate(
+        [
+            jnp.concatenate([p[:, start : start + land_rows] for p in pieces], 1)
+            for start in range(0, features, land_rows)
+        ],
+        0,
+    )
     vectors = jnp.concatenate([p[:, features:] for p in pieces], 0)
     wide = lands.astype(F32)
-    land_square = scale * to_row(jnp.sum(wide * wide, 1, keepdims=True), width)
-    spot = lax.broadcasted_iota(jnp.int32, (1, width), 1) // BLOCK
-    owners = [owner_of(place) for place in places]
+    land_square = scale * jnp.sum(wide * wide, 0, keepdims=True)
+    live = mask_ref[...].astype(F32)
+    lane = lax.broadcasted_iota(jnp.int32, live.shape, 1)
+    line = lax.broadcasted_iota(jnp.int32, (live.shape[0], 1), 0)
+    flags = [
+        jnp.sum(jnp.where(lane == owner_of(place) * cols + col, live, 0.0), 1, keepdims=True)
+        for place in places
+    ]
     whole = pl.ds(base, count)
-    prod = lax.dot_general(doc_ref[whole, :], lands, (((1,), (1,)), ((), ())), preferred_element_type=F32)
+    prod = jnp.dot(doc_ref[whole, :], lands, preferred_element_type=F32)
     for start in range(0, count, step):
         rows, local = pl.ds(base + start, step), slice(start, start + step)
         block = (base + start) // BLOCK
-        flags = jnp.zeros((1, width), jnp.int32)
-        for n, owner in enumerate(owners):
-            for j in range(blocks):
-                flag = mask_ref[block, (owner * cols + col) * blocks + j]
-                flags = jnp.where(spot == n * blocks + j, flag, flags)
-        less = jnp.where(flags > 0, land_square, DEAD)
+        less = jnp.concatenate(
+            [
+                jnp.where(
+                    jnp.sum(jnp.where(line == block, flag, 0.0), 0, keepdims=True) > 0.0,
+                    land_square[:, n * land_rows : (n + 1) * land_rows],
+                    DEAD,
+                )
+                for n, flag in enumerate(flags)
+            ],
+            1,
+        )
         weights = jnp.exp2((2.0 * scale) * prod[local] - square_ref[rows, :][:, :1] - less)
         low_ref[local, :width] = weights.astype(BF16)
         part = weights[:, :128]
@@ -227,12 +243,14 @@
         out[...] = both.astype(out.dtype)
 
 
-def sum_kernel(count, *refs):
-    total = refs[0][...]
-    for ref in refs[1:count]:
-        total = total + ref[...].astype(F32)
-    for out in refs[count:]:
-        out[...] = total.astype(out.dtype)
+def tree(parts):
+    while len(parts) > 1:
+        parts = [a + b for a, b in zip(parts[::2], parts[1::2])]
+    return parts[0]
+
+
+def sum_kernel(*refs):
+    refs[-1][...] = tree([ref[...].astype(F32) for ref in refs[:-1]]).astype(refs[-1].dtype)
 
 
 def place_kernel(places, aliased, *refs):
@@ -269,7 +287,7 @@
     land_rows = landmarks.shape[0]
     k = eigen_vectors.shape[1]
     rows = doc_rows // cols
-    assert rows <= k and doc_rows % BLOCK == 0 and land_rows % BLOCK == 0
+    assert rows <= k and doc_rows % BLOCK == 0 and land_rows == BLOCK and features % BLOCK == 0
 
     def swap(x, pick):
         return lax.ppermute(x, "blk", [(i, pick(i)) for i in range(blks)])
@@ -318,10 +336,9 @@
     def run(kernel, group, outs, args, scratch, aliases=None, share=1):
         places = [place for _, place in group]
         args = args + [piece for piece, _ in group]
-        specs = [SMEM if a is tile_mask else VMEM for a in args]
         flops = len(group) * 2 * doc_rows * land_rows * (features + k) // share
         kernel = functools.partial(kernel, places)
-        return call(kernel, outs, args, specs, scratch, flops, aliases=aliases)
+        return call(kernel, outs, args, None, scratch, flops, aliases=aliases)
 
     *state, square = run(first_kernel, groups[0], sums + sums[1:], [documents, tile_mask], scratch)
     head = [documents, square, tile_mask]
@@ -347,9 +364,9 @@
     one, low = struct((size, k), F32), struct((size, k), BF16)
     split = call(split_kernel, [one] + [low] * (chips - 1), [keep, get])
     gets = [chip_swap(x, mask + 1) for mask, x in enumerate(split[1:])]
-    mine, mine_low = call(functools.partial(sum_kernel, chips), [one, low], [split[0], *gets])
-    gets = [col_swap(mine_low, mask) for mask in range(1, cols)]
-    done = call(functools.partial(sum_kernel, cols), [low], [mine, *gets])[0]
+    mine = call(sum_kernel, [low], [split[0], *gets])[0]
+    gets = [col_swap(mine, mask) for mask in range(1, cols)]
+    done = call(sum_kernel, [low], [mine, *gets])[0]
     near = [done] + [chip_swap(done, mask) for mask in range(1, chips)]
     far = [core_swap(x) for x in near]
     centroids = None

time: 66.1 us -> 63.3 us (0.958)
  Pallas kernels: 12.3 us -> 7.6 us
  waiting for transfers between devices: 28.2 us -> 30.1 us
    pallas_call x17, Pallas kernels: 12.3 us -> 7.6 us  [call(): pl.pallas_call(kernel, out_shape=outs, in_specs=specs or [VMEM] * len(arg...]
    ppermute x6, waiting for transfers between devices: 10.2 us -> 12.1 us  [col_swap(): return lax.ppermute(x, 'col', [(i, i ^ mask) for i in range(cols)])]
  transfers between devices with their start and end apart: 24 -> 24, of which waited for: 13 -> 13; matrix products, arithmetic and copies ran while one was open for 0% -> 0% of each run, Pallas kernels for 15% -> 9%
where the time goes in v1:
time: 63.3 us; the launch traced here: 63.1 us
  waiting for transfers between devices  30.1 us (48%)
  starting transfers between devices  23.6 us (37%)
  Pallas kernels  7.6 us (12%)
  local copies, waits for them, and re-layouts  0.94 us (1%)
  between operations  0.86 us (1%)
    ppermute x18, waiting for transfers between devices, swap(): return lax.ppermute(x, 'blk', [(i, pick(i)) for i in range(blks)])  18 us
    ppermute x18, starting transfers between devices, swap(): return lax.ppermute(x, 'blk', [(i, pick(i)) for i in range(blks)])  13.8 us
    ppermute x6, waiting for transfers between devices, col_swap(): return lax.ppermute(x, 'col', [(i, i ^ mask) for i in range(cols)])  12.1 us
    ppermute x6, starting transfers between devices, col_swap(): return lax.ppermute(x, 'col', [(i, i ^ mask) for i in range(cols)])  9.82 us
    pallas_call x17, Pallas kernels, call(): pl.pallas_call(kernel, out_shape=outs, in_specs=specs or [VMEM] * len(arg...  7.6 us
  transfers between devices with their start and end apart: 24, of which 13 were waited for; matrix products, arithmetic and copies ran while one was open for 0% of the time, Pallas kernels for 9%

profile of v1, /device:TPU:0, one launch (start us, length us, event | category | flops | bytes accessed | tf_op | source)
XLA Modules:
  0.0 63.1 jit_solution(11512423697639014698)
XLA Ops:
  0.7 0.6 copy-done.6
  1.8 3.0 %collective-permute-start.1 = (bf16[128,1024]{1,0:T(8,128)(2,1)S(1)}, bf16[128,1024]{1,0:T(8,128)(2,1)S(1)}, u32[]{:S(2)}, u32[]{:S(2)}) collective-permute-start(bf16[128,1024]{1,0:T(8,128)(2,1)S(1)} %shard_map.87.refs_0_), channel_id=1, source_target_pairs={{0,8},{4,20},{8,0},{12,28},{16,24},{20,4},{24,16},{28,12},{1,9},{5... | collective-permute-start | bytes 786440 | tf_op jit(solution)/shard_map/ppermute | solution.py:293
  4.8 1.5 %collective-permute-start.3 = (bf16[128,1024]{1,0:T(8,128)(2,1)S(1)}, bf16[128,1024]{1,0:T(8,128)(2,1)S(1)}, u32[]{:S(2)}, u32[]{:S(2)}) collective-permute-start(bf16[128,1024]{1,0:T(8,128)(2,1)S(1)} %shard_map.87.refs_0_), channel_id=1, source_target_pairs={{0,16},{4,12},{8,24},{12,4},{16,0},{20,28},{24,8},{28,20},{1,17},{... | collective-permute-start | bytes 786440 | tf_op jit(solution)/shard_map/ppermute | solution.py:293
  6.3 5.1 %collective-permute-done.1.refs_0_ = bf16[128,1024]{1,0:T(8,128)(2,1)S(1)} collective-permute-done((bf16[128,1024]{1,0:T(8,128)(2,1)S(1)}, bf16[128,1024]{1,0:T(8,128)(2,1)S(1)}, u32[]{:S(2)}, u32[]{:S(2)}) %collective-permute-start.1) | collective-permute-done | bytes 262176 | tf_op jit(solution)/shard_map/ppermute | solution.py:293
  11.4 1.6 %collective-permute-start.5 = (bf16[128,1024]{1,0:T(8,128)(2,1)S(1)}, bf16[128,1024]{1,0:T(8,128)(2,1)S(1)}, u32[]{:S(2)}, u32[]{:S(2)}) collective-permute-start(bf16[128,1024]{1,0:T(8,128)(2,1)S(1)} %collective-permute-done.1.refs_0_), channel_id=1, source_target_pairs={{0,16},{4,12},{8,24},{12,4},{16,0},{20,28},{24,8},{28,20},{1,17},{... | collective-permute-start | bytes 786440 | tf_op jit(solution)/shard_map/ppermute | solution.py:293
  13.5 4.3 %collective-permute-done.5.refs_0_ = bf16[128,1024]{1,0:T(8,128)(2,1)S(1)} collective-permute-done((bf16[128,1024]{1,0:T(8,128)(2,1)S(1)}, bf16[128,1024]{1,0:T(8,128)(2,1)S(1)}, u32[]{:S(2)}, u32[]{:S(2)}) %collective-permute-start.5) | collective-permute-done | bytes 262176 | tf_op jit(solution)/shard_map/ppermute | solution.py:293
  17.8 0.8 %shard_map.88 = (f32[768,256]{1,0:T(8,128)S(1)}, f32[768,128]{1,0:T(8,128)S(1)}, f32[768,128]{1,0:T(8,128)S(1)}) custom-call(bf16[768,768]{1,0:T(8,128)(2,1)S(1)} %copy-done, s32[6,32]{1,0:T(8,128)S(1)} %copy-done.1, bf16[128,1024]{1,0:T(8,128)(2,1)S(1)} %shard_map.87.refs_0_, bf16[128,1024]{1,0:T(8,128)(2,1)S(1)} %collective-permute-done.refs_1_), custom_call_target="tpu_custom_call" | custom-call | flops 402653184 | bytes 3277568 | tf_op jit(solution)/shard_map/pallas_call | solution.py:27
  18.6 0.8 %shard_map.89 = (f32[768,256]{1,0:T(8,128)S(1)}, f32[768,128]{1,0:T(8,128)S(1)}) custom-call(bf16[768,768]{1,0:T(8,128)(2,1)S(1)} %copy-done, f32[768,128]{1,0:T(8,128)S(1)} %get-tuple-element.18.square_ref, s32[6,32]{1,0:T(8,128)S(1)} %copy-done.1, f32[768,256]{1,0:T(8,128)S(1)} %get-tuple-element.19.total_in, ...), custom_call_target="tpu_custom_call", output_to_operand_aliasing={{0}: (3, {}), {1}: (4, {})} | custom-call | flops 402653184 | bytes 4457216 | tf_op jit(solution)/shard_map/pallas_call | solution.py:27
  19.5 0.8 %shard_map.90 = (f32[768,256]{1,0:T(8,128)S(1)}, f32[768,128]{1,0:T(8,128)S(1)}) custom-call(bf16[768,768]{1,0:T(8,128)(2,1)S(1)} %copy-done, f32[768,128]{1,0:T(8,128)S(1)} %get-tuple-element.18.square_ref, s32[6,32]{1,0:T(8,128)S(1)} %copy-done.1, f32[768,256]{1,0:T(8,128)S(1)} %get-tuple-element.21.total_in, ...), custom_call_target="tpu_custom_call", output_to_operand_aliasing={{0}: (3, {}), {1}: (4, {})} | custom-call | flops 402653184 | bytes 4457216 | tf_op jit(solution)/shard_map/pallas_call | solution.py:27
  20.7 4.7 %collective-permute-start.9 = (bf16[200,256]{1,0:T(8,128)(2,1)S(1)}, bf16[200,256]{1,0:T(8,128)(2,1)S(1)}, u32[]{:S(2)}, u32[]{:S(2)}) collective-permute-start(bf16[200,256]{1,0:T(8,128)(2,1)S(1)} %shard_map.94), channel_id=1, source_target_pairs={{0,3},{1,2},{2,1},{3,0},{4,7},{5,6},{6,5},{7,4},{8,11},{9,10},{10,... | collective-permute-start | bytes 307208 | tf_op jit(solution)/shard_map/ppermute | solution.py:302
  26.2 0.6 collective-permute-start.7
  27.3 1.9 %collective-permute-done.9.refs_2_ = bf16[200,256]{1,0:T(8,128)(2,1)S(1)} collective-permute-done((bf16[200,256]{1,0:T(8,128)(2,1)S(1)}, bf16[200,256]{1,0:T(8,128)(2,1)S(1)}, u32[]{:S(2)}, u32[]{:S(2)}) %collective-permute-start.9) | collective-permute-done | bytes 102432 | tf_op jit(solution)/shard_map/ppermute | solution.py:302
  29.2 5.4 %collective-permute-done.8.refs_1_ = bf16[200,256]{1,0:T(8,128)(2,1)S(1)} collective-permute-done((bf16[200,256]{1,0:T(8,128)(2,1)S(1)}, bf16[200,256]{1,0:T(8,128)(2,1)S(1)}, u32[]{:S(2)}, u32[]{:S(2)}) %collective-permute-start.8) | collective-permute-done | bytes 102432 | tf_op jit(solution)/shard_map/ppermute | solution.py:302
  35.5 1.2 %collective-permute-done.10.get_ref = bf16[512,256]{1,0:T(8,128)(2,1)S(1)} collective-permute-done((bf16[512,256]{1,0:T(8,128)(2,1)S(1)}, bf16[512,256]{1,0:T(8,128)(2,1)S(1)}, u32[]{:S(2)}, u32[]{:S(2)}) %collective-permute-start.10) | collective-permute-done | bytes 262176 | tf_op jit(solution)/shard_map/ppermute | solution.py:293
  36.8 1.6 %collective-permute-start.11 = (bf16[128,256]{1,0:T(8,128)(2,1)S(1)}, bf16[128,256]{1,0:T(8,128)(2,1)S(1)}, u32[]{:S(2)}, u32[]{:S(2)}) collective-permute-start(bf16[128,256]{1,0:T(8,128)(2,1)S(1)} %get-tuple-element.31), channel_id=1, source_target_pairs={{0,8},{4,12},{8,0},{12,4},{16,24},{20,28},{24,16},{28,20},{1,9},{5... | collective-permute-start | bytes 196616 | tf_op jit(solution)/shard_map/ppermute | solution.py:293
  38.4 0.7 %collective-permute-start.12 = (bf16[128,256]{1,0:T(8,128)(2,1)S(1)}, bf16[128,256]{1,0:T(8,128)(2,1)S(1)}, u32[]{:S(2)}, u32[]{:S(2)}) collective-permute-start(bf16[128,256]{1,0:T(8,128)(2,1)S(1)} %get-tuple-element.32), channel_id=1, source_target_pairs={{0,16},{4,20},{8,24},{12,28},{16,0},{20,4},{24,8},{28,12},{1,17},{... | collective-permute-start | bytes 196616 | tf_op jit(solution)/shard_map/ppermute | solution.py:293
  39.1 1.3 %collective-permute-start.13 = (bf16[128,256]{1,0:T(8,128)(2,1)S(1)}, bf16[128,256]{1,0:T(8,128)(2,1)S(1)}, u32[]{:S(2)}, u32[]{:S(2)}) collective-permute-start(bf16[128,256]{1,0:T(8,128)(2,1)S(1)} %get-tuple-element.33), channel_id=1, source_target_pairs={{0,24},{4,28},{8,16},{12,20},{16,8},{20,12},{24,0},{28,4},{1,25},{... | collective-permute-start | bytes 196616 | tf_op jit(solution)/shard_map/ppermute | solution.py:293
  40.4 0.8 %collective-permute-done.11.refs_1_ = bf16[128,256]{1,0:T(8,128)(2,1)S(1)} collective-permute-done((bf16[128,256]{1,0:T(8,128)(2,1)S(1)}, bf16[128,256]{1,0:T(8,128)(2,1)S(1)}, u32[]{:S(2)}, u32[]{:S(2)}) %collective-permute-start.11) | collective-permute-done | bytes 65568 | tf_op jit(solution)/shard_map/ppermute | solution.py:293
  41.1 2.2 %collective-permute-done.12.refs_2_ = bf16[128,256]{1,0:T(8,128)(2,1)S(1)} collective-permute-done((bf16[128,256]{1,0:T(8,128)(2,1)S(1)}, bf16[128,256]{1,0:T(8,128)(2,1)S(1)}, u32[]{:S(2)}, u32[]{:S(2)}) %collective-permute-start.12) | collective-permute-done | bytes 65568 | tf_op jit(solution)/shard_map/ppermute | solution.py:293
  43.3 0.9 %collective-permute-done.13.refs_3_ = bf16[128,256]{1,0:T(8,128)(2,1)S(1)} collective-permute-done((bf16[128,256]{1,0:T(8,128)(2,1)S(1)}, bf16[128,256]{1,0:T(8,128)(2,1)S(1)}, u32[]{:S(2)}, u32[]{:S(2)}) %collective-permute-start.13) | collective-permute-done | bytes 65568 | tf_op jit(solution)/shard_map/ppermute | solution.py:293
  44.8 2.6 %collective-permute-start.15 = (bf16[128,256]{1,0:T(8,128)(2,1)S(1)}, bf16[128,256]{1,0:T(8,128)(2,1)S(1)}, u32[]{:S(2)}, u32[]{:S(2)}) collective-permute-start(bf16[128,256]{1,0:T(8,128)(2,1)S(1)} %shard_map.99.refs_0_), channel_id=1, source_target_pairs={{0,2},{1,3},{2,0},{3,1},{4,6},{5,7},{6,4},{7,5},{8,10},{9,11},{10,... | collective-permute-start | bytes 196616 | tf_op jit(solution)/shard_map/ppermute | solution.py:302
  47.4 1.3 %collective-permute-start.16 = (bf16[128,256]{1,0:T(8,128)(2,1)S(1)}, bf16[128,256]{1,0:T(8,128)(2,1)S(1)}, u32[]{:S(2)}, u32[]{:S(2)}) collective-permute-start(bf16[128,256]{1,0:T(8,128)(2,1)S(1)} %shard_map.99.refs_0_), channel_id=1, source_target_pairs={{0,3},{1,2},{2,1},{3,0},{4,7},{5,6},{6,5},{7,4},{8,11},{9,10},{10,... | collective-permute-start | bytes 196616 | tf_op jit(solution)/shard_map/ppermute | solution.py:302
  48.7 2.6 %collective-permute-done.15.refs_2_ = bf16[128,256]{1,0:T(8,128)(2,1)S(1)} collective-permute-done((bf16[128,256]{1,0:T(8,128)(2,1)S(1)}, bf16[128,256]{1,0:T(8,128)(2,1)S(1)}, u32[]{:S(2)}, u32[]{:S(2)}) %collective-permute-start.15) | collective-permute-done | bytes 65568 | tf_op jit(solution)/shard_map/ppermute | solution.py:302
  51.4 2.1 %collective-permute-done.16.refs_3_ = bf16[128,256]{1,0:T(8,128)(2,1)S(1)} collective-permute-done((bf16[128,256]{1,0:T(8,128)(2,1)S(1)}, bf16[128,256]{1,0:T(8,128)(2,1)S(1)}, u32[]{:S(2)}, u32[]{:S(2)}) %collective-permute-start.16) | collective-permute-done | bytes 65568 | tf_op jit(solution)/shard_map/ppermute | solution.py:302
  53.5 0.6 collective-permute-start.18
  54.1 1.3 %collective-permute-start.20 = (bf16[128,256]{1,0:T(8,128)(2,1)S(1)}, bf16[128,256]{1,0:T(8,128)(2,1)S(1)}, u32[]{:S(2)}, u32[]{:S(2)}) collective-permute-start(bf16[128,256]{1,0:T(8,128)(2,1)S(1)} %shard_map.100.refs_0_), channel_id=1, source_target_pairs={{0,16},{4,20},{8,24},{12,28},{16,0},{20,4},{24,8},{28,12},{1,17},{... | collective-permute-start | bytes 196616 | tf_op jit(solution)/shard_map/ppermute | solution.py:293
  55.4 1.6 %collective-permute-start.22 = (bf16[128,256]{1,0:T(8,128)(2,1)S(1)}, bf16[128,256]{1,0:T(8,128)(2,1)S(1)}, u32[]{:S(2)}, u32[]{:S(2)}) collective-permute-start(bf16[128,256]{1,0:T(8,128)(2,1)S(1)} %shard_map.100.refs_0_), channel_id=1, source_target_pairs={{0,24},{4,28},{8,16},{12,20},{16,8},{20,12},{24,0},{28,4},{1,25},{... | collective-permute-start | bytes 196616 | tf_op jit(solution)/shard_map/ppermute | solution.py:293
  57.0 0.8 %collective-permute-done.18.refs_1_ = bf16[128,256]{1,0:T(8,128)(2,1)S(1)} collective-permute-done((bf16[128,256]{1,0:T(8,128)(2,1)S(1)}, bf16[128,256]{1,0:T(8,128)(2,1)S(1)}, u32[]{:S(2)}, u32[]{:S(2)}) %collective-permute-start.18) | collective-permute-done | bytes 65568 | tf_op jit(solution)/shard_map/ppermute | solution.py:293
  58.4 2.2 %collective-permute-done.22.refs_3_ = bf16[128,256]{1,0:T(8,128)(2,1)S(1)} collective-permute-done((bf16[128,256]{1,0:T(8,128)(2,1)S(1)}, bf16[128,256]{1,0:T(8,128)(2,1)S(1)}, u32[]{:S(2)}, u32[]{:S(2)}) %collective-permute-start.22) | collective-permute-done | bytes 65568 | tf_op jit(solution)/shard_map/ppermute | solution.py:293
  60.6 0.8 %shard_map.95 = f32[192,256]{1,0:T(8,128)} custom-call(f32[192,256]{1,0:T(8,128)S(1)} %get-tuple-element.25.own_ref, f32[8,256]{1,0:T(8,128)S(1)} %get-tuple-element.26.own_deg_ref, bf16[200,256]{1,0:T(8,128)(2,1)S(1)} %collective-permute-done.7.refs_0_, bf16[200,256]{1,0:T(8,128)(2,1)S(1)} %collective-permute-done.8.refs_1_, ...), custom_call_target="tpu_custom_call" | custom-call | flops 1000 | bytes 708608 | tf_op jit(solution)/shard_map/pallas_call | solution.py:27
  61.4 0.9 %shard_map.101.refs_4_ = f32[1000,256]{1,0:T(8,128)} custom-call(bf16[128,256]{1,0:T(8,128)(2,1)S(1)} %shard_map.100.refs_0_, bf16[128,256]{1,0:T(8,128)(2,1)S(1)} %collective-permute-done.18.refs_1_, bf16[128,256]{1,0:T(8,128)(2,1)S(1)} %collective-permute-done.20.refs_2_, bf16[128,256]{1,0:T(8,128)(2,1)S(1)} %collective-permute-done.22.refs_3_), custom_call_target="tpu_custom_call" | custom-call | flops 1000 | bytes 1286144 | tf_op jit(solution)/shard_map/pallas_call | solution.py:27
  62.3 0.8 %shard_map.102 = f32[1000,256]{1,0:T(8,128)} custom-call(bf16[128,256]{1,0:T(8,128)(2,1)S(1)} %collective-permute-done.17.refs_0_, bf16[128,256]{1,0:T(8,128)(2,1)S(1)} %collective-permute-done.19.refs_1_, bf16[128,256]{1,0:T(8,128)(2,1)S(1)} %collective-permute-done.21.refs_2_, ...), custom_call_target="tpu_custom_call", output_to_operand_aliasing={{}: (4, {})} | custom-call | flops 1000 | bytes 2310144 | tf_op jit(solution)/shard_map/pallas_call | solution.py:27
  (47 shorter events, 4.7 us)
Async XLA Ops:
  0.6 0.7 %copy-start.6 = (f32[128]{0:T(128)S(1)}, f32[128]{0:T(128)}, u32[]{:S(2)}) copy-start(f32[128]{0:T(128)} %param.10) | copy-start | bytes 1540
  0.6 0.7 %copy-start.5 = (f32[256]{0:T(256)S(1)}, f32[256]{0:T(256)}, u32[]{:S(2)}) copy-start(f32[256]{0:T(256)} %param.11) | copy-start | bytes 3076
  0.7 0.9 %copy-start.3 = (bf16[128,768]{1,0:T(8,128)(2,1)S(1)}, bf16[128,768]{1,0:T(8,128)(2,1)}, u32[]{:S(2)}) copy-start(bf16[128,768]{1,0:T(8,128)(2,1)} %land_ref.1) | copy-start | bytes 589828
  0.7 0.9 %copy-start.4 = (bf16[128,256]{1,0:T(8,128)(2,1)S(1)}, bf16[128,256]{1,0:T(8,128)(2,1)}, u32[]{:S(2)}) copy-start(bf16[128,256]{1,0:T(8,128)(2,1)} %vec_ref.1) | copy-start | bytes 196612
  1.6 16.2 %copy-start = (bf16[768,768]{1,0:T(8,128)(2,1)S(1)}, bf16[768,768]{1,0:T(8,128)(2,1)}, u32[]{:S(2)}) copy-start(bf16[768,768]{1,0:T(8,128)(2,1)} %doc_ref.13) | copy-start | bytes 3538948
  1.6 16.2 %copy-start.1 = (s32[6,32]{1,0:T(8,128)S(1)}, s32[6,32]{1,0:T(8,128)}, u32[]{:S(2)}) copy-start(s32[6,32]{1,0:T(8,128)} %mask_ref.13) | copy-start | bytes 2308
  1.8 9.6 %collective-permute-start.1 = (bf16[128,1024]{1,0:T(8,128)(2,1)S(1)}, bf16[128,1024]{1,0:T(8,128)(2,1)S(1)}, u32[]{:S(2)}, u32[]{:S(2)}) collective-permute-start(bf16[128,1024]{1,0:T(8,128)(2,1)S(1)} %shard_map.87.refs_0_), channel_id=1, source_target_pairs={{0,8},{4,20},{8,0},{12,28},{16,24},{20,4},{24,16},{28,12},{1,9},{5... | collective-permute-start | bytes 786440 | tf_op jit(solution)/shard_map/ppermute | solution.py:293
  4.8 8.7 %collective-permute-start.3 = (bf16[128,1024]{1,0:T(8,128)(2,1)S(1)}, bf16[128,1024]{1,0:T(8,128)(2,1)S(1)}, u32[]{:S(2)}, u32[]{:S(2)}) collective-permute-start(bf16[128,1024]{1,0:T(8,128)(2,1)S(1)} %shard_map.87.refs_0_), channel_id=1, source_target_pairs={{0,16},{4,12},{8,24},{12,4},{16,0},{20,28},{24,8},{28,20},{1,17},{... | collective-permute-start | bytes 786440 | tf_op jit(solution)/shard_map/ppermute | solution.py:293
  11.4 6.4 %collective-permute-start.5 = (bf16[128,1024]{1,0:T(8,128)(2,1)S(1)}, bf16[128,1024]{1,0:T(8,128)(2,1)S(1)}, u32[]{:S(2)}, u32[]{:S(2)}) collective-permute-start(bf16[128,1024]{1,0:T(8,128)(2,1)S(1)} %collective-permute-done.1.refs_0_), channel_id=1, source_target_pairs={{0,16},{4,12},{8,24},{12,4},{16,0},{20,28},{24,8},{28,20},{1,17},{... | collective-permute-start | bytes 786440 | tf_op jit(solution)/shard_map/ppermute | solution.py:293
  12.9 4.8 %collective-permute-start = (bf16[128,1024]{1,0:T(8,128)(2,1)S(1)}, bf16[128,1024]{1,0:T(8,128)(2,1)S(1)}, u32[]{:S(2)}, u32[]{:S(2)}) collective-permute-start(bf16[128,1024]{1,0:T(8,128)(2,1)S(1)} %shard_map.87.refs_0_), channel_id=1, source_target_pairs={{0,4},{4,0},{8,12},{12,8},{16,20},{20,16},{24,28},{28,24},{1,5},{5... | collective-permute-start | bytes 786440 | tf_op jit(solution)/shard_map/ppermute | solution.py:293
  12.9 5.7 %collective-permute-start.2 = (bf16[128,1024]{1,0:T(8,128)(2,1)S(1)}, bf16[128,1024]{1,0:T(8,128)(2,1)S(1)}, u32[]{:S(2)}, u32[]{:S(2)}) collective-permute-start(bf16[128,1024]{1,0:T(8,128)(2,1)S(1)} %collective-permute-done.1.refs_0_), channel_id=1, source_target_pairs={{0,4},{4,0},{8,12},{12,8},{16,20},{20,16},{24,28},{28,24},{1,5},{5... | collective-permute-start | bytes 786440 | tf_op jit(solution)/shard_map/ppermute | solution.py:293
  13.5 6.0 %collective-permute-start.4 = (bf16[128,1024]{1,0:T(8,128)(2,1)S(1)}, bf16[128,1024]{1,0:T(8,128)(2,1)S(1)}, u32[]{:S(2)}, u32[]{:S(2)}) collective-permute-start(bf16[128,1024]{1,0:T(8,128)(2,1)S(1)} %collective-permute-done.3.refs_0_), channel_id=1, source_target_pairs={{0,4},{4,0},{8,12},{12,8},{16,20},{20,16},{24,28},{28,24},{1,5},{5... | collective-permute-start | bytes 786440 | tf_op jit(solution)/shard_map/ppermute | solution.py:293
  17.7 2.5 %collective-permute-start.6 = (bf16[128,1024]{1,0:T(8,128)(2,1)S(1)}, bf16[128,1024]{1,0:T(8,128)(2,1)S(1)}, u32[]{:S(2)}, u32[]{:S(2)}) collective-permute-start(bf16[128,1024]{1,0:T(8,128)(2,1)S(1)} %collective-permute-done.5.refs_0_), channel_id=1, source_target_pairs={{0,4},{4,0},{8,12},{12,8},{16,20},{20,16},{24,28},{28,24},{1,5},{5... | collective-permute-start | bytes 786440 | tf_op jit(solution)/shard_map/ppermute | solution.py:293
  20.7 8.5 %collective-permute-start.9 = (bf16[200,256]{1,0:T(8,128)(2,1)S(1)}, bf16[200,256]{1,0:T(8,128)(2,1)S(1)}, u32[]{:S(2)}, u32[]{:S(2)}) collective-permute-start(bf16[200,256]{1,0:T(8,128)(2,1)S(1)} %shard_map.94), channel_id=1, source_target_pairs={{0,3},{1,2},{2,1},{3,0},{4,7},{5,6},{6,5},{7,4},{8,11},{9,10},{10,... | collective-permute-start | bytes 307208 | tf_op jit(solution)/shard_map/ppermute | solution.py:302
  25.7 8.9 %collective-permute-start.8 = (bf16[200,256]{1,0:T(8,128)(2,1)S(1)}, bf16[200,256]{1,0:T(8,128)(2,1)S(1)}, u32[]{:S(2)}, u32[]{:S(2)}) collective-permute-start(bf16[200,256]{1,0:T(8,128)(2,1)S(1)} %shard_map.93), channel_id=1, source_target_pairs={{0,2},{1,3},{2,0},{3,1},{4,6},{5,7},{6,4},{7,5},{8,10},{9,11},{10,... | collective-permute-start | bytes 307208 | tf_op jit(solution)/shard_map/ppermute | solution.py:302
  26.2 8.4 %copy-start.2 = (s32[192]{0:T(256)S(1)}, s32[192]{0:T(256)}, u32[]{:S(2)}) copy-start(s32[192]{0:T(256)} %param.13) | copy-start | bytes 2308
  26.2 8.4 %collective-permute-start.7 = (bf16[200,256]{1,0:T(8,128)(2,1)S(1)}, bf16[200,256]{1,0:T(8,128)(2,1)S(1)}, u32[]{:S(2)}, u32[]{:S(2)}) collective-permute-start(bf16[200,256]{1,0:T(8,128)(2,1)S(1)} %shard_map.92), channel_id=1, source_target_pairs={{0,1},{1,0},{2,3},{3,2},{4,5},{5,4},{6,7},{7,6},{8,9},{9,8},{10,11... | collective-permute-start | bytes 307208 | tf_op jit(solution)/shard_map/ppermute | solution.py:302
  35.1 1.6 %collective-permute-start.10 = (bf16[512,256]{1,0:T(8,128)(2,1)S(1)}, bf16[512,256]{1,0:T(8,128)(2,1)S(1)}, u32[]{:S(2)}, u32[]{:S(2)}) collective-permute-start(bf16[512,256]{1,0:T(8,128)(2,1)S(1)} %get-tuple-element.29), channel_id=1, source_target_pairs={{0,4},{4,0},{8,12},{12,8},{16,20},{20,16},{24,28},{28,24},{1,5},{5... | collective-permute-start | bytes 786440 | tf_op jit(solution)/shard_map/ppermute | solution.py:293
  36.8 4.3 %collective-permute-start.11 = (bf16[128,256]{1,0:T(8,128)(2,1)S(1)}, bf16[128,256]{1,0:T(8,128)(2,1)S(1)}, u32[]{:S(2)}, u32[]{:S(2)}) collective-permute-start(bf16[128,256]{1,0:T(8,128)(2,1)S(1)} %get-tuple-element.31), channel_id=1, source_target_pairs={{0,8},{4,12},{8,0},{12,4},{16,24},{20,28},{24,16},{28,20},{1,9},{5... | collective-permute-start | bytes 196616 | tf_op jit(solution)/shard_map/ppermute | solution.py:293
  38.4 5.0 %collective-permute-start.12 = (bf16[128,256]{1,0:T(8,128)(2,1)S(1)}, bf16[128,256]{1,0:T(8,128)(2,1)S(1)}, u32[]{:S(2)}, u32[]{:S(2)}) collective-permute-start(bf16[128,256]{1,0:T(8,128)(2,1)S(1)} %get-tuple-element.32), channel_id=1, source_target_pairs={{0,16},{4,20},{8,24},{12,28},{16,0},{20,4},{24,8},{28,12},{1,17},{... | collective-permute-start | bytes 196616 | tf_op jit(solution)/shard_map/ppermute | solution.py:293
  39.1 5.2 %collective-permute-start.13 = (bf16[128,256]{1,0:T(8,128)(2,1)S(1)}, bf16[128,256]{1,0:T(8,128)(2,1)S(1)}, u32[]{:S(2)}, u32[]{:S(2)}) collective-permute-start(bf16[128,256]{1,0:T(8,128)(2,1)S(1)} %get-tuple-element.33), channel_id=1, source_target_pairs={{0,24},{4,28},{8,16},{12,20},{16,8},{20,12},{24,0},{28,4},{1,25},{... | collective-permute-start | bytes 196616 | tf_op jit(solution)/shard_map/ppermute | solution.py:293
  44.3 4.5 %collective-permute-start.14 = (bf16[128,256]{1,0:T(8,128)(2,1)S(1)}, bf16[128,256]{1,0:T(8,128)(2,1)S(1)}, u32[]{:S(2)}, u32[]{:S(2)}) collective-permute-start(bf16[128,256]{1,0:T(8,128)(2,1)S(1)} %shard_map.99.refs_0_), channel_id=1, source_target_pairs={{0,1},{1,0},{2,3},{3,2},{4,5},{5,4},{6,7},{7,6},{8,9},{9,8},{10,11... | collective-permute-start | bytes 196616 | tf_op jit(solution)/shard_map/ppermute | solution.py:302
  44.8 6.6 %collective-permute-start.15 = (bf16[128,256]{1,0:T(8,128)(2,1)S(1)}, bf16[128,256]{1,0:T(8,128)(2,1)S(1)}, u32[]{:S(2)}, u32[]{:S(2)}) collective-permute-start(bf16[128,256]{1,0:T(8,128)(2,1)S(1)} %shard_map.99.refs_0_), channel_id=1, source_target_pairs={{0,2},{1,3},{2,0},{3,1},{4,6},{5,7},{6,4},{7,5},{8,10},{9,11},{10,... | collective-permute-start | bytes 196616 | tf_op jit(solution)/shard_map/ppermute | solution.py:302
  47.4 6.1 %collective-permute-start.16 = (bf16[128,256]{1,0:T(8,128)(2,1)S(1)}, bf16[128,256]{1,0:T(8,128)(2,1)S(1)}, u32[]{:S(2)}, u32[]{:S(2)}) collective-permute-start(bf16[128,256]{1,0:T(8,128)(2,1)S(1)} %shard_map.99.refs_0_), channel_id=1, source_target_pairs={{0,3},{1,2},{2,1},{3,0},{4,7},{5,6},{6,5},{7,4},{8,11},{9,10},{10,... | collective-permute-start | bytes 196616 | tf_op jit(solution)/shard_map/ppermute | solution.py:302
  53.5 4.3 %collective-permute-start.18 = (bf16[128,256]{1,0:T(8,128)(2,1)S(1)}, bf16[128,256]{1,0:T(8,128)(2,1)S(1)}, u32[]{:S(2)}, u32[]{:S(2)}) collective-permute-start(bf16[128,256]{1,0:T(8,128)(2,1)S(1)} %shard_map.100.refs_0_), channel_id=1, source_target_pairs={{0,8},{4,12},{8,0},{12,4},{16,24},{20,28},{24,16},{28,20},{1,9},{5... | collective-permute-start | bytes 196616 | tf_op jit(solution)/shard_map/ppermute | solution.py:293
  54.1 4.3 %collective-permute-start.20 = (bf16[128,256]{1,0:T(8,128)(2,1)S(1)}, bf16[128,256]{1,0:T(8,128)(2,1)S(1)}, u32[]{:S(2)}, u32[]{:S(2)}) collective-permute-start(bf16[128,256]{1,0:T(8,128)(2,1)S(1)} %shard_map.100.refs_0_), channel_id=1, source_target_pairs={{0,16},{4,20},{8,24},{12,28},{16,0},{20,4},{24,8},{28,12},{1,17},{... | collective-permute-start | bytes 196616 | tf_op jit(solution)/shard_map/ppermute | solution.py:293
  55.4 5.2 %collective-permute-start.22 = (bf16[128,256]{1,0:T(8,128)(2,1)S(1)}, bf16[128,256]{1,0:T(8,128)(2,1)S(1)}, u32[]{:S(2)}, u32[]{:S(2)}) collective-permute-start(bf16[128,256]{1,0:T(8,128)(2,1)S(1)} %shard_map.100.refs_0_), channel_id=1, source_target_pairs={{0,24},{4,28},{8,16},{12,20},{16,8},{20,12},{24,0},{28,4},{1,25},{... | collective-permute-start | bytes 196616 | tf_op jit(solution)/shard_map/ppermute | solution.py:293
  57.0 5.2 %collective-permute-start.17 = (bf16[128,256]{1,0:T(8,128)(2,1)S(1)}, bf16[128,256]{1,0:T(8,128)(2,1)S(1)}, u32[]{:S(2)}, u32[]{:S(2)}) collective-permute-start(bf16[128,256]{1,0:T(8,128)(2,1)S(1)} %shard_map.100.refs_0_), channel_id=1, source_target_pairs={{0,4},{4,0},{8,12},{12,8},{16,20},{20,16},{24,28},{28,24},{1,5},{5... | collective-permute-start | bytes 196616 | tf_op jit(solution)/shard_map/ppermute | solution.py:293
  57.8 4.4 %collective-permute-start.19 = (bf16[128,256]{1,0:T(8,128)(2,1)S(1)}, bf16[128,256]{1,0:T(8,128)(2,1)S(1)}, u32[]{:S(2)}, u32[]{:S(2)}) collective-permute-start(bf16[128,256]{1,0:T(8,128)(2,1)S(1)} %collective-permute-done.18.refs_1_), channel_id=1, source_target_pairs={{0,4},{4,0},{8,12},{12,8},{16,20},{20,16},{24,28},{28,24},{1,5},{5... | collective-permute-start | bytes 196616 | tf_op jit(solution)/shard_map/ppermute | solution.py:293
  58.4 3.9 %collective-permute-start.21 = (bf16[128,256]{1,0:T(8,128)(2,1)S(1)}, bf16[128,256]{1,0:T(8,128)(2,1)S(1)}, u32[]{:S(2)}, u32[]{:S(2)}) collective-permute-start(bf16[128,256]{1,0:T(8,128)(2,1)S(1)} %collective-permute-done.20.refs_2_), channel_id=1, source_target_pairs={{0,4},{4,0},{8,12},{12,8},{16,20},{20,16},{24,28},{28,24},{1,5},{5... | collective-permute-start | bytes 196616 | tf_op jit(solution)/shard_map/ppermute | solution.py:293
  60.6 1.7 %collective-permute-start.23 = (bf16[128,256]{1,0:T(8,128)(2,1)S(1)}, bf16[128,256]{1,0:T(8,128)(2,1)S(1)}, u32[]{:S(2)}, u32[]{:S(2)}) collective-permute-start(bf16[128,256]{1,0:T(8,128)(2,1)S(1)} %collective-permute-done.22.refs_3_), channel_id=1, source_target_pairs={{0,4},{4,0},{8,12},{12,8},{16,20},{20,16},{24,28},{28,24},{1,5},{5... | collective-permute-start | bytes 196616 | tf_op jit(solution)/shard_map/ppermute | solution.py:293

commit v2 on v1

--- a/solution.py
+++ b/solution.py
@@ -60,7 +60,7 @@
     out_ref[...] = lax.broadcasted_iota(jnp.int32, out_ref.shape, 1)
 
 
-def prep_kernel(spot_ref, land_ref, vec_ref, deg_ref, val_ref, out_ref):
+def prep_kernel(spot_ref, land_ref, vec_ref, deg_ref, val_ref, out_ref, *halves):
     features = land_ref.shape[1]
     rows = land_ref.shape[0]
     for start in range(0, features, rows):
@@ -71,6 +71,14 @@
         jnp.where(here, jnp.broadcast_to(lax.rsqrt(deg_ref[...]), (rows, rows)), 0.0), 1, keepdims=True
     )
     out_ref[:, features:] = (vec_ref[...].astype(F32) * root / val_ref[...]).astype(BF16)
+    for n, half in enumerate(halves):
+        width = half.shape[1]
+        half[...] = out_ref[:, n * width : (n + 1) * width]
+
+
+def take(piece, start, size):
+    width = piece[0].shape[1]
+    return piece[start // width][:, start % width : start % width + size]
 
 
 def owner_of(place):
@@ -79,22 +87,22 @@
     return jnp.bitwise_xor(me, even if even == odd else jnp.where(me % 2 == 0, even, odd))
 
 
-def weigh(places, doc_ref, square_ref, mask_ref, pieces, low_ref, window, add_degree, add_total):
+def weigh(places, k, doc_ref, square_ref, mask_ref, pieces, low_ref, window, add_degree, add_total):
     base, count, step = window
     features = doc_ref.shape[1]
-    land_rows = pieces[0].shape[0]
+    land_rows = pieces[0][0].shape[0]
     width = len(pieces) * land_rows
     scale = 4.0 / features * LOG2E
     col = lax.axis_index("col")
     cols = lax.axis_size("col")
     lands = jnp.concatenate(
         [
-            jnp.concatenate([p[:, start : start + land_rows] for p in pieces], 1)
+            jnp.concatenate([take(p, start, land_rows) for p in pieces], 1)
             for start in range(0, features, land_rows)
         ],
         0,
     )
-    vectors = jnp.concatenate([p[:, features:] for p in pieces], 0)
+    vectors = jnp.concatenate([take(p, features, k) for p in pieces], 0)
     wide = lands.astype(F32)
     land_square = scale * jnp.sum(wide * wide, 0, keepdims=True)
     live = mask_ref[...].astype(F32)
@@ -129,8 +137,17 @@
     add_total(whole, jnp.dot(low_ref[:count, :width], vectors, preferred_element_type=F32))
 
 
+def split_parts(places, refs):
+    pieces = []
+    for count, _ in places:
+        pieces.append(refs[:count])
+        refs = refs[count:]
+    return pieces, refs
+
+
 def first_kernel(places, doc_ref, mask_ref, *refs):
-    pieces, (total_ref, degree_ref, square_ref, low_ref) = refs[:-4], refs[-4:]
+    pieces, (total_ref, degree_ref, square_ref, low_ref) = split_parts(places, refs)
+    total_k = total_ref.shape[1]
     scale = 4.0 / doc_ref.shape[1] * LOG2E
     for i in range(doc_ref.shape[0] // BLOCK):
         rows = pl.ds(i * BLOCK, BLOCK)
@@ -145,11 +162,12 @@
         total_ref[rows, :] = part
 
     window = 0, doc_ref.shape[0], BLOCK
-    weigh(places, doc_ref, square_ref, mask_ref, pieces, low_ref, window, add_degree, add_total)
+    weigh([place for _, place in places], total_k, doc_ref, square_ref, mask_ref, pieces, low_ref, window, add_degree, add_total)
 
 
 def more_kernel(places, doc_ref, square_ref, mask_ref, total_in, degree_in, *refs):
-    pieces, (total_ref, degree_ref, low_ref) = refs[:-3], refs[-3:]
+    pieces, (total_ref, degree_ref, low_ref) = split_parts(places, refs)
+    total_k = total_ref.shape[1]
 
     def add_degree(rows, local, part):
         degree_ref[rows, :] = degree_in[rows, :] + part
@@ -158,13 +176,14 @@
         total_ref[rows, :] = total_in[rows, :] + part
 
     window = 0, doc_ref.shape[0], BLOCK
-    weigh(places, doc_ref, square_ref, mask_ref, pieces, low_ref, window, add_degree, add_total)
+    weigh([place for _, place in places], total_k, doc_ref, square_ref, mask_ref, pieces, low_ref, window, add_degree, add_total)
 
 
 def part_kernel(mask, places, doc_ref, square_ref, mask_ref, total_in, degree_in, *refs):
-    pieces, refs = refs[: len(places)], refs[len(places) :]
+    pieces, refs = split_parts(places, refs)
     outs, (low_ref, part_ref) = refs[:-2], refs[-2:]
     n, k = low_ref.shape[0], total_in.shape[1]
+    total_k = k
     step = math.gcd(n, BLOCK)
     base = pl.multiple_of(jnp.bitwise_xor(lax.axis_index("col"), mask) * n, step)
     totals = []
@@ -176,7 +195,7 @@
         totals.append(total_in[rows, :] + part)
 
     window = base, n, step
-    weigh(places, doc_ref, square_ref, mask_ref, pieces, low_ref, window, add_degree, add_total)
+    weigh([place for _, place in places], total_k, doc_ref, square_ref, mask_ref, pieces, low_ref, window, add_degree, add_total)
     deg = to_row(jnp.sum(part_ref[...], 1, keepdims=True), k)
     if mask == 0:
         outs[0][...] = totals[0]
@@ -302,31 +321,35 @@
         return lax.ppermute(x, "col", [(i, i ^ mask) for i in range(cols)])
 
     spot = call(spot_kernel, [struct((8, land_rows), jnp.int32)], [], flops=HEAVY)[0]
-    own = call(
+    width = features + k
+    split_a = chips == 4 and width % (2 * land_rows) == 0 and features * 2 >= width
+    half = [struct((land_rows, width // 2), BF16)] * 2 if split_a else []
+    own, *halves = call(
         prep_kernel,
-        [struct((land_rows, features + k), BF16)],
+        [struct((land_rows, width), BF16)] + half,
         [spot, landmarks, eigen_vectors, land_degree.reshape(1, -1), eigen_values.reshape(1, -1)],
         flops=HEAVY,
-    )[0]
+    )
 
     if chips == 4:
         step_a = lambda i: i ^ 2 if i % 2 == 0 else i ^ 4
         step_b = lambda i: i ^ 4 if i % 2 == 0 else i ^ 2
-        got_a = swap(own, step_a)
+        got_a = [swap(x, step_a) for x in halves or [own]]
         got_b = swap(own, step_b)
-        got_f = swap(got_a, step_b)
-        far_own = core_swap(own)
-        far_a, far_b, far_f = core_swap(got_a), core_swap(got_b), core_swap(got_f)
+        got_f = [swap(x, step_b) for x in got_a]
+        far_own, far_b = core_swap(own), core_swap(got_b)
+        far_a = [core_swap(x) for x in got_a]
+        far_f = [core_swap(x) for x in got_f]
         groups = [
-            [(own, (0, 0)), (far_own, (1, 1))],
+            [([own], (0, 0)), ([far_own], (1, 1))],
             [(got_a, (2, 4)), (far_a, (5, 3))],
-            [(got_b, (4, 2)), (far_b, (3, 5))],
+            [([got_b], (4, 2)), ([far_b], (3, 5))],
             [(got_f, (6, 6)), (far_f, (7, 7))],
         ]
     else:
         near = [own] + [chip_swap(own, mask) for mask in range(1, chips)]
         groups = [
-            [(x, (2 * mask, 2 * mask)), (core_swap(x), (2 * mask + 1, 2 * mask + 1))]
+            [([x], (2 * mask, 2 * mask)), ([core_swap(x)], (2 * mask + 1, 2 * mask + 1))]
             for mask, x in enumerate(near)
         ]
 
@@ -334,8 +357,8 @@
     sums = [struct((doc_rows, k), F32), struct((doc_rows, 128), F32)]
 
     def run(kernel, group, outs, args, scratch, aliases=None, share=1):
-        places = [place for _, place in group]
-        args = args + [piece for piece, _ in group]
+        places = [(len(parts), place) for parts, place in group]
+        args = args + [part for parts, _ in group for part in parts]
         flops = len(group) * 2 * doc_rows * land_rows * (features + k) // share
         kernel = functools.partial(kernel, places)
         return call(kernel, outs, args, None, scratch, flops, aliases=aliases)

time: 63.3 us -> 63.5 us (level)
  starting transfers between devices: 23.6 us -> 24.4 us
    ppermute x18 -> x22, starting transfers between devices: 13.8 us -> 15.4 us  [swap(): return lax.ppermute(x, 'blk', [(i, pick(i)) for i in range(blks)])]
    ppermute x6, starting transfers between devices: 9.82 us -> 9.02 us  [col_swap(): return lax.ppermute(x, 'col', [(i, i ^ mask) for i in range(cols)])]
    ppermute x18 -> x22, waiting for transfers between devices: 18 us -> 17.6 us  [swap(): return lax.ppermute(x, 'blk', [(i, pick(i)) for i in range(blks)])]
  transfers between devices with their start and end apart: 24 -> 28, of which waited for: 13 -> 14; matrix products, arithmetic and copies ran while one was open for 0% -> 0% of each run, Pallas kernels for 9% -> 9%
where the time goes in v2:
time: 63.5 us; the launch traced here: 63.3 us
  waiting for transfers between devices  29.5 us (46%)
  starting transfers between devices  24.4 us (38%)
  Pallas kernels  7.65 us (12%)
  local copies, waits for them, and re-layouts  0.94 us (1%)
  between operations  0.87 us (1%)
    ppermute x22, waiting for transfers between devices, swap(): return lax.ppermute(x, 'blk', [(i, pick(i)) for i in range(blks)])  17.6 us
    ppermute x22, starting transfers between devices, swap(): return lax.ppermute(x, 'blk', [(i, pick(i)) for i in range(blks)])  15.4 us
    ppermute x6, waiting for transfers between devices, col_swap(): return lax.ppermute(x, 'col', [(i, i ^ mask) for i in range(cols)])  11.9 us
    ppermute x6, starting transfers between devices, col_swap(): return lax.ppermute(x, 'col', [(i, i ^ mask) for i in range(cols)])  9.02 us
    pallas_call x17, Pallas kernels, call(): pl.pallas_call(kernel, out_shape=outs, in_specs=specs or [VMEM] * len(arg...  7.65 us
  transfers between devices with their start and end apart: 28, of which 14 were waited for; matrix products, arithmetic and copies ran while one was open for 0% of the time, Pallas kernels for 9%

profile of v2, /device:TPU:0, one launch (start us, length us, event | category | flops | bytes accessed | tf_op | source)
XLA Modules:
  0.0 63.3 jit_solution(5334316819032002300)
XLA Ops:
  0.7 0.6 copy-done.6
  1.8 3.1 %collective-permute-start.5 = (bf16[128,1024]{1,0:T(8,128)(2,1)S(1)}, bf16[128,1024]{1,0:T(8,128)(2,1)S(1)}, u32[]{:S(2)}, u32[]{:S(2)}) collective-permute-start(bf16[128,1024]{1,0:T(8,128)(2,1)S(1)} %get-tuple-element.21.refs_0_), channel_id=1, source_target_pairs={{0,16},{4,12},{8,24},{12,4},{16,0},{20,28},{24,8},{28,20},{1,17},{... | collective-permute-start | bytes 786440 | tf_op jit(solution)/shard_map/ppermute | solution.py:312
  4.8 1.5 %collective-permute-start.2 = (bf16[128,512]{1,0:T(8,128)(2,1)S(1)}, bf16[128,512]{1,0:T(8,128)(2,1)S(1)}, u32[]{:S(2)}, u32[]{:S(2)}) collective-permute-start(bf16[128,512]{1,0:T(8,128)(2,1)S(1)} %get-tuple-element.26), channel_id=1, source_target_pairs={{0,8},{4,20},{8,0},{12,28},{16,24},{20,4},{24,16},{28,12},{1,9},{5... | collective-permute-start | bytes 393224 | tf_op jit(solution)/shard_map/ppermute | solution.py:312
  6.9 4.6 %collective-permute-done.5.refs_0_ = bf16[128,1024]{1,0:T(8,128)(2,1)S(1)} collective-permute-done((bf16[128,1024]{1,0:T(8,128)(2,1)S(1)}, bf16[128,1024]{1,0:T(8,128)(2,1)S(1)}, u32[]{:S(2)}, u32[]{:S(2)}) %collective-permute-start.5) | collective-permute-done | bytes 262176 | tf_op jit(solution)/shard_map/ppermute | solution.py:312
  11.5 2.5 %collective-permute-start.8 = (bf16[128,512]{1,0:T(8,128)(2,1)S(1)}, bf16[128,512]{1,0:T(8,128)(2,1)S(1)}, u32[]{:S(2)}, u32[]{:S(2)}) collective-permute-start(bf16[128,512]{1,0:T(8,128)(2,1)S(1)} %collective-permute-done.2.refs_1_), channel_id=1, source_target_pairs={{0,16},{4,12},{8,24},{12,4},{16,0},{20,28},{24,8},{28,20},{1,17},{... | collective-permute-start | bytes 393224 | tf_op jit(solution)/shard_map/ppermute | solution.py:312
  14.6 2.3 %collective-permute-done.8.refs_1_ = bf16[128,512]{1,0:T(8,128)(2,1)S(1)} collective-permute-done((bf16[128,512]{1,0:T(8,128)(2,1)S(1)}, bf16[128,512]{1,0:T(8,128)(2,1)S(1)}, u32[]{:S(2)}, u32[]{:S(2)}) %collective-permute-start.8) | collective-permute-done | bytes 131104 | tf_op jit(solution)/shard_map/ppermute | solution.py:312
  16.9 2.0 %collective-permute-done.7.refs_0_ = bf16[128,512]{1,0:T(8,128)(2,1)S(1)} collective-permute-done((bf16[128,512]{1,0:T(8,128)(2,1)S(1)}, bf16[128,512]{1,0:T(8,128)(2,1)S(1)}, u32[]{:S(2)}, u32[]{:S(2)}) %collective-permute-start.7) | collective-permute-done | bytes 131104 | tf_op jit(solution)/shard_map/ppermute | solution.py:312
  18.9 0.9 %shard_map.88 = (f32[768,256]{1,0:T(8,128)S(1)}, f32[768,128]{1,0:T(8,128)S(1)}, f32[768,128]{1,0:T(8,128)S(1)}) custom-call(bf16[768,768]{1,0:T(8,128)(2,1)S(1)} %copy-done, s32[6,32]{1,0:T(8,128)S(1)} %copy-done.1, bf16[128,1024]{1,0:T(8,128)(2,1)S(1)} %get-tuple-element.21.refs_0_, bf16[128,1024]{1,0:T(8,128)(2,1)S(1)} %collective-permute-done.refs_1_), custom_call_target="tpu_custom_call" | custom-call | flops 402653184 | bytes 3277568 | tf_op jit(solution)/shard_map/pallas_call | solution.py:27
  19.8 0.8 %shard_map.89 = (f32[768,256]{1,0:T(8,128)S(1)}, f32[768,128]{1,0:T(8,128)S(1)}) custom-call(bf16[768,768]{1,0:T(8,128)(2,1)S(1)} %copy-done, f32[768,128]{1,0:T(8,128)S(1)} %get-tuple-element.22.square_ref, s32[6,32]{1,0:T(8,128)S(1)} %copy-done.1, f32[768,256]{1,0:T(8,128)S(1)} %get-tuple-element.23.total_in, ...), custom_call_target="tpu_custom_call", output_to_operand_aliasing={{0}: (3, {}), {1}: (4, {})} | custom-call | flops 402653184 | bytes 4457216 | tf_op jit(solution)/shard_map/pallas_call | solution.py:27
  20.6 0.8 %shard_map.90 = (f32[768,256]{1,0:T(8,128)S(1)}, f32[768,128]{1,0:T(8,128)S(1)}) custom-call(bf16[768,768]{1,0:T(8,128)(2,1)S(1)} %copy-done, f32[768,128]{1,0:T(8,128)S(1)} %get-tuple-element.22.square_ref, s32[6,32]{1,0:T(8,128)S(1)} %copy-done.1, f32[768,256]{1,0:T(8,128)S(1)} %get-tuple-element.27.total_in, ...), custom_call_target="tpu_custom_call", output_to_operand_aliasing={{0}: (3, {}), {1}: (4, {})} | custom-call | flops 402653184 | bytes 4457216 | tf_op jit(solution)/shard_map/pallas_call | solution.py:27
  21.9 3.7 %collective-permute-start.13 = (bf16[200,256]{1,0:T(8,128)(2,1)S(1)}, bf16[200,256]{1,0:T(8,128)(2,1)S(1)}, u32[]{:S(2)}, u32[]{:S(2)}) collective-permute-start(bf16[200,256]{1,0:T(8,128)(2,1)S(1)} %shard_map.94), channel_id=1, source_target_pairs={{0,3},{1,2},{2,1},{3,0},{4,7},{5,6},{6,5},{7,4},{8,11},{9,10},{10,... | collective-permute-start | bytes 307208 | tf_op jit(solution)/shard_map/ppermute | solution.py:321
  26.4 0.8 %collective-permute-start.11 = (bf16[200,256]{1,0:T(8,128)(2,1)S(1)}, bf16[200,256]{1,0:T(8,128)(2,1)S(1)}, u32[]{:S(2)}, u32[]{:S(2)}) collective-permute-start(bf16[200,256]{1,0:T(8,128)(2,1)S(1)} %shard_map.92), channel_id=1, source_target_pairs={{0,1},{1,0},{2,3},{3,2},{4,5},{5,4},{6,7},{7,6},{8,9},{9,8},{10,11... | collective-permute-start | bytes 307208 | tf_op jit(solution)/shard_map/ppermute | solution.py:321
  27.7 1.9 %collective-permute-done.13.refs_2_ = bf16[200,256]{1,0:T(8,128)(2,1)S(1)} collective-permute-done((bf16[200,256]{1,0:T(8,128)(2,1)S(1)}, bf16[200,256]{1,0:T(8,128)(2,1)S(1)}, u32[]{:S(2)}, u32[]{:S(2)}) %collective-permute-start.13) | collective-permute-done | bytes 102432 | tf_op jit(solution)/shard_map/ppermute | solution.py:321
  29.6 5.2 %collective-permute-done.12.refs_1_ = bf16[200,256]{1,0:T(8,128)(2,1)S(1)} collective-permute-done((bf16[200,256]{1,0:T(8,128)(2,1)S(1)}, bf16[200,256]{1,0:T(8,128)(2,1)S(1)}, u32[]{:S(2)}, u32[]{:S(2)}) %collective-permute-start.12) | collective-permute-done | bytes 102432 | tf_op jit(solution)/shard_map/ppermute | solution.py:321
  35.7 1.2 %collective-permute-done.14.get_ref = bf16[512,256]{1,0:T(8,128)(2,1)S(1)} collective-permute-done((bf16[512,256]{1,0:T(8,128)(2,1)S(1)}, bf16[512,256]{1,0:T(8,128)(2,1)S(1)}, u32[]{:S(2)}, u32[]{:S(2)}) %collective-permute-start.14) | collective-permute-done | bytes 262176 | tf_op jit(solution)/shard_map/ppermute | solution.py:312
  37.0 1.6 %collective-permute-start.15 = (bf16[128,256]{1,0:T(8,128)(2,1)S(1)}, bf16[128,256]{1,0:T(8,128)(2,1)S(1)}, u32[]{:S(2)}, u32[]{:S(2)}) collective-permute-start(bf16[128,256]{1,0:T(8,128)(2,1)S(1)} %get-tuple-element.37), channel_id=1, source_target_pairs={{0,8},{4,12},{8,0},{12,4},{16,24},{20,28},{24,16},{28,20},{1,9},{5... | collective-permute-start | bytes 196616 | tf_op jit(solution)/shard_map/ppermute | solution.py:312
  38.6 1.4 %collective-permute-start.16 = (bf16[128,256]{1,0:T(8,128)(2,1)S(1)}, bf16[128,256]{1,0:T(8,128)(2,1)S(1)}, u32[]{:S(2)}, u32[]{:S(2)}) collective-permute-start(bf16[128,256]{1,0:T(8,128)(2,1)S(1)} %get-tuple-element.38), channel_id=1, source_target_pairs={{0,16},{4,20},{8,24},{12,28},{16,0},{20,4},{24,8},{28,12},{1,17},{... | collective-permute-start | bytes 196616 | tf_op jit(solution)/shard_map/ppermute | solution.py:312
  40.0 0.6 collective-permute-start.17
  40.6 0.8 %collective-permute-done.15.refs_1_ = bf16[128,256]{1,0:T(8,128)(2,1)S(1)} collective-permute-done((bf16[128,256]{1,0:T(8,128)(2,1)S(1)}, bf16[128,256]{1,0:T(8,128)(2,1)S(1)}, u32[]{:S(2)}, u32[]{:S(2)}) %collective-permute-start.15) | collective-permute-done | bytes 65568 | tf_op jit(solution)/shard_map/ppermute | solution.py:312
  41.3 1.5 %collective-permute-done.16.refs_2_ = bf16[128,256]{1,0:T(8,128)(2,1)S(1)} collective-permute-done((bf16[128,256]{1,0:T(8,128)(2,1)S(1)}, bf16[128,256]{1,0:T(8,128)(2,1)S(1)}, u32[]{:S(2)}, u32[]{:S(2)}) %collective-permute-start.16) | collective-permute-done | bytes 65568 | tf_op jit(solution)/shard_map/ppermute | solution.py:312
  42.9 2.3 %collective-permute-done.17.refs_3_ = bf16[128,256]{1,0:T(8,128)(2,1)S(1)} collective-permute-done((bf16[128,256]{1,0:T(8,128)(2,1)S(1)}, bf16[128,256]{1,0:T(8,128)(2,1)S(1)}, u32[]{:S(2)}, u32[]{:S(2)}) %collective-permute-start.17) | collective-permute-done | bytes 65568 | tf_op jit(solution)/shard_map/ppermute | solution.py:312
  45.7 2.6 %collective-permute-start.19 = (bf16[128,256]{1,0:T(8,128)(2,1)S(1)}, bf16[128,256]{1,0:T(8,128)(2,1)S(1)}, u32[]{:S(2)}, u32[]{:S(2)}) collective-permute-start(bf16[128,256]{1,0:T(8,128)(2,1)S(1)} %shard_map.99.refs_0_), channel_id=1, source_target_pairs={{0,2},{1,3},{2,0},{3,1},{4,6},{5,7},{6,4},{7,5},{8,10},{9,11},{10,... | collective-permute-start | bytes 196616 | tf_op jit(solution)/shard_map/ppermute | solution.py:321
  48.3 1.3 %collective-permute-start.20 = (bf16[128,256]{1,0:T(8,128)(2,1)S(1)}, bf16[128,256]{1,0:T(8,128)(2,1)S(1)}, u32[]{:S(2)}, u32[]{:S(2)}) collective-permute-start(bf16[128,256]{1,0:T(8,128)(2,1)S(1)} %shard_map.99.refs_0_), channel_id=1, source_target_pairs={{0,3},{1,2},{2,1},{3,0},{4,7},{5,6},{6,5},{7,4},{8,11},{9,10},{10,... | collective-permute-start | bytes 196616 | tf_op jit(solution)/shard_map/ppermute | solution.py:321
  49.7 2.6 %collective-permute-done.19.refs_2_ = bf16[128,256]{1,0:T(8,128)(2,1)S(1)} collective-permute-done((bf16[128,256]{1,0:T(8,128)(2,1)S(1)}, bf16[128,256]{1,0:T(8,128)(2,1)S(1)}, u32[]{:S(2)}, u32[]{:S(2)}) %collective-permute-start.19) | collective-permute-done | bytes 65568 | tf_op jit(solution)/shard_map/ppermute | solution.py:321
  52.3 2.1 %collective-permute-done.20.refs_3_ = bf16[128,256]{1,0:T(8,128)(2,1)S(1)} collective-permute-done((bf16[128,256]{1,0:T(8,128)(2,1)S(1)}, bf16[128,256]{1,0:T(8,128)(2,1)S(1)}, u32[]{:S(2)}, u32[]{:S(2)}) %collective-permute-start.20) | collective-permute-done | bytes 65568 | tf_op jit(solution)/shard_map/ppermute | solution.py:321
  55.0 0.6 collective-permute-start.24
  55.6 2.4 %collective-permute-start.26 = (bf16[128,256]{1,0:T(8,128)(2,1)S(1)}, bf16[128,256]{1,0:T(8,128)(2,1)S(1)}, u32[]{:S(2)}, u32[]{:S(2)}) collective-permute-start(bf16[128,256]{1,0:T(8,128)(2,1)S(1)} %shard_map.100.refs_0_), channel_id=1, source_target_pairs={{0,24},{4,28},{8,16},{12,20},{16,8},{20,12},{24,0},{28,4},{1,25},{... | collective-permute-start | bytes 196616 | tf_op jit(solution)/shard_map/ppermute | solution.py:312
  58.0 0.8 %collective-permute-done.22.refs_1_ = bf16[128,256]{1,0:T(8,128)(2,1)S(1)} collective-permute-done((bf16[128,256]{1,0:T(8,128)(2,1)S(1)}, bf16[128,256]{1,0:T(8,128)(2,1)S(1)}, u32[]{:S(2)}, u32[]{:S(2)}) %collective-permute-start.22) | collective-permute-done | bytes 65568 | tf_op jit(solution)/shard_map/ppermute | solution.py:312
  59.3 1.5 %collective-permute-done.26.refs_3_ = bf16[128,256]{1,0:T(8,128)(2,1)S(1)} collective-permute-done((bf16[128,256]{1,0:T(8,128)(2,1)S(1)}, bf16[128,256]{1,0:T(8,128)(2,1)S(1)}, u32[]{:S(2)}, u32[]{:S(2)}) %collective-permute-start.26) | collective-permute-done | bytes 65568 | tf_op jit(solution)/shard_map/ppermute | solution.py:312
  60.8 0.8 %shard_map.95 = f32[192,256]{1,0:T(8,128)} custom-call(f32[192,256]{1,0:T(8,128)S(1)} %get-tuple-element.31.own_ref, f32[8,256]{1,0:T(8,128)S(1)} %get-tuple-element.32.own_deg_ref, bf16[200,256]{1,0:T(8,128)(2,1)S(1)} %collective-permute-done.11.refs_0_, bf16[200,256]{1,0:T(8,128)(2,1)S(1)} %collective-permute-done.12.refs_1_, ...), custom_call_target="tpu_custom_call" | custom-call | flops 1000 | bytes 708608 | tf_op jit(solution)/shard_map/pallas_call | solution.py:27
  61.6 0.9 %shard_map.101.refs_4_ = f32[1000,256]{1,0:T(8,128)} custom-call(bf16[128,256]{1,0:T(8,128)(2,1)S(1)} %shard_map.100.refs_0_, bf16[128,256]{1,0:T(8,128)(2,1)S(1)} %collective-permute-done.22.refs_1_, bf16[128,256]{1,0:T(8,128)(2,1)S(1)} %collective-permute-done.24.refs_2_, bf16[128,256]{1,0:T(8,128)(2,1)S(1)} %collective-permute-done.26.refs_3_), custom_call_target="tpu_custom_call" | custom-call | flops 1000 | bytes 1286144 | tf_op jit(solution)/shard_map/pallas_call | solution.py:27
  62.5 0.8 %shard_map.102 = f32[1000,256]{1,0:T(8,128)} custom-call(bf16[128,256]{1,0:T(8,128)(2,1)S(1)} %collective-permute-done.21.refs_0_, bf16[128,256]{1,0:T(8,128)(2,1)S(1)} %collective-permute-done.23.refs_1_, bf16[128,256]{1,0:T(8,128)(2,1)S(1)} %collective-permute-done.25.refs_2_, ...), custom_call_target="tpu_custom_call", output_to_operand_aliasing={{}: (4, {})} | custom-call | flops 1000 | bytes 2310144 | tf_op jit(solution)/shard_map/pallas_call | solution.py:27
  (55 shorter events, 5.9 us)
Async XLA Ops:
  0.7 0.9 %copy-start.3 = (bf16[128,768]{1,0:T(8,128)(2,1)S(1)}, bf16[128,768]{1,0:T(8,128)(2,1)}, u32[]{:S(2)}) copy-start(bf16[128,768]{1,0:T(8,128)(2,1)} %land_ref.1) | copy-start | bytes 589828
  1.6 17.3 %copy-start = (bf16[768,768]{1,0:T(8,128)(2,1)S(1)}, bf16[768,768]{1,0:T(8,128)(2,1)}, u32[]{:S(2)}) copy-start(bf16[768,768]{1,0:T(8,128)(2,1)} %doc_ref.13) | copy-start | bytes 3538948
  1.6 17.3 %copy-start.1 = (s32[6,32]{1,0:T(8,128)S(1)}, s32[6,32]{1,0:T(8,128)}, u32[]{:S(2)}) copy-start(s32[6,32]{1,0:T(8,128)} %mask_ref.13) | copy-start | bytes 2308
  1.8 9.7 %collective-permute-start.5 = (bf16[128,1024]{1,0:T(8,128)(2,1)S(1)}, bf16[128,1024]{1,0:T(8,128)(2,1)S(1)}, u32[]{:S(2)}, u32[]{:S(2)}) collective-permute-start(bf16[128,1024]{1,0:T(8,128)(2,1)S(1)} %get-tuple-element.21.refs_0_), channel_id=1, source_target_pairs={{0,16},{4,12},{8,24},{12,4},{16,0},{20,28},{24,8},{28,20},{1,17},{... | collective-permute-start | bytes 786440 | tf_op jit(solution)/shard_map/ppermute | solution.py:312
  4.8 9.2 %collective-permute-start = (bf16[128,1024]{1,0:T(8,128)(2,1)S(1)}, bf16[128,1024]{1,0:T(8,128)(2,1)S(1)}, u32[]{:S(2)}, u32[]{:S(2)}) collective-permute-start(bf16[128,1024]{1,0:T(8,128)(2,1)S(1)} %get-tuple-element.21.refs_0_), channel_id=1, source_target_pairs={{0,4},{4,0},{8,12},{12,8},{16,20},{20,16},{24,28},{28,24},{1,5},{5... | collective-permute-start | bytes 786440 | tf_op jit(solution)/shard_map/ppermute | solution.py:312
  4.8 6.6 %collective-permute-start.2 = (bf16[128,512]{1,0:T(8,128)(2,1)S(1)}, bf16[128,512]{1,0:T(8,128)(2,1)S(1)}, u32[]{:S(2)}, u32[]{:S(2)}) collective-permute-start(bf16[128,512]{1,0:T(8,128)(2,1)S(1)} %get-tuple-element.26), channel_id=1, source_target_pairs={{0,8},{4,20},{8,0},{12,28},{16,24},{20,4},{24,16},{28,12},{1,9},{5... | collective-permute-start | bytes 393224 | tf_op jit(solution)/shard_map/ppermute | solution.py:312
  6.3 7.6 %collective-permute-start.1 = (bf16[128,512]{1,0:T(8,128)(2,1)S(1)}, bf16[128,512]{1,0:T(8,128)(2,1)S(1)}, u32[]{:S(2)}, u32[]{:S(2)}) collective-permute-start(bf16[128,512]{1,0:T(8,128)(2,1)S(1)} %get-tuple-element.25), channel_id=1, source_target_pairs={{0,8},{4,20},{8,0},{12,28},{16,24},{20,4},{24,16},{28,12},{1,9},{5... | collective-permute-start | bytes 393224 | tf_op jit(solution)/shard_map/ppermute | solution.py:312
  11.5 9.2 %collective-permute-start.6 = (bf16[128,1024]{1,0:T(8,128)(2,1)S(1)}, bf16[128,1024]{1,0:T(8,128)(2,1)S(1)}, u32[]{:S(2)}, u32[]{:S(2)}) collective-permute-start(bf16[128,1024]{1,0:T(8,128)(2,1)S(1)} %collective-permute-done.5.refs_0_), channel_id=1, source_target_pairs={{0,4},{4,0},{8,12},{12,8},{16,20},{20,16},{24,28},{28,24},{1,5},{5... | collective-permute-start | bytes 786440 | tf_op jit(solution)/shard_map/ppermute | solution.py:312
  11.5 5.4 %collective-permute-start.8 = (bf16[128,512]{1,0:T(8,128)(2,1)S(1)}, bf16[128,512]{1,0:T(8,128)(2,1)S(1)}, u32[]{:S(2)}, u32[]{:S(2)}) collective-permute-start(bf16[128,512]{1,0:T(8,128)(2,1)S(1)} %collective-permute-done.2.refs_1_), channel_id=1, source_target_pairs={{0,16},{4,12},{8,24},{12,4},{16,0},{20,28},{24,8},{28,20},{1,17},{... | collective-permute-start | bytes 393224 | tf_op jit(solution)/shard_map/ppermute | solution.py:312
  14.0 5.0 %collective-permute-start.7 = (bf16[128,512]{1,0:T(8,128)(2,1)S(1)}, bf16[128,512]{1,0:T(8,128)(2,1)S(1)}, u32[]{:S(2)}, u32[]{:S(2)}) collective-permute-start(bf16[128,512]{1,0:T(8,128)(2,1)S(1)} %collective-permute-done.1.refs_0_), channel_id=1, source_target_pairs={{0,16},{4,12},{8,24},{12,4},{16,0},{20,28},{24,8},{28,20},{1,17},{... | collective-permute-start | bytes 393224 | tf_op jit(solution)/shard_map/ppermute | solution.py:312
  14.0 5.8 %collective-permute-start.3 = (bf16[128,512]{1,0:T(8,128)(2,1)S(1)}, bf16[128,512]{1,0:T(8,128)(2,1)S(1)}, u32[]{:S(2)}, u32[]{:S(2)}) collective-permute-start(bf16[128,512]{1,0:T(8,128)(2,1)S(1)} %collective-permute-done.1.refs_0_), channel_id=1, source_target_pairs={{0,4},{4,0},{8,12},{12,8},{16,20},{20,16},{24,28},{28,24},{1,5},{5... | collective-permute-start | bytes 393224 | tf_op jit(solution)/shard_map/ppermute | solution.py:312
  14.0 5.8 %collective-permute-start.4 = (bf16[128,512]{1,0:T(8,128)(2,1)S(1)}, bf16[128,512]{1,0:T(8,128)(2,1)S(1)}, u32[]{:S(2)}, u32[]{:S(2)}) collective-permute-start(bf16[128,512]{1,0:T(8,128)(2,1)S(1)} %collective-permute-done.2.refs_1_), channel_id=1, source_target_pairs={{0,4},{4,0},{8,12},{12,8},{16,20},{20,16},{24,28},{28,24},{1,5},{5... | collective-permute-start | bytes 393224 | tf_op jit(solution)/shard_map/ppermute | solution.py:312
  16.9 4.6 %collective-permute-start.10 = (bf16[128,512]{1,0:T(8,128)(2,1)S(1)}, bf16[128,512]{1,0:T(8,128)(2,1)S(1)}, u32[]{:S(2)}, u32[]{:S(2)}) collective-permute-start(bf16[128,512]{1,0:T(8,128)(2,1)S(1)} %collective-permute-done.8.refs_1_), channel_id=1, source_target_pairs={{0,4},{4,0},{8,12},{12,8},{16,20},{20,16},{24,28},{28,24},{1,5},{5... | collective-permute-start | bytes 393224 | tf_op jit(solution)/shard_map/ppermute | solution.py:312
  18.9 2.5 %collective-permute-start.9 = (bf16[128,512]{1,0:T(8,128)(2,1)S(1)}, bf16[128,512]{1,0:T(8,128)(2,1)S(1)}, u32[]{:S(2)}, u32[]{:S(2)}) collective-permute-start(bf16[128,512]{1,0:T(8,128)(2,1)S(1)} %collective-permute-done.7.refs_0_), channel_id=1, source_target_pairs={{0,4},{4,0},{8,12},{12,8},{16,20},{20,16},{24,28},{28,24},{1,5},{5... | collective-permute-start | bytes 393224 | tf_op jit(solution)/shard_map/ppermute | solution.py:312
  21.9 7.7 %collective-permute-start.13 = (bf16[200,256]{1,0:T(8,128)(2,1)S(1)}, bf16[200,256]{1,0:T(8,128)(2,1)S(1)}, u32[]{:S(2)}, u32[]{:S(2)}) collective-permute-start(bf16[200,256]{1,0:T(8,128)(2,1)S(1)} %shard_map.94), channel_id=1, source_target_pairs={{0,3},{1,2},{2,1},{3,0},{4,7},{5,6},{6,5},{7,4},{8,11},{9,10},{10,... | collective-permute-start | bytes 307208 | tf_op jit(solution)/shard_map/ppermute | solution.py:321
  25.9 8.9 %collective-permute-start.12 = (bf16[200,256]{1,0:T(8,128)(2,1)S(1)}, bf16[200,256]{1,0:T(8,128)(2,1)S(1)}, u32[]{:S(2)}, u32[]{:S(2)}) collective-permute-start(bf16[200,256]{1,0:T(8,128)(2,1)S(1)} %shard_map.93), channel_id=1, source_target_pairs={{0,2},{1,3},{2,0},{3,1},{4,6},{5,7},{6,4},{7,5},{8,10},{9,11},{10,... | collective-permute-start | bytes 307208 | tf_op jit(solution)/shard_map/ppermute | solution.py:321
  26.4 8.4 %copy-start.2 = (s32[192]{0:T(256)S(1)}, s32[192]{0:T(256)}, u32[]{:S(2)}) copy-start(s32[192]{0:T(256)} %param.13) | copy-start | bytes 2308
  26.4 8.4 %collective-permute-start.11 = (bf16[200,256]{1,0:T(8,128)(2,1)S(1)}, bf16[200,256]{1,0:T(8,128)(2,1)S(1)}, u32[]{:S(2)}, u32[]{:S(2)}) collective-permute-start(bf16[200,256]{1,0:T(8,128)(2,1)S(1)} %shard_map.92), channel_id=1, source_target_pairs={{0,1},{1,0},{2,3},{3,2},{4,5},{5,4},{6,7},{7,6},{8,9},{9,8},{10,11... | collective-permute-start | bytes 307208 | tf_op jit(solution)/shard_map/ppermute | solution.py:321
  35.3 1.6 %collective-permute-start.14 = (bf16[512,256]{1,0:T(8,128)(2,1)S(1)}, bf16[512,256]{1,0:T(8,128)(2,1)S(1)}, u32[]{:S(2)}, u32[]{:S(2)}) collective-permute-start(bf16[512,256]{1,0:T(8,128)(2,1)S(1)} %get-tuple-element.35), channel_id=1, source_target_pairs={{0,4},{4,0},{8,12},{12,8},{16,20},{20,16},{24,28},{28,24},{1,5},{5... | collective-permute-start | bytes 786440 | tf_op jit(solution)/shard_map/ppermute | solution.py:312
  37.0 4.3 %collective-permute-start.15 = (bf16[128,256]{1,0:T(8,128)(2,1)S(1)}, bf16[128,256]{1,0:T(8,128)(2,1)S(1)}, u32[]{:S(2)}, u32[]{:S(2)}) collective-permute-start(bf16[128,256]{1,0:T(8,128)(2,1)S(1)} %get-tuple-element.37), channel_id=1, source_target_pairs={{0,8},{4,12},{8,0},{12,4},{16,24},{20,28},{24,16},{28,20},{1,9},{5... | collective-permute-start | bytes 196616 | tf_op jit(solution)/shard_map/ppermute | solution.py:312
  38.6 4.3 %collective-permute-start.16 = (bf16[128,256]{1,0:T(8,128)(2,1)S(1)}, bf16[128,256]{1,0:T(8,128)(2,1)S(1)}, u32[]{:S(2)}, u32[]{:S(2)}) collective-permute-start(bf16[128,256]{1,0:T(8,128)(2,1)S(1)} %get-tuple-element.38), channel_id=1, source_target_pairs={{0,16},{4,20},{8,24},{12,28},{16,0},{20,4},{24,8},{28,12},{1,17},{... | collective-permute-start | bytes 196616 | tf_op jit(solution)/shard_map/ppermute | solution.py:312
  40.0 5.2 %collective-permute-start.17 = (bf16[128,256]{1,0:T(8,128)(2,1)S(1)}, bf16[128,256]{1,0:T(8,128)(2,1)S(1)}, u32[]{:S(2)}, u32[]{:S(2)}) collective-permute-start(bf16[128,256]{1,0:T(8,128)(2,1)S(1)} %get-tuple-element.39), channel_id=1, source_target_pairs={{0,24},{4,28},{8,16},{12,20},{16,8},{20,12},{24,0},{28,4},{1,25},{... | collective-permute-start | bytes 196616 | tf_op jit(solution)/shard_map/ppermute | solution.py:312
  45.2 4.5 %collective-permute-start.18 = (bf16[128,256]{1,0:T(8,128)(2,1)S(1)}, bf16[128,256]{1,0:T(8,128)(2,1)S(1)}, u32[]{:S(2)}, u32[]{:S(2)}) collective-permute-start(bf16[128,256]{1,0:T(8,128)(2,1)S(1)} %shard_map.99.refs_0_), channel_id=1, source_target_pairs={{0,1},{1,0},{2,3},{3,2},{4,5},{5,4},{6,7},{7,6},{8,9},{9,8},{10,11... | collective-permute-start | bytes 196616 | tf_op jit(solution)/shard_map/ppermute | solution.py:321
  45.7 6.6 %collective-permute-start.19 = (bf16[128,256]{1,0:T(8,128)(2,1)S(1)}, bf16[128,256]{1,0:T(8,128)(2,1)S(1)}, u32[]{:S(2)}, u32[]{:S(2)}) collective-permute-start(bf16[128,256]{1,0:T(8,128)(2,1)S(1)} %shard_map.99.refs_0_), channel_id=1, source_target_pairs={{0,2},{1,3},{2,0},{3,1},{4,6},{5,7},{6,4},{7,5},{8,10},{9,11},{10,... | collective-permute-start | bytes 196616 | tf_op jit(solution)/shard_map/ppermute | solution.py:321
  48.3 6.1 %collective-permute-start.20 = (bf16[128,256]{1,0:T(8,128)(2,1)S(1)}, bf16[128,256]{1,0:T(8,128)(2,1)S(1)}, u32[]{:S(2)}, u32[]{:S(2)}) collective-permute-start(bf16[128,256]{1,0:T(8,128)(2,1)S(1)} %shard_map.99.refs_0_), channel_id=1, source_target_pairs={{0,3},{1,2},{2,1},{3,0},{4,7},{5,6},{6,5},{7,4},{8,11},{9,10},{10,... | collective-permute-start | bytes 196616 | tf_op jit(solution)/shard_map/ppermute | solution.py:321
  54.4 4.3 %collective-permute-start.22 = (bf16[128,256]{1,0:T(8,128)(2,1)S(1)}, bf16[128,256]{1,0:T(8,128)(2,1)S(1)}, u32[]{:S(2)}, u32[]{:S(2)}) collective-permute-start(bf16[128,256]{1,0:T(8,128)(2,1)S(1)} %shard_map.100.refs_0_), channel_id=1, source_target_pairs={{0,8},{4,12},{8,0},{12,4},{16,24},{20,28},{24,16},{28,20},{1,9},{5... | collective-permute-start | bytes 196616 | tf_op jit(solution)/shard_map/ppermute | solution.py:312
  55.0 4.3 %collective-permute-start.24 = (bf16[128,256]{1,0:T(8,128)(2,1)S(1)}, bf16[128,256]{1,0:T(8,128)(2,1)S(1)}, u32[]{:S(2)}, u32[]{:S(2)}) collective-permute-start(bf16[128,256]{1,0:T(8,128)(2,1)S(1)} %shard_map.100.refs_0_), channel_id=1, source_target_pairs={{0,16},{4,20},{8,24},{12,28},{16,0},{20,4},{24,8},{28,12},{1,17},{... | collective-permute-start | bytes 196616 | tf_op jit(solution)/shard_map/ppermute | solution.py:312
  55.6 5.2 %collective-permute-start.26 = (bf16[128,256]{1,0:T(8,128)(2,1)S(1)}, bf16[128,256]{1,0:T(8,128)(2,1)S(1)}, u32[]{:S(2)}, u32[]{:S(2)}) collective-permute-start(bf16[128,256]{1,0:T(8,128)(2,1)S(1)} %shard_map.100.refs_0_), channel_id=1, source_target_pairs={{0,24},{4,28},{8,16},{12,20},{16,8},{20,12},{24,0},{28,4},{1,25},{... | collective-permute-start | bytes 196616 | tf_op jit(solution)/shard_map/ppermute | solution.py:312
  58.0 4.5 %collective-permute-start.21 = (bf16[128,256]{1,0:T(8,128)(2,1)S(1)}, bf16[128,256]{1,0:T(8,128)(2,1)S(1)}, u32[]{:S(2)}, u32[]{:S(2)}) collective-permute-start(bf16[128,256]{1,0:T(8,128)(2,1)S(1)} %shard_map.100.refs_0_), channel_id=1, source_target_pairs={{0,4},{4,0},{8,12},{12,8},{16,20},{20,16},{24,28},{28,24},{1,5},{5... | collective-permute-start | bytes 196616 | tf_op jit(solution)/shard_map/ppermute | solution.py:312
  58.7 3.7 %collective-permute-start.23 = (bf16[128,256]{1,0:T(8,128)(2,1)S(1)}, bf16[128,256]{1,0:T(8,128)(2,1)S(1)}, u32[]{:S(2)}, u32[]{:S(2)}) collective-permute-start(bf16[128,256]{1,0:T(8,128)(2,1)S(1)} %collective-permute-done.22.refs_1_), channel_id=1, source_target_pairs={{0,4},{4,0},{8,12},{12,8},{16,20},{20,16},{24,28},{28,24},{1,5},{5... | collective-permute-start | bytes 196616 | tf_op jit(solution)/shard_map/ppermute | solution.py:312
  59.2 3.2 %collective-permute-start.25 = (bf16[128,256]{1,0:T(8,128)(2,1)S(1)}, bf16[128,256]{1,0:T(8,128)(2,1)S(1)}, u32[]{:S(2)}, u32[]{:S(2)}) collective-permute-start(bf16[128,256]{1,0:T(8,128)(2,1)S(1)} %collective-permute-done.24.refs_2_), channel_id=1, source_target_pairs={{0,4},{4,0},{8,12},{12,8},{16,20},{20,16},{24,28},{28,24},{1,5},{5... | collective-permute-start | bytes 196616 | tf_op jit(solution)/shard_map/ppermute | solution.py:312
  60.8 1.7 %collective-permute-start.27 = (bf16[128,256]{1,0:T(8,128)(2,1)S(1)}, bf16[128,256]{1,0:T(8,128)(2,1)S(1)}, u32[]{:S(2)}, u32[]{:S(2)}) collective-permute-start(bf16[128,256]{1,0:T(8,128)(2,1)S(1)} %collective-permute-done.26.refs_3_), channel_id=1, source_target_pairs={{0,4},{4,0},{8,12},{12,8},{16,20},{20,16},{24,28},{28,24},{1,5},{5... | collective-permute-start | bytes 196616 | tf_op jit(solution)/shard_map/ppermute | solution.py:312
  (3 other events, 2.3 us)

commit v3 on v2

--- a/solution.py
+++ b/solution.py
@@ -287,16 +287,17 @@
             out_hbm.at[pl.ds(pl.multiple_of(jnp.minimum(owner, whole - 1) * size, 8), size), :],
             sem.at[n],
         )
-        copies.append((owner < whole, full))
+        here = [(owner < whole, full)]
         if rest:
             end = pltpu.make_async_copy(
                 wide_ref.at[n, pl.ds(0, rest), :], out_hbm.at[pl.ds(whole * size, rest), :], sem.at[n]
             )
-            copies.append((owner == whole, end))
-    for here, copy in copies:
-        pl.when(here)(copy.start)
-    for here, copy in copies:
-        pl.when(here)(copy.wait)
+            here.append((owner == whole, end))
+        for flag, copy in here:
+            pl.when(flag)(copy.start)
+        copies += here
+    for flag, copy in copies:
+        pl.when(flag)(copy.wait)
 
 
 def body(documents, landmarks, eigen_vectors, land_degree, eigen_values, tile_mask, labels):
@@ -394,15 +395,16 @@
     far = [core_swap(x) for x in near]
     centroids = None
     hbm = pl.BlockSpec(memory_space=pl.ANY)
-    for core, chunks in enumerate((near, far)):
+    chunks = [(x, 2 * mask) for mask, x in enumerate(near)] + [(x, 2 * mask + 1) for mask, x in enumerate(far)]
+    for some in (chunks[: chips + 1], chunks[chips + 1 :]):
         extra = [] if centroids is None else [centroids]
         centroids = call(
-            functools.partial(place_kernel, [2 * mask + core for mask in range(chips)], bool(extra)),
+            functools.partial(place_kernel, [place for _, place in some], bool(extra)),
             [struct((C, k), F32)],
-            chunks + extra,
-            [VMEM] * chips + [hbm] * len(extra),
-            [pltpu.VMEM((chips, size, k), F32), pltpu.SemaphoreType.DMA((chips,))],
-            aliases={chips: 0} if extra else None,
+            [x for x, _ in some] + extra,
+            [VMEM] * len(some) + [hbm] * len(extra),
+            [pltpu.VMEM((len(some), size, k), F32), pltpu.SemaphoreType.DMA((len(some),))],
+            aliases={len(some): 0} if extra else None,
             out_specs=[hbm],
         )[0]
     return (embedding, centroids)

time: 63.5 us -> 63.5 us (level)
  no operation moved by 1% of the time
where the time goes in v3:
time: 63.5 us; the launch traced here: 63.3 us
  waiting for transfers between devices  29.5 us (46%)
  starting transfers between devices  24.4 us (38%)
  Pallas kernels  7.61 us (12%)
  local copies, waits for them, and re-layouts  0.94 us (1%)
  between operations  0.86 us (1%)
    ppermute x22, waiting for transfers between devices, swap(): return lax.ppermute(x, 'blk', [(i, pick(i)) for i in range(blks)])  17.6 us
    ppermute x22, starting transfers between devices, swap(): return lax.ppermute(x, 'blk', [(i, pick(i)) for i in range(blks)])  15.4 us
    ppermute x6, waiting for transfers between devices, col_swap(): return lax.ppermute(x, 'col', [(i, i ^ mask) for i in range(cols)])  11.9 us
    ppermute x6, starting transfers between devices, col_swap(): return lax.ppermute(x, 'col', [(i, i ^ mask) for i in range(cols)])  9.02 us
    pallas_call x17, Pallas kernels, call(): pl.pallas_call(kernel, out_shape=outs, in_specs=specs or [VMEM] * len(arg...  7.61 us
  transfers between devices with their start and end apart: 28, of which 14 were waited for; matrix products, arithmetic and copies ran while one was open for 0% of the time, Pallas kernels for 9%

profile of v3, /device:TPU:0, one launch (start us, length us, event | category | flops | bytes accessed | tf_op | source)
XLA Modules:
  0.0 63.3 jit_solution(12632060624464671432)
XLA Ops:
  0.7 0.6 copy-done.6
  1.8 3.1 %collective-permute-start.5 = (bf16[128,1024]{1,0:T(8,128)(2,1)S(1)}, bf16[128,1024]{1,0:T(8,128)(2,1)S(1)}, u32[]{:S(2)}, u32[]{:S(2)}) collective-permute-start(bf16[128,1024]{1,0:T(8,128)(2,1)S(1)} %get-tuple-element.21.refs_0_), channel_id=1, source_target_pairs={{0,16},{4,12},{8,24},{12,4},{16,0},{20,28},{24,8},{28,20},{1,17},{... | collective-permute-start | bytes 786440 | tf_op jit(solution)/shard_map/ppermute | solution.py:313
  4.8 1.5 %collective-permute-start.2 = (bf16[128,512]{1,0:T(8,128)(2,1)S(1)}, bf16[128,512]{1,0:T(8,128)(2,1)S(1)}, u32[]{:S(2)}, u32[]{:S(2)}) collective-permute-start(bf16[128,512]{1,0:T(8,128)(2,1)S(1)} %get-tuple-element.26), channel_id=1, source_target_pairs={{0,8},{4,20},{8,0},{12,28},{16,24},{20,4},{24,16},{28,12},{1,9},{5... | collective-permute-start | bytes 393224 | tf_op jit(solution)/shard_map/ppermute | solution.py:313
  6.9 4.6 %collective-permute-done.5.refs_0_ = bf16[128,1024]{1,0:T(8,128)(2,1)S(1)} collective-permute-done((bf16[128,1024]{1,0:T(8,128)(2,1)S(1)}, bf16[128,1024]{1,0:T(8,128)(2,1)S(1)}, u32[]{:S(2)}, u32[]{:S(2)}) %collective-permute-start.5) | collective-permute-done | bytes 262176 | tf_op jit(solution)/shard_map/ppermute | solution.py:313
  11.5 2.5 %collective-permute-start.8 = (bf16[128,512]{1,0:T(8,128)(2,1)S(1)}, bf16[128,512]{1,0:T(8,128)(2,1)S(1)}, u32[]{:S(2)}, u32[]{:S(2)}) collective-permute-start(bf16[128,512]{1,0:T(8,128)(2,1)S(1)} %collective-permute-done.2.refs_1_), channel_id=1, source_target_pairs={{0,16},{4,12},{8,24},{12,4},{16,0},{20,28},{24,8},{28,20},{1,17},{... | collective-permute-start | bytes 393224 | tf_op jit(solution)/shard_map/ppermute | solution.py:313
  14.6 2.3 %collective-permute-done.8.refs_1_ = bf16[128,512]{1,0:T(8,128)(2,1)S(1)} collective-permute-done((bf16[128,512]{1,0:T(8,128)(2,1)S(1)}, bf16[128,512]{1,0:T(8,128)(2,1)S(1)}, u32[]{:S(2)}, u32[]{:S(2)}) %collective-permute-start.8) | collective-permute-done | bytes 131104 | tf_op jit(solution)/shard_map/ppermute | solution.py:313
  16.9 2.0 %collective-permute-done.7.refs_0_ = bf16[128,512]{1,0:T(8,128)(2,1)S(1)} collective-permute-done((bf16[128,512]{1,0:T(8,128)(2,1)S(1)}, bf16[128,512]{1,0:T(8,128)(2,1)S(1)}, u32[]{:S(2)}, u32[]{:S(2)}) %collective-permute-start.7) | collective-permute-done | bytes 131104 | tf_op jit(solution)/shard_map/ppermute | solution.py:313
  18.9 0.9 %shard_map.88 = (f32[768,256]{1,0:T(8,128)S(1)}, f32[768,128]{1,0:T(8,128)S(1)}, f32[768,128]{1,0:T(8,128)S(1)}) custom-call(bf16[768,768]{1,0:T(8,128)(2,1)S(1)} %copy-done, s32[6,32]{1,0:T(8,128)S(1)} %copy-done.1, bf16[128,1024]{1,0:T(8,128)(2,1)S(1)} %get-tuple-element.21.refs_0_, bf16[128,1024]{1,0:T(8,128)(2,1)S(1)} %collective-permute-done.refs_1_), custom_call_target="tpu_custom_call" | custom-call | flops 402653184 | bytes 3277568 | tf_op jit(solution)/shard_map/pallas_call | solution.py:27
  19.8 0.8 %shard_map.89 = (f32[768,256]{1,0:T(8,128)S(1)}, f32[768,128]{1,0:T(8,128)S(1)}) custom-call(bf16[768,768]{1,0:T(8,128)(2,1)S(1)} %copy-done, f32[768,128]{1,0:T(8,128)S(1)} %get-tuple-element.22.square_ref, s32[6,32]{1,0:T(8,128)S(1)} %copy-done.1, f32[768,256]{1,0:T(8,128)S(1)} %get-tuple-element.23.total_in, ...), custom_call_target="tpu_custom_call", output_to_operand_aliasing={{0}: (3, {}), {1}: (4, {})} | custom-call | flops 402653184 | bytes 4457216 | tf_op jit(solution)/shard_map/pallas_call | solution.py:27
  20.6 0.8 %shard_map.90 = (f32[768,256]{1,0:T(8,128)S(1)}, f32[768,128]{1,0:T(8,128)S(1)}) custom-call(bf16[768,768]{1,0:T(8,128)(2,1)S(1)} %copy-done, f32[768,128]{1,0:T(8,128)S(1)} %get-tuple-element.22.square_ref, s32[6,32]{1,0:T(8,128)S(1)} %copy-done.1, f32[768,256]{1,0:T(8,128)S(1)} %get-tuple-element.27.total_in, ...), custom_call_target="tpu_custom_call", output_to_operand_aliasing={{0}: (3, {}), {1}: (4, {})} | custom-call | flops 402653184 | bytes 4457216 | tf_op jit(solution)/shard_map/pallas_call | solution.py:27
  21.9 3.7 %collective-permute-start.13 = (bf16[200,256]{1,0:T(8,128)(2,1)S(1)}, bf16[200,256]{1,0:T(8,128)(2,1)S(1)}, u32[]{:S(2)}, u32[]{:S(2)}) collective-permute-start(bf16[200,256]{1,0:T(8,128)(2,1)S(1)} %shard_map.94), channel_id=1, source_target_pairs={{0,3},{1,2},{2,1},{3,0},{4,7},{5,6},{6,5},{7,4},{8,11},{9,10},{10,... | collective-permute-start | bytes 307208 | tf_op jit(solution)/shard_map/ppermute | solution.py:322
  26.4 0.8 %collective-permute-start.11 = (bf16[200,256]{1,0:T(8,128)(2,1)S(1)}, bf16[200,256]{1,0:T(8,128)(2,1)S(1)}, u32[]{:S(2)}, u32[]{:S(2)}) collective-permute-start(bf16[200,256]{1,0:T(8,128)(2,1)S(1)} %shard_map.92), channel_id=1, source_target_pairs={{0,1},{1,0},{2,3},{3,2},{4,5},{5,4},{6,7},{7,6},{8,9},{9,8},{10,11... | collective-permute-start | bytes 307208 | tf_op jit(solution)/shard_map/ppermute | solution.py:322
  27.7 1.9 %collective-permute-done.13.refs_2_ = bf16[200,256]{1,0:T(8,128)(2,1)S(1)} collective-permute-done((bf16[200,256]{1,0:T(8,128)(2,1)S(1)}, bf16[200,256]{1,0:T(8,128)(2,1)S(1)}, u32[]{:S(2)}, u32[]{:S(2)}) %collective-permute-start.13) | collective-permute-done | bytes 102432 | tf_op jit(solution)/shard_map/ppermute | solution.py:322
  29.6 5.2 %collective-permute-done.12.refs_1_ = bf16[200,256]{1,0:T(8,128)(2,1)S(1)} collective-permute-done((bf16[200,256]{1,0:T(8,128)(2,1)S(1)}, bf16[200,256]{1,0:T(8,128)(2,1)S(1)}, u32[]{:S(2)}, u32[]{:S(2)}) %collective-permute-start.12) | collective-permute-done | bytes 102432 | tf_op jit(solution)/shard_map/ppermute | solution.py:322
  35.7 1.2 %collective-permute-done.14.get_ref = bf16[512,256]{1,0:T(8,128)(2,1)S(1)} collective-permute-done((bf16[512,256]{1,0:T(8,128)(2,1)S(1)}, bf16[512,256]{1,0:T(8,128)(2,1)S(1)}, u32[]{:S(2)}, u32[]{:S(2)}) %collective-permute-start.14) | collective-permute-done | bytes 262176 | tf_op jit(solution)/shard_map/ppermute | solution.py:313
  37.0 1.6 %collective-permute-start.15 = (bf16[128,256]{1,0:T(8,128)(2,1)S(1)}, bf16[128,256]{1,0:T(8,128)(2,1)S(1)}, u32[]{:S(2)}, u32[]{:S(2)}) collective-permute-start(bf16[128,256]{1,0:T(8,128)(2,1)S(1)} %get-tuple-element.37), channel_id=1, source_target_pairs={{0,8},{4,12},{8,0},{12,4},{16,24},{20,28},{24,16},{28,20},{1,9},{5... | collective-permute-start | bytes 196616 | tf_op jit(solution)/shard_map/ppermute | solution.py:313
  38.6 1.4 %collective-permute-start.16 = (bf16[128,256]{1,0:T(8,128)(2,1)S(1)}, bf16[128,256]{1,0:T(8,128)(2,1)S(1)}, u32[]{:S(2)}, u32[]{:S(2)}) collective-permute-start(bf16[128,256]{1,0:T(8,128)(2,1)S(1)} %get-tuple-element.38), channel_id=1, source_target_pairs={{0,16},{4,20},{8,24},{12,28},{16,0},{20,4},{24,8},{28,12},{1,17},{... | collective-permute-start | bytes 196616 | tf_op jit(solution)/shard_map/ppermute | solution.py:313
  40.0 0.6 collective-permute-start.17
  40.6 0.8 %collective-permute-done.15.refs_1_ = bf16[128,256]{1,0:T(8,128)(2,1)S(1)} collective-permute-done((bf16[128,256]{1,0:T(8,128)(2,1)S(1)}, bf16[128,256]{1,0:T(8,128)(2,1)S(1)}, u32[]{:S(2)}, u32[]{:S(2)}) %collective-permute-start.15) | collective-permute-done | bytes 65568 | tf_op jit(solution)/shard_map/ppermute | solution.py:313
  41.3 1.5 %collective-permute-done.16.refs_2_ = bf16[128,256]{1,0:T(8,128)(2,1)S(1)} collective-permute-done((bf16[128,256]{1,0:T(8,128)(2,1)S(1)}, bf16[128,256]{1,0:T(8,128)(2,1)S(1)}, u32[]{:S(2)}, u32[]{:S(2)}) %collective-permute-start.16) | collective-permute-done | bytes 65568 | tf_op jit(solution)/shard_map/ppermute | solution.py:313
  42.9 2.3 %collective-permute-done.17.refs_3_ = bf16[128,256]{1,0:T(8,128)(2,1)S(1)} collective-permute-done((bf16[128,256]{1,0:T(8,128)(2,1)S(1)}, bf16[128,256]{1,0:T(8,128)(2,1)S(1)}, u32[]{:S(2)}, u32[]{:S(2)}) %collective-permute-start.17) | collective-permute-done | bytes 65568 | tf_op jit(solution)/shard_map/ppermute | solution.py:313
  45.7 2.6 %collective-permute-start.19 = (bf16[128,256]{1,0:T(8,128)(2,1)S(1)}, bf16[128,256]{1,0:T(8,128)(2,1)S(1)}, u32[]{:S(2)}, u32[]{:S(2)}) collective-permute-start(bf16[128,256]{1,0:T(8,128)(2,1)S(1)} %shard_map.99.refs_0_), channel_id=1, source_target_pairs={{0,2},{1,3},{2,0},{3,1},{4,6},{5,7},{6,4},{7,5},{8,10},{9,11},{10,... | collective-permute-start | bytes 196616 | tf_op jit(solution)/shard_map/ppermute | solution.py:322
  48.3 1.3 %collective-permute-start.20 = (bf16[128,256]{1,0:T(8,128)(2,1)S(1)}, bf16[128,256]{1,0:T(8,128)(2,1)S(1)}, u32[]{:S(2)}, u32[]{:S(2)}) collective-permute-start(bf16[128,256]{1,0:T(8,128)(2,1)S(1)} %shard_map.99.refs_0_), channel_id=1, source_target_pairs={{0,3},{1,2},{2,1},{3,0},{4,7},{5,6},{6,5},{7,4},{8,11},{9,10},{10,... | collective-permute-start | bytes 196616 | tf_op jit(solution)/shard_map/ppermute | solution.py:322
  49.7 2.6 %collective-permute-done.19.refs_2_ = bf16[128,256]{1,0:T(8,128)(2,1)S(1)} collective-permute-done((bf16[128,256]{1,0:T(8,128)(2,1)S(1)}, bf16[128,256]{1,0:T(8,128)(2,1)S(1)}, u32[]{:S(2)}, u32[]{:S(2)}) %collective-permute-start.19) | collective-permute-done | bytes 65568 | tf_op jit(solution)/shard_map/ppermute | solution.py:322
  52.3 2.1 %collective-permute-done.20.refs_3_ = bf16[128,256]{1,0:T(8,128)(2,1)S(1)} collective-permute-done((bf16[128,256]{1,0:T(8,128)(2,1)S(1)}, bf16[128,256]{1,0:T(8,128)(2,1)S(1)}, u32[]{:S(2)}, u32[]{:S(2)}) %collective-permute-start.20) | collective-permute-done | bytes 65568 | tf_op jit(solution)/shard_map/ppermute | solution.py:322
  55.0 0.6 %collective-permute-start.23 = (bf16[128,256]{1,0:T(8,128)(2,1)S(1)}, bf16[128,256]{1,0:T(8,128)(2,1)S(1)}, u32[]{:S(2)}, u32[]{:S(2)}) collective-permute-start(bf16[128,256]{1,0:T(8,128)(2,1)S(1)} %shard_map.100.refs_0_), channel_id=1, source_target_pairs={{0,16},{4,20},{8,24},{12,28},{16,0},{20,4},{24,8},{28,12},{1,17},{... | collective-permute-start | bytes 196616 | tf_op jit(solution)/shard_map/ppermute | solution.py:313
  55.6 2.4 %collective-permute-start.25 = (bf16[128,256]{1,0:T(8,128)(2,1)S(1)}, bf16[128,256]{1,0:T(8,128)(2,1)S(1)}, u32[]{:S(2)}, u32[]{:S(2)}) collective-permute-start(bf16[128,256]{1,0:T(8,128)(2,1)S(1)} %shard_map.100.refs_0_), channel_id=1, source_target_pairs={{0,24},{4,28},{8,16},{12,20},{16,8},{20,12},{24,0},{28,4},{1,25},{... | collective-permute-start | bytes 196616 | tf_op jit(solution)/shard_map/ppermute | solution.py:313
  58.0 0.8 %collective-permute-done.21.refs_1_ = bf16[128,256]{1,0:T(8,128)(2,1)S(1)} collective-permute-done((bf16[128,256]{1,0:T(8,128)(2,1)S(1)}, bf16[128,256]{1,0:T(8,128)(2,1)S(1)}, u32[]{:S(2)}, u32[]{:S(2)}) %collective-permute-start.21) | collective-permute-done | bytes 65568 | tf_op jit(solution)/shard_map/ppermute | solution.py:313
  59.3 1.5 %collective-permute-done.25.refs_3_ = bf16[128,256]{1,0:T(8,128)(2,1)S(1)} collective-permute-done((bf16[128,256]{1,0:T(8,128)(2,1)S(1)}, bf16[128,256]{1,0:T(8,128)(2,1)S(1)}, u32[]{:S(2)}, u32[]{:S(2)}) %collective-permute-start.25) | collective-permute-done | bytes 65568 | tf_op jit(solution)/shard_map/ppermute | solution.py:313
  60.8 0.8 %shard_map.95 = f32[192,256]{1,0:T(8,128)} custom-call(f32[192,256]{1,0:T(8,128)S(1)} %get-tuple-element.31.own_ref, f32[8,256]{1,0:T(8,128)S(1)} %get-tuple-element.32.own_deg_ref, bf16[200,256]{1,0:T(8,128)(2,1)S(1)} %collective-permute-done.11.refs_0_, bf16[200,256]{1,0:T(8,128)(2,1)S(1)} %collective-permute-done.12.refs_1_, ...), custom_call_target="tpu_custom_call" | custom-call | flops 1000 | bytes 708608 | tf_op jit(solution)/shard_map/pallas_call | solution.py:27
  61.6 0.9 %shard_map.101.refs_3_ = f32[1000,256]{1,0:T(8,128)} custom-call(bf16[128,256]{1,0:T(8,128)(2,1)S(1)} %shard_map.100.refs_0_, bf16[128,256]{1,0:T(8,128)(2,1)S(1)} %collective-permute-done.21.refs_1_, bf16[128,256]{1,0:T(8,128)(2,1)S(1)} %collective-permute-done.23.refs_2_, bf16[128,256]{1,0:T(8,128)(2,1)S(1)} %collective-permute-done.25.refs_3_, ...), custom_call_target="tpu_custom_call" | custom-call | flops 1000 | bytes 1351680 | tf_op jit(solution)/shard_map/pallas_call | solution.py:27
  62.5 0.8 %shard_map.102 = f32[1000,256]{1,0:T(8,128)} custom-call(bf16[128,256]{1,0:T(8,128)(2,1)S(1)} %collective-permute-done.22.refs_0_, bf16[128,256]{1,0:T(8,128)(2,1)S(1)} %collective-permute-done.24.refs_1_, bf16[128,256]{1,0:T(8,128)(2,1)S(1)} %collective-permute-done.26.refs_2_, f32[1000,256]{1,0:T(8,128)} %shard_map.101.refs_3_), custom_call_target="tpu_custom_call", output_to_operand_aliasing={{}: (3, {})} | custom-call | flops 1000 | bytes 2244608 | tf_op jit(solution)/shard_map/pallas_call | solution.py:27
  (55 shorter events, 5.9 us)
Async XLA Ops:
  0.7 0.9 %copy-start.3 = (bf16[128,768]{1,0:T(8,128)(2,1)S(1)}, bf16[128,768]{1,0:T(8,128)(2,1)}, u32[]{:S(2)}) copy-start(bf16[128,768]{1,0:T(8,128)(2,1)} %land_ref.1) | copy-start | bytes 589828
  1.6 17.3 %copy-start = (bf16[768,768]{1,0:T(8,128)(2,1)S(1)}, bf16[768,768]{1,0:T(8,128)(2,1)}, u32[]{:S(2)}) copy-start(bf16[768,768]{1,0:T(8,128)(2,1)} %doc_ref.13) | copy-start | bytes 3538948
  1.6 17.3 %copy-start.1 = (s32[6,32]{1,0:T(8,128)S(1)}, s32[6,32]{1,0:T(8,128)}, u32[]{:S(2)}) copy-start(s32[6,32]{1,0:T(8,128)} %mask_ref.13) | copy-start | bytes 2308
  1.8 9.7 %collective-permute-start.5 = (bf16[128,1024]{1,0:T(8,128)(2,1)S(1)}, bf16[128,1024]{1,0:T(8,128)(2,1)S(1)}, u32[]{:S(2)}, u32[]{:S(2)}) collective-permute-start(bf16[128,1024]{1,0:T(8,128)(2,1)S(1)} %get-tuple-element.21.refs_0_), channel_id=1, source_target_pairs={{0,16},{4,12},{8,24},{12,4},{16,0},{20,28},{24,8},{28,20},{1,17},{... | collective-permute-start | bytes 786440 | tf_op jit(solution)/shard_map/ppermute | solution.py:313
  4.8 9.2 %collective-permute-start = (bf16[128,1024]{1,0:T(8,128)(2,1)S(1)}, bf16[128,1024]{1,0:T(8,128)(2,1)S(1)}, u32[]{:S(2)}, u32[]{:S(2)}) collective-permute-start(bf16[128,1024]{1,0:T(8,128)(2,1)S(1)} %get-tuple-element.21.refs_0_), channel_id=1, source_target_pairs={{0,4},{4,0},{8,12},{12,8},{16,20},{20,16},{24,28},{28,24},{1,5},{5... | collective-permute-start | bytes 786440 | tf_op jit(solution)/shard_map/ppermute | solution.py:313
  4.8 6.6 %collective-permute-start.2 = (bf16[128,512]{1,0:T(8,128)(2,1)S(1)}, bf16[128,512]{1,0:T(8,128)(2,1)S(1)}, u32[]{:S(2)}, u32[]{:S(2)}) collective-permute-start(bf16[128,512]{1,0:T(8,128)(2,1)S(1)} %get-tuple-element.26), channel_id=1, source_target_pairs={{0,8},{4,20},{8,0},{12,28},{16,24},{20,4},{24,16},{28,12},{1,9},{5... | collective-permute-start | bytes 393224 | tf_op jit(solution)/shard_map/ppermute | solution.py:313
  6.3 7.6 %collective-permute-start.1 = (bf16[128,512]{1,0:T(8,128)(2,1)S(1)}, bf16[128,512]{1,0:T(8,128)(2,1)S(1)}, u32[]{:S(2)}, u32[]{:S(2)}) collective-permute-start(bf16[128,512]{1,0:T(8,128)(2,1)S(1)} %get-tuple-element.25), channel_id=1, source_target_pairs={{0,8},{4,20},{8,0},{12,28},{16,24},{20,4},{24,16},{28,12},{1,9},{5... | collective-permute-start | bytes 393224 | tf_op jit(solution)/shard_map/ppermute | solution.py:313
  11.5 9.2 %collective-permute-start.6 = (bf16[128,1024]{1,0:T(8,128)(2,1)S(1)}, bf16[128,1024]{1,0:T(8,128)(2,1)S(1)}, u32[]{:S(2)}, u32[]{:S(2)}) collective-permute-start(bf16[128,1024]{1,0:T(8,128)(2,1)S(1)} %collective-permute-done.5.refs_0_), channel_id=1, source_target_pairs={{0,4},{4,0},{8,12},{12,8},{16,20},{20,16},{24,28},{28,24},{1,5},{5... | collective-permute-start | bytes 786440 | tf_op jit(solution)/shard_map/ppermute | solution.py:313
  11.5 5.4 %collective-permute-start.8 = (bf16[128,512]{1,0:T(8,128)(2,1)S(1)}, bf16[128,512]{1,0:T(8,128)(2,1)S(1)}, u32[]{:S(2)}, u32[]{:S(2)}) collective-permute-start(bf16[128,512]{1,0:T(8,128)(2,1)S(1)} %collective-permute-done.2.refs_1_), channel_id=1, source_target_pairs={{0,16},{4,12},{8,24},{12,4},{16,0},{20,28},{24,8},{28,20},{1,17},{... | collective-permute-start | bytes 393224 | tf_op jit(solution)/shard_map/ppermute | solution.py:313
  14.0 5.0 %collective-permute-start.7 = (bf16[128,512]{1,0:T(8,128)(2,1)S(1)}, bf16[128,512]{1,0:T(8,128)(2,1)S(1)}, u32[]{:S(2)}, u32[]{:S(2)}) collective-permute-start(bf16[128,512]{1,0:T(8,128)(2,1)S(1)} %collective-permute-done.1.refs_0_), channel_id=1, source_target_pairs={{0,16},{4,12},{8,24},{12,4},{16,0},{20,28},{24,8},{28,20},{1,17},{... | collective-permute-start | bytes 393224 | tf_op jit(solution)/shard_map/ppermute | solution.py:313
  14.0 5.8 %collective-permute-start.3 = (bf16[128,512]{1,0:T(8,128)(2,1)S(1)}, bf16[128,512]{1,0:T(8,128)(2,1)S(1)}, u32[]{:S(2)}, u32[]{:S(2)}) collective-permute-start(bf16[128,512]{1,0:T(8,128)(2,1)S(1)} %collective-permute-done.1.refs_0_), channel_id=1, source_target_pairs={{0,4},{4,0},{8,12},{12,8},{16,20},{20,16},{24,28},{28,24},{1,5},{5... | collective-permute-start | bytes 393224 | tf_op jit(solution)/shard_map/ppermute | solution.py:313
  14.0 5.8 %collective-permute-start.4 = (bf16[128,512]{1,0:T(8,128)(2,1)S(1)}, bf16[128,512]{1,0:T(8,128)(2,1)S(1)}, u32[]{:S(2)}, u32[]{:S(2)}) collective-permute-start(bf16[128,512]{1,0:T(8,128)(2,1)S(1)} %collective-permute-done.2.refs_1_), channel_id=1, source_target_pairs={{0,4},{4,0},{8,12},{12,8},{16,20},{20,16},{24,28},{28,24},{1,5},{5... | collective-permute-start | bytes 393224 | tf_op jit(solution)/shard_map/ppermute | solution.py:313
  16.9 4.6 %collective-permute-start.10 = (bf16[128,512]{1,0:T(8,128)(2,1)S(1)}, bf16[128,512]{1,0:T(8,128)(2,1)S(1)}, u32[]{:S(2)}, u32[]{:S(2)}) collective-permute-start(bf16[128,512]{1,0:T(8,128)(2,1)S(1)} %collective-permute-done.8.refs_1_), channel_id=1, source_target_pairs={{0,4},{4,0},{8,12},{12,8},{16,20},{20,16},{24,28},{28,24},{1,5},{5... | collective-permute-start | bytes 393224 | tf_op jit(solution)/shard_map/ppermute | solution.py:313
  18.9 2.5 %collective-permute-start.9 = (bf16[128,512]{1,0:T(8,128)(2,1)S(1)}, bf16[128,512]{1,0:T(8,128)(2,1)S(1)}, u32[]{:S(2)}, u32[]{:S(2)}) collective-permute-start(bf16[128,512]{1,0:T(8,128)(2,1)S(1)} %collective-permute-done.7.refs_0_), channel_id=1, source_target_pairs={{0,4},{4,0},{8,12},{12,8},{16,20},{20,16},{24,28},{28,24},{1,5},{5... | collective-permute-start | bytes 393224 | tf_op jit(solution)/shard_map/ppermute | solution.py:313
  21.9 7.7 %collective-permute-start.13 = (bf16[200,256]{1,0:T(8,128)(2,1)S(1)}, bf16[200,256]{1,0:T(8,128)(2,1)S(1)}, u32[]{:S(2)}, u32[]{:S(2)}) collective-permute-start(bf16[200,256]{1,0:T(8,128)(2,1)S(1)} %shard_map.94), channel_id=1, source_target_pairs={{0,3},{1,2},{2,1},{3,0},{4,7},{5,6},{6,5},{7,4},{8,11},{9,10},{10,... | collective-permute-start | bytes 307208 | tf_op jit(solution)/shard_map/ppermute | solution.py:322
  25.9 8.9 %collective-permute-start.12 = (bf16[200,256]{1,0:T(8,128)(2,1)S(1)}, bf16[200,256]{1,0:T(8,128)(2,1)S(1)}, u32[]{:S(2)}, u32[]{:S(2)}) collective-permute-start(bf16[200,256]{1,0:T(8,128)(2,1)S(1)} %shard_map.93), channel_id=1, source_target_pairs={{0,2},{1,3},{2,0},{3,1},{4,6},{5,7},{6,4},{7,5},{8,10},{9,11},{10,... | collective-permute-start | bytes 307208 | tf_op jit(solution)/shard_map/ppermute | solution.py:322
  26.4 8.4 %copy-start.2 = (s32[192]{0:T(256)S(1)}, s32[192]{0:T(256)}, u32[]{:S(2)}) copy-start(s32[192]{0:T(256)} %param.13) | copy-start | bytes 2308
  26.4 8.4 %collective-permute-start.11 = (bf16[200,256]{1,0:T(8,128)(2,1)S(1)}, bf16[200,256]{1,0:T(8,128)(2,1)S(1)}, u32[]{:S(2)}, u32[]{:S(2)}) collective-permute-start(bf16[200,256]{1,0:T(8,128)(2,1)S(1)} %shard_map.92), channel_id=1, source_target_pairs={{0,1},{1,0},{2,3},{3,2},{4,5},{5,4},{6,7},{7,6},{8,9},{9,8},{10,11... | collective-permute-start | bytes 307208 | tf_op jit(solution)/shard_map/ppermute | solution.py:322
  35.3 1.6 %collective-permute-start.14 = (bf16[512,256]{1,0:T(8,128)(2,1)S(1)}, bf16[512,256]{1,0:T(8,128)(2,1)S(1)}, u32[]{:S(2)}, u32[]{:S(2)}) collective-permute-start(bf16[512,256]{1,0:T(8,128)(2,1)S(1)} %get-tuple-element.35), channel_id=1, source_target_pairs={{0,4},{4,0},{8,12},{12,8},{16,20},{20,16},{24,28},{28,24},{1,5},{5... | collective-permute-start | bytes 786440 | tf_op jit(solution)/shard_map/ppermute | solution.py:313
  37.0 4.3 %collective-permute-start.15 = (bf16[128,256]{1,0:T(8,128)(2,1)S(1)}, bf16[128,256]{1,0:T(8,128)(2,1)S(1)}, u32[]{:S(2)}, u32[]{:S(2)}) collective-permute-start(bf16[128,256]{1,0:T(8,128)(2,1)S(1)} %get-tuple-element.37), channel_id=1, source_target_pairs={{0,8},{4,12},{8,0},{12,4},{16,24},{20,28},{24,16},{28,20},{1,9},{5... | collective-permute-start | bytes 196616 | tf_op jit(solution)/shard_map/ppermute | solution.py:313
  38.6 4.3 %collective-permute-start.16 = (bf16[128,256]{1,0:T(8,128)(2,1)S(1)}, bf16[128,256]{1,0:T(8,128)(2,1)S(1)}, u32[]{:S(2)}, u32[]{:S(2)}) collective-permute-start(bf16[128,256]{1,0:T(8,128)(2,1)S(1)} %get-tuple-element.38), channel_id=1, source_target_pairs={{0,16},{4,20},{8,24},{12,28},{16,0},{20,4},{24,8},{28,12},{1,17},{... | collective-permute-start | bytes 196616 | tf_op jit(solution)/shard_map/ppermute | solution.py:313
  40.0 5.2 %collective-permute-start.17 = (bf16[128,256]{1,0:T(8,128)(2,1)S(1)}, bf16[128,256]{1,0:T(8,128)(2,1)S(1)}, u32[]{:S(2)}, u32[]{:S(2)}) collective-permute-start(bf16[128,256]{1,0:T(8,128)(2,1)S(1)} %get-tuple-element.39), channel_id=1, source_target_pairs={{0,24},{4,28},{8,16},{12,20},{16,8},{20,12},{24,0},{28,4},{1,25},{... | collective-permute-start | bytes 196616 | tf_op jit(solution)/shard_map/ppermute | solution.py:313
  45.2 4.5 %collective-permute-start.18 = (bf16[128,256]{1,0:T(8,128)(2,1)S(1)}, bf16[128,256]{1,0:T(8,128)(2,1)S(1)}, u32[]{:S(2)}, u32[]{:S(2)}) collective-permute-start(bf16[128,256]{1,0:T(8,128)(2,1)S(1)} %shard_map.99.refs_0_), channel_id=1, source_target_pairs={{0,1},{1,0},{2,3},{3,2},{4,5},{5,4},{6,7},{7,6},{8,9},{9,8},{10,11... | collective-permute-start | bytes 196616 | tf_op jit(solution)/shard_map/ppermute | solution.py:322
  45.7 6.6 %collective-permute-start.19 = (bf16[128,256]{1,0:T(8,128)(2,1)S(1)}, bf16[128,256]{1,0:T(8,128)(2,1)S(1)}, u32[]{:S(2)}, u32[]{:S(2)}) collective-permute-start(bf16[128,256]{1,0:T(8,128)(2,1)S(1)} %shard_map.99.refs_0_), channel_id=1, source_target_pairs={{0,2},{1,3},{2,0},{3,1},{4,6},{5,7},{6,4},{7,5},{8,10},{9,11},{10,... | collective-permute-start | bytes 196616 | tf_op jit(solution)/shard_map/ppermute | solution.py:322
  48.3 6.1 %collective-permute-start.20 = (bf16[128,256]{1,0:T(8,128)(2,1)S(1)}, bf16[128,256]{1,0:T(8,128)(2,1)S(1)}, u32[]{:S(2)}, u32[]{:S(2)}) collective-permute-start(bf16[128,256]{1,0:T(8,128)(2,1)S(1)} %shard_map.99.refs_0_), channel_id=1, source_target_pairs={{0,3},{1,2},{2,1},{3,0},{4,7},{5,6},{6,5},{7,4},{8,11},{9,10},{10,... | collective-permute-start | bytes 196616 | tf_op jit(solution)/shard_map/ppermute | solution.py:322
  54.4 4.3 %collective-permute-start.21 = (bf16[128,256]{1,0:T(8,128)(2,1)S(1)}, bf16[128,256]{1,0:T(8,128)(2,1)S(1)}, u32[]{:S(2)}, u32[]{:S(2)}) collective-permute-start(bf16[128,256]{1,0:T(8,128)(2,1)S(1)} %shard_map.100.refs_0_), channel_id=1, source_target_pairs={{0,8},{4,12},{8,0},{12,4},{16,24},{20,28},{24,16},{28,20},{1,9},{5... | collective-permute-start | bytes 196616 | tf_op jit(solution)/shard_map/ppermute | solution.py:313
  55.0 4.3 %collective-permute-start.23 = (bf16[128,256]{1,0:T(8,128)(2,1)S(1)}, bf16[128,256]{1,0:T(8,128)(2,1)S(1)}, u32[]{:S(2)}, u32[]{:S(2)}) collective-permute-start(bf16[128,256]{1,0:T(8,128)(2,1)S(1)} %shard_map.100.refs_0_), channel_id=1, source_target_pairs={{0,16},{4,20},{8,24},{12,28},{16,0},{20,4},{24,8},{28,12},{1,17},{... | collective-permute-start | bytes 196616 | tf_op jit(solution)/shard_map/ppermute | solution.py:313
  55.6 5.2 %collective-permute-start.25 = (bf16[128,256]{1,0:T(8,128)(2,1)S(1)}, bf16[128,256]{1,0:T(8,128)(2,1)S(1)}, u32[]{:S(2)}, u32[]{:S(2)}) collective-permute-start(bf16[128,256]{1,0:T(8,128)(2,1)S(1)} %shard_map.100.refs_0_), channel_id=1, source_target_pairs={{0,24},{4,28},{8,16},{12,20},{16,8},{20,12},{24,0},{28,4},{1,25},{... | collective-permute-start | bytes 196616 | tf_op jit(solution)/shard_map/ppermute | solution.py:313
  58.0 3.6 %collective-permute-start.27 = (bf16[128,256]{1,0:T(8,128)(2,1)S(1)}, bf16[128,256]{1,0:T(8,128)(2,1)S(1)}, u32[]{:S(2)}, u32[]{:S(2)}) collective-permute-start(bf16[128,256]{1,0:T(8,128)(2,1)S(1)} %shard_map.100.refs_0_), channel_id=1, source_target_pairs={{0,4},{4,0},{8,12},{12,8},{16,20},{20,16},{24,28},{28,24},{1,5},{5... | collective-permute-start | bytes 196616 | tf_op jit(solution)/shard_map/ppermute | solution.py:313
  58.7 3.7 %collective-permute-start.22 = (bf16[128,256]{1,0:T(8,128)(2,1)S(1)}, bf16[128,256]{1,0:T(8,128)(2,1)S(1)}, u32[]{:S(2)}, u32[]{:S(2)}) collective-permute-start(bf16[128,256]{1,0:T(8,128)(2,1)S(1)} %collective-permute-done.21.refs_1_), channel_id=1, source_target_pairs={{0,4},{4,0},{8,12},{12,8},{16,20},{20,16},{24,28},{28,24},{1,5},{5... | collective-permute-start | bytes 196616 | tf_op jit(solution)/shard_map/ppermute | solution.py:313
  59.2 3.2 %collective-permute-start.24 = (bf16[128,256]{1,0:T(8,128)(2,1)S(1)}, bf16[128,256]{1,0:T(8,128)(2,1)S(1)}, u32[]{:S(2)}, u32[]{:S(2)}) collective-permute-start(bf16[128,256]{1,0:T(8,128)(2,1)S(1)} %collective-permute-done.23.refs_2_), channel_id=1, source_target_pairs={{0,4},{4,0},{8,12},{12,8},{16,20},{20,16},{24,28},{28,24},{1,5},{5... | collective-permute-start | bytes 196616 | tf_op jit(solution)/shard_map/ppermute | solution.py:313
  60.8 1.7 %collective-permute-start.26 = (bf16[128,256]{1,0:T(8,128)(2,1)S(1)}, bf16[128,256]{1,0:T(8,128)(2,1)S(1)}, u32[]{:S(2)}, u32[]{:S(2)}) collective-permute-start(bf16[128,256]{1,0:T(8,128)(2,1)S(1)} %collective-permute-done.25.refs_3_), channel_id=1, source_target_pairs={{0,4},{4,0},{8,12},{12,8},{16,20},{20,16},{24,28},{28,24},{1,5},{5... | collective-permute-start | bytes 196616 | tf_op jit(solution)/shard_map/ppermute | solution.py:313
  (3 other events, 2.3 us)

commit v4 on v2

--- a/solution.py
+++ b/solution.py
@@ -223,43 +223,42 @@
     refs[-1][...] = embed(own_ref, own_deg_ref, refs[:-1])
 
 
-def gather_rows(core, label_ref, high, low, out_ref):
+def hot_kernel(*refs):
     me = lax.axis_index("blk")
     chips = lax.axis_size("blk") // 2
-    n = high.shape[0]
-    size = out_ref.shape[0] // chips
-    labels = jnp.broadcast_to(label_ref[...], (size, n))
-    spot = lax.broadcasted_iota(jnp.int32, (size, n), 0)
-    for chip in range(chips):
-        owner = jnp.bitwise_xor(me, 2 * chip + core)
-        hot = jnp.where(labels == spot + owner * size, 1.0, 0.0).astype(BF16)
-        part = jnp.dot(hot, high, preferred_element_type=F32)
-        part = part + jnp.dot(hot, low, preferred_element_type=F32)
-        out_ref[chip * size : (chip + 1) * size, :] = part.astype(out_ref.dtype)
-
-
-def norm_kernel(own_ref, own_deg_ref, label_ref, *refs):
-    send_ref, high_ref, low_ref = refs[-3:]
-    emb = embed(own_ref, own_deg_ref, refs[:-3])
+    for label_ref, out in zip(refs[:2], refs[2:]):
+        size, n = out.shape[0] // chips, out.shape[1]
+        labels = jnp.broadcast_to(label_ref[...], (size, n))
+        spot = lax.broadcasted_iota(jnp.int32, (size, n), 0)
+        for chip in range(chips):
+            owner = jnp.bitwise_xor(me, 2 * chip)
+            hot = jnp.where(labels == spot + owner * size, 1.0, 0.0)
+            out[chip * size : (chip + 1) * size, :] = hot.astype(BF16)
+
+
+def add_rows(hot, high, low):
+    return jnp.dot(hot, high, preferred_element_type=F32) + jnp.dot(hot, low, preferred_element_type=F32)
+
+
+def norm_kernel(own_ref, own_deg_ref, *refs):
+    high_ref, low_ref = refs[-2:]
+    emb = embed(own_ref, own_deg_ref, refs[:-2])
     unit = emb * lax.rsqrt(jnp.sum(emb * emb, 1, keepdims=True) + 1e-06)
     high = unit.astype(BF16)
     low = (unit - high.astype(F32)).astype(BF16)
     high_ref[...] = high
     low_ref[...] = low
-    gather_rows(1, label_ref, high, low, send_ref)
-
-
-def keep_kernel(label_ref, high_ref, low_ref, keep_ref):
-    gather_rows(0, label_ref, high_ref[...], low_ref[...], keep_ref)
-
-
-def split_kernel(keep_ref, get_ref, own_ref, *sends):
+
+
+def keep_kernel(hot_ref, high_ref, low_ref, keep_ref):
+    keep_ref[...] = add_rows(hot_ref[...], high_ref[...], low_ref[...])
+
+
+def split_kernel(keep_ref, hot_ref, get_ref, own_ref, *sends):
     size = own_ref.shape[0]
-    for chip in range(len(sends) + 1):
-        rows = slice(chip * size, (chip + 1) * size)
-        both = keep_ref[rows, :] + get_ref[rows, :].astype(F32)
-        out = sends[chip - 1] if chip else own_ref
-        out[...] = both.astype(out.dtype)
+    both = keep_ref[...] + jnp.dot(hot_ref[...], get_ref[...], preferred_element_type=F32)
+    for chip, out in enumerate((own_ref, *sends)):
+        out[...] = both[chip * size : (chip + 1) * size].astype(out.dtype)
 
 
 def tree(parts):
@@ -378,14 +377,17 @@
     gets = [col_swap(x, mask + 1) for mask, x in enumerate(sends)]
     size = -(-(-(-C // blks)) // 16) * 16
     names = labels.reshape(1, -1)
-    wide, half = struct((chips * size, k), F32), struct((chips * size, k), BF16)
+    wide = struct((chips * size, k), F32)
     unit = struct((rows, k), BF16)
-    send, high, low = call(norm_kernel, [half, unit, unit], [parts[0], parts[1], names, *gets])
-    get = core_swap(send)
-    keep = call(keep_kernel, [wide], [names, high, low])[0]
+    hot = struct((chips * size, rows), BF16)
+    far_names = core_swap(names)
+    hot_keep, hot_far = call(hot_kernel, [hot, hot], [names, far_names])
+    high, low = call(norm_kernel, [unit, unit], [parts[0], parts[1], *gets])
+    get = core_swap(high)
+    keep = call(keep_kernel, [wide], [hot_keep, high, low])[0]
     embedding = call(embed_kernel, [struct((rows, k), F32)], [parts[0], parts[1], *gets])[0]
     one, low = struct((size, k), F32), struct((size, k), BF16)
-    split = call(split_kernel, [one] + [low] * (chips - 1), [keep, get])
+    split = call(split_kernel, [one] + [low] * (chips - 1), [keep, hot_far, get])
     gets = [chip_swap(x, mask + 1) for mask, x in enumerate(split[1:])]
     mine = call(sum_kernel, [low], [split[0], *gets])[0]
     gets = [col_swap(mine, mask) for mask in range(1, cols)]

time: 63.5 us -> 63.6 us (level)
    ppermute x22 -> x23, starting transfers between devices: 15.4 us -> 15.9 us  [swap(): return lax.ppermute(x, 'blk', [(i, pick(i)) for i in range(blks)])]
    ppermute x22 -> x23, waiting for transfers between devices: 17.6 us -> 17.2 us  [swap(): return lax.ppermute(x, 'blk', [(i, pick(i)) for i in range(blks)])]
    pallas_call x17 -> x18, Pallas kernels: 7.65 us -> 7.62 us  [call(): pl.pallas_call(kernel, out_shape=outs, in_specs=specs or [VMEM] * len(arg...]
  transfers between devices with their start and end apart: 28 -> 29, of which waited for: 14 -> 14; matrix products, arithmetic and copies ran while one was open for 0% -> 0% of each run, Pallas kernels for 9% -> 9%
where the time goes in v4:
time: 63.6 us; the launch traced here: 63.4 us
  waiting for transfers between devices  29.1 us (46%)
  starting transfers between devices  24.9 us (39%)
  Pallas kernels  7.62 us (12%)
  local copies, waits for them, and re-layouts  0.94 us (1%)
  between operations  0.89 us (1%)
    ppermute x23, waiting for transfers between devices, swap(): return lax.ppermute(x, 'blk', [(i, pick(i)) for i in range(blks)])  17.2 us
    ppermute x23, starting transfers between devices, swap(): return lax.ppermute(x, 'blk', [(i, pick(i)) for i in range(blks)])  15.9 us
    ppermute x6, waiting for transfers between devices, col_swap(): return lax.ppermute(x, 'col', [(i, i ^ mask) for i in range(cols)])  11.9 us
    ppermute x6, starting transfers between devices, col_swap(): return lax.ppermute(x, 'col', [(i, i ^ mask) for i in range(cols)])  9.02 us
    pallas_call x18, Pallas kernels, call(): pl.pallas_call(kernel, out_shape=outs, in_specs=specs or [VMEM] * len(arg...  7.62 us
  transfers between devices with their start and end apart: 29, of which 14 were waited for; matrix products, arithmetic and copies ran while one was open for 0% of the time, Pallas kernels for 9%

profile of v4, /device:TPU:0, one launch (start us, length us, event | category | flops | bytes accessed | tf_op | source)
XLA Modules:
  0.0 63.4 jit_solution(10522923045619683215)
XLA Ops:
  0.7 0.6 copy-done.6
  1.8 3.1 %collective-permute-start.5 = (bf16[128,1024]{1,0:T(8,128)(2,1)S(1)}, bf16[128,1024]{1,0:T(8,128)(2,1)S(1)}, u32[]{:S(2)}, u32[]{:S(2)}) collective-permute-start(bf16[128,1024]{1,0:T(8,128)(2,1)S(1)} %get-tuple-element.22.refs_0_), channel_id=1, source_target_pairs={{0,16},{4,12},{8,24},{12,4},{16,0},{20,28},{24,8},{28,20},{1,17},{... | collective-permute-start | bytes 786440 | tf_op jit(solution)/shard_map/ppermute | solution.py:311
  4.8 1.5 %collective-permute-start.2 = (bf16[128,512]{1,0:T(8,128)(2,1)S(1)}, bf16[128,512]{1,0:T(8,128)(2,1)S(1)}, u32[]{:S(2)}, u32[]{:S(2)}) collective-permute-start(bf16[128,512]{1,0:T(8,128)(2,1)S(1)} %get-tuple-element.27), channel_id=1, source_target_pairs={{0,8},{4,20},{8,0},{12,28},{16,24},{20,4},{24,16},{28,12},{1,9},{5... | collective-permute-start | bytes 393224 | tf_op jit(solution)/shard_map/ppermute | solution.py:311
  6.9 4.6 %collective-permute-done.5.refs_0_ = bf16[128,1024]{1,0:T(8,128)(2,1)S(1)} collective-permute-done((bf16[128,1024]{1,0:T(8,128)(2,1)S(1)}, bf16[128,1024]{1,0:T(8,128)(2,1)S(1)}, u32[]{:S(2)}, u32[]{:S(2)}) %collective-permute-start.5) | collective-permute-done | bytes 262176 | tf_op jit(solution)/shard_map/ppermute | solution.py:311
  11.5 2.5 %collective-permute-start.8 = (bf16[128,512]{1,0:T(8,128)(2,1)S(1)}, bf16[128,512]{1,0:T(8,128)(2,1)S(1)}, u32[]{:S(2)}, u32[]{:S(2)}) collective-permute-start(bf16[128,512]{1,0:T(8,128)(2,1)S(1)} %collective-permute-done.2.refs_1_), channel_id=1, source_target_pairs={{0,16},{4,12},{8,24},{12,4},{16,0},{20,28},{24,8},{28,20},{1,17},{... | collective-permute-start | bytes 393224 | tf_op jit(solution)/shard_map/ppermute | solution.py:311
  14.6 2.3 %collective-permute-done.8.refs_1_ = bf16[128,512]{1,0:T(8,128)(2,1)S(1)} collective-permute-done((bf16[128,512]{1,0:T(8,128)(2,1)S(1)}, bf16[128,512]{1,0:T(8,128)(2,1)S(1)}, u32[]{:S(2)}, u32[]{:S(2)}) %collective-permute-start.8) | collective-permute-done | bytes 131104 | tf_op jit(solution)/shard_map/ppermute | solution.py:311
  16.9 2.0 %collective-permute-done.7.refs_0_ = bf16[128,512]{1,0:T(8,128)(2,1)S(1)} collective-permute-done((bf16[128,512]{1,0:T(8,128)(2,1)S(1)}, bf16[128,512]{1,0:T(8,128)(2,1)S(1)}, u32[]{:S(2)}, u32[]{:S(2)}) %collective-permute-start.7) | collective-permute-done | bytes 131104 | tf_op jit(solution)/shard_map/ppermute | solution.py:311
  18.9 0.9 %shard_map.88 = (f32[768,256]{1,0:T(8,128)S(1)}, f32[768,128]{1,0:T(8,128)S(1)}, f32[768,128]{1,0:T(8,128)S(1)}) custom-call(bf16[768,768]{1,0:T(8,128)(2,1)S(1)} %copy-done, s32[6,32]{1,0:T(8,128)S(1)} %copy-done.1, bf16[128,1024]{1,0:T(8,128)(2,1)S(1)} %get-tuple-element.22.refs_0_, bf16[128,1024]{1,0:T(8,128)(2,1)S(1)} %collective-permute-done.refs_1_), custom_call_target="tpu_custom_call" | custom-call | flops 402653184 | bytes 3277568 | tf_op jit(solution)/shard_map/pallas_call | solution.py:27
  19.8 0.8 %shard_map.89 = (f32[768,256]{1,0:T(8,128)S(1)}, f32[768,128]{1,0:T(8,128)S(1)}) custom-call(bf16[768,768]{1,0:T(8,128)(2,1)S(1)} %copy-done, f32[768,128]{1,0:T(8,128)S(1)} %get-tuple-element.23.square_ref, s32[6,32]{1,0:T(8,128)S(1)} %copy-done.1, f32[768,256]{1,0:T(8,128)S(1)} %get-tuple-element.24.total_in, ...), custom_call_target="tpu_custom_call", output_to_operand_aliasing={{0}: (3, {}), {1}: (4, {})} | custom-call | flops 402653184 | bytes 4457216 | tf_op jit(solution)/shard_map/pallas_call | solution.py:27
  20.6 0.8 %shard_map.90 = (f32[768,256]{1,0:T(8,128)S(1)}, f32[768,128]{1,0:T(8,128)S(1)}) custom-call(bf16[768,768]{1,0:T(8,128)(2,1)S(1)} %copy-done, f32[768,128]{1,0:T(8,128)S(1)} %get-tuple-element.23.square_ref, s32[6,32]{1,0:T(8,128)S(1)} %copy-done.1, f32[768,256]{1,0:T(8,128)S(1)} %get-tuple-element.28.total_in, ...), custom_call_target="tpu_custom_call", output_to_operand_aliasing={{0}: (3, {}), {1}: (4, {})} | custom-call | flops 402653184 | bytes 4457216 | tf_op jit(solution)/shard_map/pallas_call | solution.py:27
  21.9 3.7 %collective-permute-start.13 = (bf16[200,256]{1,0:T(8,128)(2,1)S(1)}, bf16[200,256]{1,0:T(8,128)(2,1)S(1)}, u32[]{:S(2)}, u32[]{:S(2)}) collective-permute-start(bf16[200,256]{1,0:T(8,128)(2,1)S(1)} %shard_map.94), channel_id=1, source_target_pairs={{0,3},{1,2},{2,1},{3,0},{4,7},{5,6},{6,5},{7,4},{8,11},{9,10},{10,... | collective-permute-start | bytes 307208 | tf_op jit(solution)/shard_map/ppermute | solution.py:320
  26.4 0.8 %collective-permute-start.11 = (bf16[200,256]{1,0:T(8,128)(2,1)S(1)}, bf16[200,256]{1,0:T(8,128)(2,1)S(1)}, u32[]{:S(2)}, u32[]{:S(2)}) collective-permute-start(bf16[200,256]{1,0:T(8,128)(2,1)S(1)} %shard_map.92), channel_id=1, source_target_pairs={{0,1},{1,0},{2,3},{3,2},{4,5},{5,4},{6,7},{7,6},{8,9},{9,8},{10,11... | collective-permute-start | bytes 307208 | tf_op jit(solution)/shard_map/ppermute | solution.py:320
  27.7 1.9 %collective-permute-done.13.refs_2_ = bf16[200,256]{1,0:T(8,128)(2,1)S(1)} collective-permute-done((bf16[200,256]{1,0:T(8,128)(2,1)S(1)}, bf16[200,256]{1,0:T(8,128)(2,1)S(1)}, u32[]{:S(2)}, u32[]{:S(2)}) %collective-permute-start.13) | collective-permute-done | bytes 102432 | tf_op jit(solution)/shard_map/ppermute | solution.py:320
  29.6 5.2 %collective-permute-done.12.refs_1_ = bf16[200,256]{1,0:T(8,128)(2,1)S(1)} collective-permute-done((bf16[200,256]{1,0:T(8,128)(2,1)S(1)}, bf16[200,256]{1,0:T(8,128)(2,1)S(1)}, u32[]{:S(2)}, u32[]{:S(2)}) %collective-permute-start.12) | collective-permute-done | bytes 102432 | tf_op jit(solution)/shard_map/ppermute | solution.py:320
  35.6 0.8 %collective-permute-done.14.refs_1_ = s32[1,192]{1,0:T(1,128)S(1)} collective-permute-done((s32[1,192]{1,0:T(1,128)S(1)}, s32[1,192]{1,0:T(1,128)S(1)}, u32[]{:S(2)}, u32[]{:S(2)}) %collective-permute-start.14) | collective-permute-done | bytes 800 | tf_op jit(solution)/shard_map/ppermute | solution.py:311
  37.1 1.6 %collective-permute-start.16 = (bf16[128,256]{1,0:T(8,128)(2,1)S(1)}, bf16[128,256]{1,0:T(8,128)(2,1)S(1)}, u32[]{:S(2)}, u32[]{:S(2)}) collective-permute-start(bf16[128,256]{1,0:T(8,128)(2,1)S(1)} %get-tuple-element.39), channel_id=1, source_target_pairs={{0,8},{4,12},{8,0},{12,4},{16,24},{20,28},{24,16},{28,20},{1,9},{5... | collective-permute-start | bytes 196616 | tf_op jit(solution)/shard_map/ppermute | solution.py:311
  38.7 1.4 %collective-permute-start.17 = (bf16[128,256]{1,0:T(8,128)(2,1)S(1)}, bf16[128,256]{1,0:T(8,128)(2,1)S(1)}, u32[]{:S(2)}, u32[]{:S(2)}) collective-permute-start(bf16[128,256]{1,0:T(8,128)(2,1)S(1)} %get-tuple-element.40), channel_id=1, source_target_pairs={{0,16},{4,20},{8,24},{12,28},{16,0},{20,4},{24,8},{28,12},{1,17},{... | collective-permute-start | bytes 196616 | tf_op jit(solution)/shard_map/ppermute | solution.py:311
  40.6 0.9 %collective-permute-done.16.refs_1_ = bf16[128,256]{1,0:T(8,128)(2,1)S(1)} collective-permute-done((bf16[128,256]{1,0:T(8,128)(2,1)S(1)}, bf16[128,256]{1,0:T(8,128)(2,1)S(1)}, u32[]{:S(2)}, u32[]{:S(2)}) %collective-permute-start.16) | collective-permute-done | bytes 65568 | tf_op jit(solution)/shard_map/ppermute | solution.py:311
  41.5 1.4 %collective-permute-done.17.refs_2_ = bf16[128,256]{1,0:T(8,128)(2,1)S(1)} collective-permute-done((bf16[128,256]{1,0:T(8,128)(2,1)S(1)}, bf16[128,256]{1,0:T(8,128)(2,1)S(1)}, u32[]{:S(2)}, u32[]{:S(2)}) %collective-permute-start.17) | collective-permute-done | bytes 65568 | tf_op jit(solution)/shard_map/ppermute | solution.py:311
  42.9 2.3 %collective-permute-done.18.refs_3_ = bf16[128,256]{1,0:T(8,128)(2,1)S(1)} collective-permute-done((bf16[128,256]{1,0:T(8,128)(2,1)S(1)}, bf16[128,256]{1,0:T(8,128)(2,1)S(1)}, u32[]{:S(2)}, u32[]{:S(2)}) %collective-permute-start.18) | collective-permute-done | bytes 65568 | tf_op jit(solution)/shard_map/ppermute | solution.py:311
  45.8 2.6 %collective-permute-start.20 = (bf16[128,256]{1,0:T(8,128)(2,1)S(1)}, bf16[128,256]{1,0:T(8,128)(2,1)S(1)}, u32[]{:S(2)}, u32[]{:S(2)}) collective-permute-start(bf16[128,256]{1,0:T(8,128)(2,1)S(1)} %shard_map.100.refs_0_), channel_id=1, source_target_pairs={{0,2},{1,3},{2,0},{3,1},{4,6},{5,7},{6,4},{7,5},{8,10},{9,11},{10,... | collective-permute-start | bytes 196616 | tf_op jit(solution)/shard_map/ppermute | solution.py:320
  48.4 1.3 %collective-permute-start.21 = (bf16[128,256]{1,0:T(8,128)(2,1)S(1)}, bf16[128,256]{1,0:T(8,128)(2,1)S(1)}, u32[]{:S(2)}, u32[]{:S(2)}) collective-permute-start(bf16[128,256]{1,0:T(8,128)(2,1)S(1)} %shard_map.100.refs_0_), channel_id=1, source_target_pairs={{0,3},{1,2},{2,1},{3,0},{4,7},{5,6},{6,5},{7,4},{8,11},{9,10},{10,... | collective-permute-start | bytes 196616 | tf_op jit(solution)/shard_map/ppermute | solution.py:320
  49.7 1.2 %collective-permute-done.20.refs_2_ = bf16[128,256]{1,0:T(8,128)(2,1)S(1)} collective-permute-done((bf16[128,256]{1,0:T(8,128)(2,1)S(1)}, bf16[128,256]{1,0:T(8,128)(2,1)S(1)}, u32[]{:S(2)}, u32[]{:S(2)}) %collective-permute-start.20) | collective-permute-done | bytes 65568 | tf_op jit(solution)/shard_map/ppermute | solution.py:320
  51.0 3.5 %collective-permute-done.21.refs_3_ = bf16[128,256]{1,0:T(8,128)(2,1)S(1)} collective-permute-done((bf16[128,256]{1,0:T(8,128)(2,1)S(1)}, bf16[128,256]{1,0:T(8,128)(2,1)S(1)}, u32[]{:S(2)}, u32[]{:S(2)}) %collective-permute-start.21) | collective-permute-done | bytes 65568 | tf_op jit(solution)/shard_map/ppermute | solution.py:320
  54.5 0.6 collective-permute-start.23
  55.1 0.6 collective-permute-start.25
  55.7 2.4 %collective-permute-start.27 = (bf16[128,256]{1,0:T(8,128)(2,1)S(1)}, bf16[128,256]{1,0:T(8,128)(2,1)S(1)}, u32[]{:S(2)}, u32[]{:S(2)}) collective-permute-start(bf16[128,256]{1,0:T(8,128)(2,1)S(1)} %shard_map.101.refs_0_), channel_id=1, source_target_pairs={{0,24},{4,28},{8,16},{12,20},{16,8},{20,12},{24,0},{28,4},{1,25},{... | collective-permute-start | bytes 196616 | tf_op jit(solution)/shard_map/ppermute | solution.py:311
  58.1 0.8 %collective-permute-done.23.refs_1_ = bf16[128,256]{1,0:T(8,128)(2,1)S(1)} collective-permute-done((bf16[128,256]{1,0:T(8,128)(2,1)S(1)}, bf16[128,256]{1,0:T(8,128)(2,1)S(1)}, u32[]{:S(2)}, u32[]{:S(2)}) %collective-permute-start.23) | collective-permute-done | bytes 65568 | tf_op jit(solution)/shard_map/ppermute | solution.py:311
  59.3 1.5 %collective-permute-done.27.refs_3_ = bf16[128,256]{1,0:T(8,128)(2,1)S(1)} collective-permute-done((bf16[128,256]{1,0:T(8,128)(2,1)S(1)}, bf16[128,256]{1,0:T(8,128)(2,1)S(1)}, u32[]{:S(2)}, u32[]{:S(2)}) %collective-permute-start.27) | collective-permute-done | bytes 65568 | tf_op jit(solution)/shard_map/ppermute | solution.py:311
  60.9 0.8 %shard_map.95 = f32[192,256]{1,0:T(8,128)} custom-call(f32[192,256]{1,0:T(8,128)S(1)} %get-tuple-element.32.own_ref, f32[8,256]{1,0:T(8,128)S(1)} %get-tuple-element.33.own_deg_ref, bf16[200,256]{1,0:T(8,128)(2,1)S(1)} %collective-permute-done.11.refs_0_, bf16[200,256]{1,0:T(8,128)(2,1)S(1)} %collective-permute-done.12.refs_1_, ...), custom_call_target="tpu_custom_call" | custom-call | flops 1000 | bytes 708608 | tf_op jit(solution)/shard_map/pallas_call | solution.py:27
  61.7 0.9 %shard_map.102.refs_4_ = f32[1000,256]{1,0:T(8,128)} custom-call(bf16[128,256]{1,0:T(8,128)(2,1)S(1)} %shard_map.101.refs_0_, bf16[128,256]{1,0:T(8,128)(2,1)S(1)} %collective-permute-done.23.refs_1_, bf16[128,256]{1,0:T(8,128)(2,1)S(1)} %collective-permute-done.25.refs_2_, bf16[128,256]{1,0:T(8,128)(2,1)S(1)} %collective-permute-done.27.refs_3_), custom_call_target="tpu_custom_call" | custom-call | flops 1000 | bytes 1286144 | tf_op jit(solution)/shard_map/pallas_call | solution.py:27
  62.6 0.8 %shard_map.103 = f32[1000,256]{1,0:T(8,128)} custom-call(bf16[128,256]{1,0:T(8,128)(2,1)S(1)} %collective-permute-done.22.refs_0_, bf16[128,256]{1,0:T(8,128)(2,1)S(1)} %collective-permute-done.24.refs_1_, bf16[128,256]{1,0:T(8,128)(2,1)S(1)} %collective-permute-done.26.refs_2_, ...), custom_call_target="tpu_custom_call", output_to_operand_aliasing={{}: (4, {})} | custom-call | flops 1000 | bytes 2310144 | tf_op jit(solution)/shard_map/pallas_call | solution.py:27
  (58 shorter events, 6.4 us)
Async XLA Ops:
  1.6 17.3 %copy-start = (bf16[768,768]{1,0:T(8,128)(2,1)S(1)}, bf16[768,768]{1,0:T(8,128)(2,1)}, u32[]{:S(2)}) copy-start(bf16[768,768]{1,0:T(8,128)(2,1)} %doc_ref.13) | copy-start | bytes 3538948
  1.6 17.3 %copy-start.1 = (s32[6,32]{1,0:T(8,128)S(1)}, s32[6,32]{1,0:T(8,128)}, u32[]{:S(2)}) copy-start(s32[6,32]{1,0:T(8,128)} %mask_ref.13) | copy-start | bytes 2308
  1.8 9.7 %collective-permute-start.5 = (bf16[128,1024]{1,0:T(8,128)(2,1)S(1)}, bf16[128,1024]{1,0:T(8,128)(2,1)S(1)}, u32[]{:S(2)}, u32[]{:S(2)}) collective-permute-start(bf16[128,1024]{1,0:T(8,128)(2,1)S(1)} %get-tuple-element.22.refs_0_), channel_id=1, source_target_pairs={{0,16},{4,12},{8,24},{12,4},{16,0},{20,28},{24,8},{28,20},{1,17},{... | collective-permute-start | bytes 786440 | tf_op jit(solution)/shard_map/ppermute | solution.py:311
  4.8 9.2 %collective-permute-start = (bf16[128,1024]{1,0:T(8,128)(2,1)S(1)}, bf16[128,1024]{1,0:T(8,128)(2,1)S(1)}, u32[]{:S(2)}, u32[]{:S(2)}) collective-permute-start(bf16[128,1024]{1,0:T(8,128)(2,1)S(1)} %get-tuple-element.22.refs_0_), channel_id=1, source_target_pairs={{0,4},{4,0},{8,12},{12,8},{16,20},{20,16},{24,28},{28,24},{1,5},{5... | collective-permute-start | bytes 786440 | tf_op jit(solution)/shard_map/ppermute | solution.py:311
  4.8 6.6 %collective-permute-start.2 = (bf16[128,512]{1,0:T(8,128)(2,1)S(1)}, bf16[128,512]{1,0:T(8,128)(2,1)S(1)}, u32[]{:S(2)}, u32[]{:S(2)}) collective-permute-start(bf16[128,512]{1,0:T(8,128)(2,1)S(1)} %get-tuple-element.27), channel_id=1, source_target_pairs={{0,8},{4,20},{8,0},{12,28},{16,24},{20,4},{24,16},{28,12},{1,9},{5... | collective-permute-start | bytes 393224 | tf_op jit(solution)/shard_map/ppermute | solution.py:311
  6.3 7.6 %collective-permute-start.1 = (bf16[128,512]{1,0:T(8,128)(2,1)S(1)}, bf16[128,512]{1,0:T(8,128)(2,1)S(1)}, u32[]{:S(2)}, u32[]{:S(2)}) collective-permute-start(bf16[128,512]{1,0:T(8,128)(2,1)S(1)} %get-tuple-element.26), channel_id=1, source_target_pairs={{0,8},{4,20},{8,0},{12,28},{16,24},{20,4},{24,16},{28,12},{1,9},{5... | collective-permute-start | bytes 393224 | tf_op jit(solution)/shard_map/ppermute | solution.py:311
  11.5 9.2 %collective-permute-start.6 = (bf16[128,1024]{1,0:T(8,128)(2,1)S(1)}, bf16[128,1024]{1,0:T(8,128)(2,1)S(1)}, u32[]{:S(2)}, u32[]{:S(2)}) collective-permute-start(bf16[128,1024]{1,0:T(8,128)(2,1)S(1)} %collective-permute-done.5.refs_0_), channel_id=1, source_target_pairs={{0,4},{4,0},{8,12},{12,8},{16,20},{20,16},{24,28},{28,24},{1,5},{5... | collective-permute-start | bytes 786440 | tf_op jit(solution)/shard_map/ppermute | solution.py:311
  11.5 5.4 %collective-permute-start.8 = (bf16[128,512]{1,0:T(8,128)(2,1)S(1)}, bf16[128,512]{1,0:T(8,128)(2,1)S(1)}, u32[]{:S(2)}, u32[]{:S(2)}) collective-permute-start(bf16[128,512]{1,0:T(8,128)(2,1)S(1)} %collective-permute-done.2.refs_1_), channel_id=1, source_target_pairs={{0,16},{4,12},{8,24},{12,4},{16,0},{20,28},{24,8},{28,20},{1,17},{... | collective-permute-start | bytes 393224 | tf_op jit(solution)/shard_map/ppermute | solution.py:311
  14.0 5.0 %collective-permute-start.7 = (bf16[128,512]{1,0:T(8,128)(2,1)S(1)}, bf16[128,512]{1,0:T(8,128)(2,1)S(1)}, u32[]{:S(2)}, u32[]{:S(2)}) collective-permute-start(bf16[128,512]{1,0:T(8,128)(2,1)S(1)} %collective-permute-done.1.refs_0_), channel_id=1, source_target_pairs={{0,16},{4,12},{8,24},{12,4},{16,0},{20,28},{24,8},{28,20},{1,17},{... | collective-permute-start | bytes 393224 | tf_op jit(solution)/shard_map/ppermute | solution.py:311
  14.0 5.8 %collective-permute-start.3 = (bf16[128,512]{1,0:T(8,128)(2,1)S(1)}, bf16[128,512]{1,0:T(8,128)(2,1)S(1)}, u32[]{:S(2)}, u32[]{:S(2)}) collective-permute-start(bf16[128,512]{1,0:T(8,128)(2,1)S(1)} %collective-permute-done.1.refs_0_), channel_id=1, source_target_pairs={{0,4},{4,0},{8,12},{12,8},{16,20},{20,16},{24,28},{28,24},{1,5},{5... | collective-permute-start | bytes 393224 | tf_op jit(solution)/shard_map/ppermute | solution.py:311
  14.0 5.8 %collective-permute-start.4 = (bf16[128,512]{1,0:T(8,128)(2,1)S(1)}, bf16[128,512]{1,0:T(8,128)(2,1)S(1)}, u32[]{:S(2)}, u32[]{:S(2)}) collective-permute-start(bf16[128,512]{1,0:T(8,128)(2,1)S(1)} %collective-permute-done.2.refs_1_), channel_id=1, source_target_pairs={{0,4},{4,0},{8,12},{12,8},{16,20},{20,16},{24,28},{28,24},{1,5},{5... | collective-permute-start | bytes 393224 | tf_op jit(solution)/shard_map/ppermute | solution.py:311
  16.9 4.6 %collective-permute-start.10 = (bf16[128,512]{1,0:T(8,128)(2,1)S(1)}, bf16[128,512]{1,0:T(8,128)(2,1)S(1)}, u32[]{:S(2)}, u32[]{:S(2)}) collective-permute-start(bf16[128,512]{1,0:T(8,128)(2,1)S(1)} %collective-permute-done.8.refs_1_), channel_id=1, source_target_pairs={{0,4},{4,0},{8,12},{12,8},{16,20},{20,16},{24,28},{28,24},{1,5},{5... | collective-permute-start | bytes 393224 | tf_op jit(solution)/shard_map/ppermute | solution.py:311
  18.9 2.5 %collective-permute-start.9 = (bf16[128,512]{1,0:T(8,128)(2,1)S(1)}, bf16[128,512]{1,0:T(8,128)(2,1)S(1)}, u32[]{:S(2)}, u32[]{:S(2)}) collective-permute-start(bf16[128,512]{1,0:T(8,128)(2,1)S(1)} %collective-permute-done.7.refs_0_), channel_id=1, source_target_pairs={{0,4},{4,0},{8,12},{12,8},{16,20},{20,16},{24,28},{28,24},{1,5},{5... | collective-permute-start | bytes 393224 | tf_op jit(solution)/shard_map/ppermute | solution.py:311
  21.9 7.7 %collective-permute-start.13 = (bf16[200,256]{1,0:T(8,128)(2,1)S(1)}, bf16[200,256]{1,0:T(8,128)(2,1)S(1)}, u32[]{:S(2)}, u32[]{:S(2)}) collective-permute-start(bf16[200,256]{1,0:T(8,128)(2,1)S(1)} %shard_map.94), channel_id=1, source_target_pairs={{0,3},{1,2},{2,1},{3,0},{4,7},{5,6},{6,5},{7,4},{8,11},{9,10},{10,... | collective-permute-start | bytes 307208 | tf_op jit(solution)/shard_map/ppermute | solution.py:320
  25.9 8.9 %collective-permute-start.12 = (bf16[200,256]{1,0:T(8,128)(2,1)S(1)}, bf16[200,256]{1,0:T(8,128)(2,1)S(1)}, u32[]{:S(2)}, u32[]{:S(2)}) collective-permute-start(bf16[200,256]{1,0:T(8,128)(2,1)S(1)} %shard_map.93), channel_id=1, source_target_pairs={{0,2},{1,3},{2,0},{3,1},{4,6},{5,7},{6,4},{7,5},{8,10},{9,11},{10,... | collective-permute-start | bytes 307208 | tf_op jit(solution)/shard_map/ppermute | solution.py:320
  26.4 8.7 %copy-start.2 = (s32[192]{0:T(256)S(1)}, s32[192]{0:T(256)}, u32[]{:S(2)}) copy-start(s32[192]{0:T(256)} %param.13) | copy-start | bytes 2308
  26.4 8.4 %collective-permute-start.11 = (bf16[200,256]{1,0:T(8,128)(2,1)S(1)}, bf16[200,256]{1,0:T(8,128)(2,1)S(1)}, u32[]{:S(2)}, u32[]{:S(2)}) collective-permute-start(bf16[200,256]{1,0:T(8,128)(2,1)S(1)} %shard_map.92), channel_id=1, source_target_pairs={{0,1},{1,0},{2,3},{3,2},{4,5},{5,4},{6,7},{7,6},{8,9},{9,8},{10,11... | collective-permute-start | bytes 307208 | tf_op jit(solution)/shard_map/ppermute | solution.py:320
  35.1 1.8 %collective-permute-start.15 = (bf16[192,256]{1,0:T(8,128)(2,1)S(1)}, bf16[192,256]{1,0:T(8,128)(2,1)S(1)}, u32[]{:S(2)}, u32[]{:S(2)}) collective-permute-start(bf16[192,256]{1,0:T(8,128)(2,1)S(1)} %get-tuple-element.35.high_ref), channel_id=1, source_target_pairs={{0,4},{4,0},{8,12},{12,8},{16,20},{20,16},{24,28},{28,24},{1,5},{5... | collective-permute-start | bytes 294920 | tf_op jit(solution)/shard_map/ppermute | solution.py:311
  35.1 1.3 %collective-permute-start.14 = (s32[1,192]{1,0:T(1,128)S(1)}, s32[1,192]{1,0:T(1,128)S(1)}, u32[]{:S(2)}, u32[]{:S(2)}) collective-permute-start(s32[1,192]{1,0:T(1,128)S(1)} %bitcast.3), channel_id=1, source_target_pairs={{0,4},{4,0},{8,12},{12,8},{16,20},{20,16},{24,28},{28,24},{1,5},{5... | collective-permute-start | bytes 2312 | tf_op jit(solution)/shard_map/ppermute | solution.py:311
  37.1 4.4 %collective-permute-start.16 = (bf16[128,256]{1,0:T(8,128)(2,1)S(1)}, bf16[128,256]{1,0:T(8,128)(2,1)S(1)}, u32[]{:S(2)}, u32[]{:S(2)}) collective-permute-start(bf16[128,256]{1,0:T(8,128)(2,1)S(1)} %get-tuple-element.39), channel_id=1, source_target_pairs={{0,8},{4,12},{8,0},{12,4},{16,24},{20,28},{24,16},{28,20},{1,9},{5... | collective-permute-start | bytes 196616 | tf_op jit(solution)/shard_map/ppermute | solution.py:311
  38.7 4.3 %collective-permute-start.17 = (bf16[128,256]{1,0:T(8,128)(2,1)S(1)}, bf16[128,256]{1,0:T(8,128)(2,1)S(1)}, u32[]{:S(2)}, u32[]{:S(2)}) collective-permute-start(bf16[128,256]{1,0:T(8,128)(2,1)S(1)} %get-tuple-element.40), channel_id=1, source_target_pairs={{0,16},{4,20},{8,24},{12,28},{16,0},{20,4},{24,8},{28,12},{1,17},{... | collective-permute-start | bytes 196616 | tf_op jit(solution)/shard_map/ppermute | solution.py:311
  40.1 5.2 %collective-permute-start.18 = (bf16[128,256]{1,0:T(8,128)(2,1)S(1)}, bf16[128,256]{1,0:T(8,128)(2,1)S(1)}, u32[]{:S(2)}, u32[]{:S(2)}) collective-permute-start(bf16[128,256]{1,0:T(8,128)(2,1)S(1)} %get-tuple-element.41), channel_id=1, source_target_pairs={{0,24},{4,28},{8,16},{12,20},{16,8},{20,12},{24,0},{28,4},{1,25},{... | collective-permute-start | bytes 196616 | tf_op jit(solution)/shard_map/ppermute | solution.py:311
  45.3 4.5 %collective-permute-start.19 = (bf16[128,256]{1,0:T(8,128)(2,1)S(1)}, bf16[128,256]{1,0:T(8,128)(2,1)S(1)}, u32[]{:S(2)}, u32[]{:S(2)}) collective-permute-start(bf16[128,256]{1,0:T(8,128)(2,1)S(1)} %shard_map.100.refs_0_), channel_id=1, source_target_pairs={{0,1},{1,0},{2,3},{3,2},{4,5},{5,4},{6,7},{7,6},{8,9},{9,8},{10,11... | collective-permute-start | bytes 196616 | tf_op jit(solution)/shard_map/ppermute | solution.py:320
  45.8 5.2 %collective-permute-start.20 = (bf16[128,256]{1,0:T(8,128)(2,1)S(1)}, bf16[128,256]{1,0:T(8,128)(2,1)S(1)}, u32[]{:S(2)}, u32[]{:S(2)}) collective-permute-start(bf16[128,256]{1,0:T(8,128)(2,1)S(1)} %shard_map.100.refs_0_), channel_id=1, source_target_pairs={{0,2},{1,3},{2,0},{3,1},{4,6},{5,7},{6,4},{7,5},{8,10},{9,11},{10,... | collective-permute-start | bytes 196616 | tf_op jit(solution)/shard_map/ppermute | solution.py:320
  48.4 6.1 %collective-permute-start.21 = (bf16[128,256]{1,0:T(8,128)(2,1)S(1)}, bf16[128,256]{1,0:T(8,128)(2,1)S(1)}, u32[]{:S(2)}, u32[]{:S(2)}) collective-permute-start(bf16[128,256]{1,0:T(8,128)(2,1)S(1)} %shard_map.100.refs_0_), channel_id=1, source_target_pairs={{0,3},{1,2},{2,1},{3,0},{4,7},{5,6},{6,5},{7,4},{8,11},{9,10},{10,... | collective-permute-start | bytes 196616 | tf_op jit(solution)/shard_map/ppermute | solution.py:320
  54.5 4.3 %collective-permute-start.23 = (bf16[128,256]{1,0:T(8,128)(2,1)S(1)}, bf16[128,256]{1,0:T(8,128)(2,1)S(1)}, u32[]{:S(2)}, u32[]{:S(2)}) collective-permute-start(bf16[128,256]{1,0:T(8,128)(2,1)S(1)} %shard_map.101.refs_0_), channel_id=1, source_target_pairs={{0,8},{4,12},{8,0},{12,4},{16,24},{20,28},{24,16},{28,20},{1,9},{5... | collective-permute-start | bytes 196616 | tf_op jit(solution)/shard_map/ppermute | solution.py:311
  55.1 4.3 %collective-permute-start.25 = (bf16[128,256]{1,0:T(8,128)(2,1)S(1)}, bf16[128,256]{1,0:T(8,128)(2,1)S(1)}, u32[]{:S(2)}, u32[]{:S(2)}) collective-permute-start(bf16[128,256]{1,0:T(8,128)(2,1)S(1)} %shard_map.101.refs_0_), channel_id=1, source_target_pairs={{0,16},{4,20},{8,24},{12,28},{16,0},{20,4},{24,8},{28,12},{1,17},{... | collective-permute-start | bytes 196616 | tf_op jit(solution)/shard_map/ppermute | solution.py:311
  55.7 5.2 %collective-permute-start.27 = (bf16[128,256]{1,0:T(8,128)(2,1)S(1)}, bf16[128,256]{1,0:T(8,128)(2,1)S(1)}, u32[]{:S(2)}, u32[]{:S(2)}) collective-permute-start(bf16[128,256]{1,0:T(8,128)(2,1)S(1)} %shard_map.101.refs_0_), channel_id=1, source_target_pairs={{0,24},{4,28},{8,16},{12,20},{16,8},{20,12},{24,0},{28,4},{1,25},{... | collective-permute-start | bytes 196616 | tf_op jit(solution)/shard_map/ppermute | solution.py:311
  58.0 4.5 %collective-permute-start.22 = (bf16[128,256]{1,0:T(8,128)(2,1)S(1)}, bf16[128,256]{1,0:T(8,128)(2,1)S(1)}, u32[]{:S(2)}, u32[]{:S(2)}) collective-permute-start(bf16[128,256]{1,0:T(8,128)(2,1)S(1)} %shard_map.101.refs_0_), channel_id=1, source_target_pairs={{0,4},{4,0},{8,12},{12,8},{16,20},{20,16},{24,28},{28,24},{1,5},{5... | collective-permute-start | bytes 196616 | tf_op jit(solution)/shard_map/ppermute | solution.py:311
  58.8 3.7 %collective-permute-start.24 = (bf16[128,256]{1,0:T(8,128)(2,1)S(1)}, bf16[128,256]{1,0:T(8,128)(2,1)S(1)}, u32[]{:S(2)}, u32[]{:S(2)}) collective-permute-start(bf16[128,256]{1,0:T(8,128)(2,1)S(1)} %collective-permute-done.23.refs_1_), channel_id=1, source_target_pairs={{0,4},{4,0},{8,12},{12,8},{16,20},{20,16},{24,28},{28,24},{1,5},{5... | collective-permute-start | bytes 196616 | tf_op jit(solution)/shard_map/ppermute | solution.py:311
  59.3 3.2 %collective-permute-start.26 = (bf16[128,256]{1,0:T(8,128)(2,1)S(1)}, bf16[128,256]{1,0:T(8,128)(2,1)S(1)}, u32[]{:S(2)}, u32[]{:S(2)}) collective-permute-start(bf16[128,256]{1,0:T(8,128)(2,1)S(1)} %collective-permute-done.25.refs_2_), channel_id=1, source_target_pairs={{0,4},{4,0},{8,12},{12,8},{16,20},{20,16},{24,28},{28,24},{1,5},{5... | collective-permute-start | bytes 196616 | tf_op jit(solution)/shard_map/ppermute | solution.py:311
  60.9 1.7 %collective-permute-start.28 = (bf16[128,256]{1,0:T(8,128)(2,1)S(1)}, bf16[128,256]{1,0:T(8,128)(2,1)S(1)}, u32[]{:S(2)}, u32[]{:S(2)}) collective-permute-start(bf16[128,256]{1,0:T(8,128)(2,1)S(1)} %collective-permute-done.27.refs_3_), channel_id=1, source_target_pairs={{0,4},{4,0},{8,12},{12,8},{16,20},{20,16},{24,28},{28,24},{1,5},{5... | collective-permute-start | bytes 196616 | tf_op jit(solution)/shard_map/ppermute | solution.py:311
  (4 other events, 3.2 us)
